TPU v7x, 32 devices: a whole 2x2x4 slice. The times are simulated.
32 devices in a mesh: dp: 8 (over y, x, core), mp: 4 (over z).
Axes of the slice: x: 2, y: 2, z: 4, core: 2. Of those that a mesh axis runs over, the one named last changes fastest.
Arguments:
- tokens: bfloat16 [128, 542, 768], P(('dp', 'mp')), may hold values from -6 to 6
- cotangent: bfloat16 [128, 542, 768], P(('dp', 'mp')), may hold values from -6 to 6
- kept_index: int32 [128, 268], P(('dp', 'mp')), may hold values from 0 to 541, as said below
- attention_weights: float32 [768, 3072], P(None, ('dp', 'mp')), may hold values from -0.4082483 to 0.4082483
- attention_first: float32 [768, 3072], P(None, ('dp', 'mp')), may hold values from -224 to 224
- attention_second: float32 [768, 3072], P(None, ('dp', 'mp')), may hold values from 1372.16 to 5488.64
- attention_average: float32 [768, 3072], P(None, ('dp', 'mp')), may hold values from -0.4082483 to 0.4082483
- feedforward_weights: float32 [2, 768, 3072], P(None, 'dp', 'mp'), may hold values from -0.14433757 to 0.14433757
- feedforward_first: float32 [2, 768, 3072], P(None, 'dp', 'mp'), may hold values from -448 to 448
- feedforward_second: float32 [2, 768, 3072], P(None, 'dp', 'mp'), may hold values from 5488.64 to 21954.56
- feedforward_average: float32 [2, 768, 3072], P(None, 'dp', 'mp'), may hold values from -0.14433757 to 0.14433757
- vector_weights: float32 [13, 768], replicated, may hold values from -1.2 to 1.3
- vector_first: float32 [13, 768], replicated, may hold values from -1024 to 1024
- vector_second: float32 [13, 768], replicated, may hold values from 34304 to 137216
- vector_average: float32 [13, 768], replicated, may hold values from -1.2 to 1.3
Outputs:
- block_output: bfloat16 [128, 542, 768], P(('dp', 'mp'))
- input_gradient: float32 [128, 542, 768], P(('dp', 'mp'))
- attention_gradient: float32 [768, 3072], P(None, ('dp', 'mp'))
- attention_first_new: float32 [768, 3072], P(None, ('dp', 'mp'))
- attention_second_new: float32 [768, 3072], P(None, ('dp', 'mp'))
- attention_weights_new: float32 [768, 3072], P(None, ('dp', 'mp'))
- attention_average_new: float32 [768, 3072], P(None, ('dp', 'mp'))
- attention_copy: bfloat16 [768, 3072], P(None, ('dp', 'mp'))
- feedforward_gradient: float32 [2, 768, 3072], P(None, 'dp', 'mp')
- feedforward_first_new: float32 [2, 768, 3072], P(None, 'dp', 'mp')
- feedforward_second_new: float32 [2, 768, 3072], P(None, 'dp', 'mp')
- feedforward_weights_new: float32 [2, 768, 3072], P(None, 'dp', 'mp')
- feedforward_average_new: float32 [2, 768, 3072], P(None, 'dp', 'mp')
- feedforward_copy: bfloat16 [2, 768, 3072], P(None, 'dp', 'mp')
- vector_gradient: float32 [13, 768], replicated
- vector_first_new: float32 [13, 768], replicated
- vector_second_new: float32 [13, 768], replicated
- vector_weights_new: float32 [13, 768], replicated
- vector_average_new: float32 [13, 768], replicated
- query_bias_gradient: float32 [768], replicated
Inputs may be any that keep to these rules, and one draw needn't show every extreme that they name: `kept_index`: for each image and each of its six crops in order, 197//2 (global crops) or 37//2 (local crops) distinct increasing positions inside that crop; the crop's first and last positions are always among them.
All inputs are finite; a program needn't handle non-finite values.
Results may differ from a plain program's by a relative error of at most 0.0098.
The roundings to bfloat16 on the way count: a program that leaves them out, or rounds other values in their place, can miss the bound.
Values may be sent and summed in bfloat16 or wider, within the bound.
A program may use at most 192 MiB of HBM per device.

v0:
```python
import jax
import jax.numpy as jnp
import numpy as np
from jax import lax
from jax.sharding import PartitionSpec as P

H = 12
HD = 64
FF = 3072
LG = 197
LL = 37


HIGHEST = lax.Precision.HIGHEST


def crop_labels():
    labels = [0] * (LG // 2) + [1] * (LG // 2)
    for crop in range(2, 6):
        labels = labels + [crop] * (LL // 2)
    return np.array(labels, np.int32)


def normalize(rows):
    center = rows - jnp.mean(rows, axis=-1, keepdims=True)
    spread = jnp.mean(center * center, axis=-1, keepdims=True)
    inverse = lax.rsqrt(spread + 1e-06)
    return (center * inverse, inverse)


def norm_backward(upstream, standard, inverse, gain):
    scaled = upstream * gain
    return inverse * (
        scaled
        - jnp.mean(scaled, axis=-1, keepdims=True)
        - standard * jnp.mean(scaled * standard, axis=-1, keepdims=True)
    )


def gelu_slope(inner):
    return (
        0.5 * (1.0 + lax.erf(inner * 0.7071067811865476))
        + inner * jnp.exp(-0.5 * inner * inner) * 0.3989422804014327
    )


def transpose_product(left, right):
    return lax.dot_general(
        left, right, (((0,), (0,)), ((), ())), preferred_element_type=jnp.float32
    )


def product_transposed(left, right):
    return lax.dot_general(
        left, right, (((1,), (1,)), ((), ())), preferred_element_type=jnp.float32
    )


def adamw(grad, first, second, master, average, rate, decay):
    first_new = 0.5 * first + 0.5 * grad
    second_new = 0.5 * second + 0.5 * grad * grad
    update = first_new / (jnp.sqrt(second_new) + 1e-08)
    master_new = master - rate * (update + decay * master)
    average_new = 0.9 * average + 0.1 * master_new
    return (first_new, second_new, master_new, average_new)


def per_device(
    tokens,
    cotangent,
    kept_index,
    attention_weights,
    attention_first,
    attention_second,
    attention_average,
    feedforward_weights,
    feedforward_first,
    feedforward_second,
    feedforward_average,
    vector_weights,
    vector_first,
    vector_second,
    vector_average,
):
    images, length = kept_index.shape
    width = tokens.shape[2]
    heads = H
    head_size = HD
    hidden = FF
    hidden_local = feedforward_weights.shape[2]
    rows_count = images * length
    labels = crop_labels()
    same_crop = jnp.asarray(labels[:, None] == labels[None, :])
    factor = head_size ** (-0.5)
    bf16 = jnp.bfloat16
    f32 = jnp.float32
    attention_full = lax.all_gather(
        attention_weights.astype(bf16), ("dp", "mp"), axis=1, tiled=True
    )
    feed_rows = lax.all_gather(feedforward_weights.astype(bf16), "dp", axis=1, tiled=True)
    first_bias = vector_weights[9:].reshape(hidden)
    bias_used = lax.dynamic_slice_in_dim(
        first_bias, lax.axis_index("mp") * hidden_local, hidden_local
    )
    tokens_float = tokens.astype(f32)
    kept_rows = jnp.take_along_axis(tokens_float, kept_index[:, :, None], axis=1).reshape(
        rows_count, width
    )
    standard_one, inverse_one = normalize(kept_rows)
    normed = (standard_one * vector_weights[0] + vector_weights[1]).astype(bf16)
    normed_float = normed.astype(f32)
    score = jax.nn.sigmoid(jnp.dot(normed_float, vector_weights[2], precision=HIGHEST))
    bias_three = jnp.concatenate(
        [vector_weights[3], jnp.zeros_like(vector_weights[3]), vector_weights[4]]
    )
    project = (
        jnp.dot(normed, attention_full[:, : 3 * width], preferred_element_type=f32) + bias_three
    ).astype(bf16)
    query = project[:, :width].reshape(images, length, heads, head_size)
    keys = project[:, width : 2 * width].reshape(images, length, heads, head_size)
    values = project[:, 2 * width :].reshape(images, length, heads, head_size)
    scores = factor * jnp.einsum("ikhd,ijhd->ihkj", query, keys, preferred_element_type=f32)
    scores = jnp.where(same_crop, scores, -1000000000.0)
    total = jax.nn.logsumexp(scores, axis=-1, keepdims=True)
    probs_low = jnp.exp(scores - total).astype(bf16)
    mixed = (
        jnp.einsum("ihkj,ijhd->ikhd", probs_low, values, preferred_element_type=f32)
        .reshape(rows_count, width)
        .astype(bf16)
    )
    branch = (
        jnp.dot(mixed, attention_full[:, 3 * width :], preferred_element_type=f32)
        + vector_weights[5]
    )
    residual = kept_rows + score[:, None] * branch
    standard_two, inverse_two = normalize(residual)
    normed_two = (standard_two * vector_weights[6] + vector_weights[7]).astype(bf16)
    rows_all = lax.all_gather(normed_two, "mp", axis=0, tiled=True)
    inner = jnp.dot(rows_all, feed_rows[0], preferred_element_type=f32) + bias_used
    activated = jax.nn.gelu(inner, approximate=False).astype(bf16)
    piece = activated
    output = lax.psum_scatter(
        product_transposed(piece, feed_rows[1]).astype(jnp.bfloat16),
        "mp",
        scatter_dimension=0,
        tiled=True,
    ).astype(jnp.float32)
    result = residual + output + vector_weights[8]
    image_index = jnp.arange(images)[:, None]
    block_output = tokens.at[image_index, kept_index].set(
        result.reshape(images, length, width).astype(bf16)
    )
    cot_float = cotangent.astype(f32)
    cot_kept = jnp.take_along_axis(cotangent, kept_index[:, :, None], axis=1).reshape(
        rows_count, width
    )
    cot_all = lax.all_gather(cot_kept, "mp", axis=0, tiled=True)
    down_grad = transpose_product(cot_all, activated)
    active_grad = jnp.dot(cot_all, feed_rows[1], preferred_element_type=f32)
    inner_grad = (active_grad * gelu_slope(inner)).astype(bf16)
    up_grad = transpose_product(rows_all, inner_grad)
    bias_grad_local = jnp.sum(inner_grad.astype(f32), axis=0)
    piece = inner_grad
    normed_two_grad = lax.psum_scatter(
        product_transposed(piece, feed_rows[0]), "mp", scatter_dimension=0, tiled=True
    )
    cot_rows = cot_kept.astype(f32)
    residual_grad = cot_rows + norm_backward(
        normed_two_grad, standard_two, inverse_two, vector_weights[6]
    )
    gain_two_grad = jnp.sum(normed_two_grad * standard_two, axis=0)
    shift_two_grad = jnp.sum(normed_two_grad, axis=0)
    second_bias_grad = jnp.sum(cot_rows, axis=0)
    branch_grad = (score[:, None] * residual_grad).astype(bf16)
    router_grad = jnp.sum(residual_grad * branch, axis=1) * score * (1.0 - score)
    router_weight_grad = jnp.dot(router_grad, normed_float, precision=HIGHEST)
    out_grad = transpose_product(mixed, branch_grad)
    out_bias_grad = jnp.sum(branch_grad.astype(f32), axis=0)
    mixed_grad = product_transposed(branch_grad, attention_full[:, 3 * width :]).astype(bf16)
    mixed_grad = mixed_grad.reshape(images, length, heads, head_size)
    scores_again = factor * jnp.einsum("ikhd,ijhd->ihkj", query, keys, preferred_element_type=f32)
    probs = jnp.exp(jnp.where(same_crop, scores_again, -1000000000.0) - total)
    probs_grad = jnp.einsum("ikhd,ijhd->ihkj", mixed_grad, values, preferred_element_type=f32)
    inner_sum = jnp.sum(probs * probs_grad, axis=-1, keepdims=True)
    scores_grad = (probs * (probs_grad - inner_sum)).astype(bf16)
    query_grad = factor * jnp.einsum(
        "ihkj,ijhd->ikhd", scores_grad, keys, preferred_element_type=f32
    )
    key_grad = factor * jnp.einsum(
        "ihkj,ikhd->ijhd", scores_grad, query, preferred_element_type=f32
    )
    value_grad = jnp.einsum("ihkj,ikhd->ijhd", probs_low, mixed_grad, preferred_element_type=f32)
    project_grad = jnp.concatenate(
        [
            query_grad.reshape(rows_count, width),
            key_grad.reshape(rows_count, width),
            value_grad.reshape(rows_count, width),
        ],
        axis=1,
    ).astype(bf16)
    in_grad = transpose_product(normed, project_grad)
    project_float = project_grad.astype(f32)
    query_bias_grad = jnp.sum(project_float[:, :width], axis=0)
    value_bias_grad = jnp.sum(project_float[:, 2 * width :], axis=0)
    normed_grad = router_grad[:, None] * vector_weights[2] + product_transposed(
        project_grad, attention_full[:, : 3 * width]
    )
    gain_one_grad = jnp.sum(normed_grad * standard_one, axis=0)
    shift_one_grad = jnp.sum(normed_grad, axis=0)
    kept_grad = residual_grad + norm_backward(
        normed_grad, standard_one, inverse_one, vector_weights[0]
    )
    input_gradient = cot_float.at[image_index, kept_index].set(
        kept_grad.reshape(images, length, width)
    )
    attention_local = jnp.concatenate([in_grad, out_grad], axis=1)
    attention_gradient = lax.psum_scatter(
        attention_local, ("dp", "mp"), scatter_dimension=1, tiled=True
    )
    feed_local = jnp.stack([up_grad, down_grad])
    bias_full = lax.dynamic_update_slice_in_dim(
        jnp.zeros((hidden,), f32), bias_grad_local, lax.axis_index("mp") * hidden_local, 0
    )
    feedforward_gradient = lax.psum_scatter(feed_local, "dp", scatter_dimension=1, tiled=True)
    vector_local = jnp.concatenate(
        [
            jnp.stack(
                [
                    gain_one_grad,
                    shift_one_grad,
                    router_weight_grad,
                    query_bias_grad,
                    value_bias_grad,
                    out_bias_grad,
                    gain_two_grad,
                    shift_two_grad,
                    second_bias_grad,
                ]
            ),
            bias_full.reshape(-1, width),
        ],
        axis=0,
    )
    vector_gradient = lax.psum(vector_local, ("dp", "mp"))
    attention_new = adamw(
        attention_gradient,
        attention_first,
        attention_second,
        attention_weights,
        attention_average,
        0.02,
        0.05,
    )
    feedforward_new = adamw(
        feedforward_gradient,
        feedforward_first,
        feedforward_second,
        feedforward_weights,
        feedforward_average,
        0.02,
        0.05,
    )
    vector_new = adamw(
        vector_gradient, vector_first, vector_second, vector_weights, vector_average, 0.2, 0.0
    )
    return (
        block_output,
        input_gradient,
        attention_gradient,
        attention_new[0],
        attention_new[1],
        attention_new[2],
        attention_new[3],
        attention_new[2].astype(bf16),
        feedforward_gradient,
        feedforward_new[0],
        feedforward_new[1],
        feedforward_new[2],
        feedforward_new[3],
        feedforward_new[2].astype(bf16),
        vector_gradient,
        vector_new[0],
        vector_new[1],
        vector_new[2],
        vector_new[3],
        vector_gradient[3],
    )


def solution(mesh):
    in_specs = (
        P(("dp", "mp"), None, None),
        P(("dp", "mp"), None, None),
        P(("dp", "mp"), None),
        P(None, ("dp", "mp")),
        P(None, ("dp", "mp")),
        P(None, ("dp", "mp")),
        P(None, ("dp", "mp")),
        P(None, "dp", "mp"),
        P(None, "dp", "mp"),
        P(None, "dp", "mp"),
        P(None, "dp", "mp"),
        P(),
        P(),
        P(),
        P(),
    )
    out_specs = (
        P(("dp", "mp"), None, None),
        P(("dp", "mp"), None, None),
        P(None, ("dp", "mp")),
        P(None, ("dp", "mp")),
        P(None, ("dp", "mp")),
        P(None, ("dp", "mp")),
        P(None, ("dp", "mp")),
        P(None, ("dp", "mp")),
        P(None, "dp", "mp"),
        P(None, "dp", "mp"),
        P(None, "dp", "mp"),
        P(None, "dp", "mp"),
        P(None, "dp", "mp"),
        P(None, "dp", "mp"),
        P(),
        P(),
        P(),
        P(),
        P(),
        P(),
    )
    return jax.shard_map(
        per_device, mesh=mesh, in_specs=in_specs, out_specs=out_specs, check_vma=False
    )
```

profile of v0, /device:TPU:0, one launch (start us, length us, event | category | flops | bytes accessed | tf_op | source)
XLA Modules:
  0.0 997.2 jit_solution(14015516016372770413)
XLA Ops:
  14.1 18.1 %gather_fusion.1 = bf16[1072,768]{1,0:T(8,128)(2,1)S(1)} fusion(bf16[4,542,768]{2,0,1:T(4,128)(2,1)} %param.17, s32[1072]{0:T(1024)S(1)} %reshape.324), kind=kCustom, calls=%fused_computation.1 | custom fusion | bytes 3301760 | tf_op jit(solution)/shard_map/jit(take_along_axis)/gather | solution.py:154
  34.0 5.6 convert_element_type.94
  39.7 16.3 %gather_fusion = f32[1072,768]{1,0:T(8,128)S(1)} fusion(f32[4,542,768]{2,0,1:T(4,128)} %convert_element_type.94, s32[1072]{0:T(1024)S(1)} %reshape.324), kind=kCustom, calls=%fused_computation | custom fusion | bytes 6594944 | tf_op jit(solution)/shard_map/jit(take_along_axis)/gather | solution.py:106
  77.7 6.6 fusion.17
  86.6 6.1 reshape.362
  92.7 6.9 copy.128
  99.6 6.1 reshape.361
  105.7 7.1 copy.127
  112.8 12.7 %fusion = (f32[4,12,268]{2,1,0:T(8,128)S(1)}, f32[4,12,268,268]{2,3,1,0:T(8,128)}) fusion(pred[268,268]{0,1:T(8,128)(4,1)S(1)} %copy-done.18, bf16[4,268,12,64]{1,3,2,0:T(8,128)(2,1)} %copy.127, bf16[4,268,12,64]{1,3,2,0:T(8,128)(2,1)} %copy.128), kind=kOutput, calls=%fused_computation.11 | convolution fusion | flops 451616448 | bytes 17206672 | tf_op jit(solution)/shard_map/ikhd,ijhd->ihkj/dot_general | solution.py:122
  126.2 12.0 %exponential_reduce_fusion = f32[4,12,268]{2,1,0:T(8,128)} fusion(f32[4,12,268,268]{2,3,1,0:T(8,128)} %get-tuple-element.142, f32[4,12,268]{2,1,0:T(8,128)} %is-finite_select_fusion, pred[268,268]{0,1:T(8,128)(4,1)S(1)} %copy-done.18), kind=kLoop, calls=%fused_computation.7 | loop fusion | flops 13777344 | bytes 13964944 | tf_op jit(solution)/shard_map/reduce_sum | solution.py:124
  138.2 6.1 reshape.360
  144.3 7.1 copy.129
  152.3 12.4 %convert_bitcast_fusion.2 = bf16[4,268,12,64]{1,3,2,0:T(8,128)(2,1)S(1)} fusion(bf16[4,268,12,64]{1,3,2,0:T(8,128)(2,1)} %copy.129, f32[4,12,268,268]{2,3,1,0:T(8,128)} %get-tuple-element.142, f32[4,12,268]{2,1,0:T(8,128)S(1)} %log_add_fusion, pred[268,268]{0,1:T(8,128)(4,1)S(1)} %copy-done.18), kind=kOutput, calls=%fused_computation.84 | convolution fusion | flops 455900160 | bytes 17206672 | tf_op jit(solution)/shard_map/ihkj,ijhd->ikhd/dot_general | solution.py:127
  168.0 4.7 convert_element_type.103
  172.8 5.8 fusion.57
  183.8 119.9 %all-gather.7.cloned.1.call-done = bf16[4288,768]{1,0:T(8,128)(2,1)} async-done(((bf16[1072,768]{1,0:T(8,128)(2,1)}), bf16[4288,768]{1,0:T(8,128)(2,1)}) %all-gather.7.cloned.1.call-update) | async-done | bytes 6586384 | tf_op jit(solution)/shard_map/all_gather | solution.py:138
  303.7 38.2 %fusion.3 = (bf16[4288,768]{1,0:T(8,128)(2,1)}, f32[4288,768]{1,0:T(8,128)}) fusion(f32[768]{0:T(1024)S(1)} %dynamic_slice.3, bf16[4288,768]{1,0:T(8,128)(2,1)} %all-gather.7.cloned.1.call-done, bf16[2,768,768]{2,1,0:T(8,128)(2,1)} %all-gather.9.cloned.1.call-done), kind=kOutput, calls=%fused_computation.15 | convolution fusion | flops 5275680768 | bytes 27528192 | tf_op jit(solution)/shard_map/dot_general | solution.py:139
  341.9 81.6 %all-gather.11.cloned.1.call-done = bf16[4288,768]{1,0:T(8,128)(2,1)} async-done(((bf16[1072,768]{1,0:T(8,128)(2,1)}), bf16[4288,768]{1,0:T(8,128)(2,1)}) %all-gather.11.cloned.1.call-update) | async-done | bytes 6586384 | tf_op jit(solution)/shard_map/all_gather | solution.py:157
  423.5 11.5 %convert_reduce_fusion = (f32[768]{0:T(1024)S(1)}, bf16[4288,768]{1,0:T(8,128)(2,1)S(1)}) fusion(f32[4288,768]{1,0:T(8,128)} %get-tuple-element.145, f32[768]{0:T(1024)S(1)} %dynamic_slice.3, bf16[4288,768]{1,0:T(8,128)(2,1)} %all-gather.11.cloned.1.call-done, bf16[2,768,768]{2,1,0:T(8,128)(2,1)S(1)} %copy-done.64), kind=kOutput, calls=%fused_computation.22 | convolution fusion | flops 5101140992 | bytes 27532288 | tf_op jit(solution)/shard_map/dot_general | solution.py:159
  437.7 8.5 fusion.36
  446.3 9.7 convolution_bitcast_fusion.1
  456.0 9.5 convolution_bitcast_fusion
  468.0 10.1 %convolution_convert_fusion = bf16[4288,768]{1,0:T(8,128)(2,1)} fusion(bf16[4288,768]{1,0:T(8,128)(2,1)} %get-tuple-element.144, bf16[2,768,768]{2,1,0:T(8,128)(2,1)S(1)} %copy-done.64), kind=kOutput, calls=%fused_computation.41 | convolution fusion | flops 5061623808 | bytes 14352384 | tf_op jit(solution)/shard_map/dot_general | solution.py:54
  478.2 187.8 %reduce-scatter.9.cloned.1.call-done = f32[1072,768]{1,0:T(8,128)} async-done(((f32[4288,768]{1,0:T(8,128)}), f32[1072,768]{1,0:T(8,128)}) %reduce-scatter.9.cloned.1.call-update) | async-done | bytes 3293200 | tf_op jit(solution)/shard_map/reduce_scatter | solution.py:164
  678.0 6.2 reshape.363
  684.2 6.9 copy.133
  691.2 14.5 %convert_bitcast_fusion.1 = bf16[4,268,12,64]{1,3,2,0:T(8,128)(2,1)} fusion(bf16[4,268,12,64]{1,3,2,0:T(8,128)(2,1)} %copy.133, f32[4,12,268,268]{2,3,1,0:T(8,128)} %get-tuple-element.142, f32[4,12,268]{2,1,0:T(8,128)S(1)} %copy-done.26, pred[268,268]{0,1:T(8,128)(4,1)S(1)} %copy-done.19), kind=kOutput, calls=%fused_computation.83 | convolution fusion | flops 455900160 | bytes 17206672 | tf_op jit(solution)/shard_map/ihkj,ikhd->ijhd/dot_general | solution.py:192
  705.7 5.0 copy.143
  710.7 4.7 reshape.313
  715.4 15.5 %multiply_reduce_fusion = (f32[4,12,268]{2,1,0:T(8,128)S(1)}, f32[4,12,268,268]{2,3,1,0:T(8,128)}) fusion(f32[4,12,268,268]{2,3,1,0:T(8,128)} %get-tuple-element.142, f32[4,12,268]{2,1,0:T(8,128)S(1)} %copy-done.26, pred[268,268]{0,1:T(8,128)(4,1)S(1)} %copy-done.19, bf16[4,268,12,64]{1,3,2,0:T(8,128)(2,1)} %copy.133, bf16[4,268,12,64]{1,3,2,0:T(8,128)(2,1)} %copy.129), kind=kOutput, calls=%fused_computation.5 | convolution fusion | flops 458511552 | bytes 31048336 | tf_op jit(solution)/shard_map/ikhd,ijhd->ihkj/dot_general | solution.py:183
  730.9 15.8 %multiply_convert_fusion = bf16[4,12,268,268]{2,3,1,0:T(8,128)(2,1)S(1)} fusion(f32[4,12,268,268]{2,3,1,0:T(8,128)} %get-tuple-element.147, f32[4,12,268,268]{2,3,1,0:T(8,128)} %get-tuple-element.142, f32[4,12,268]{2,1,0:T(8,128)S(1)} %get-tuple-element.146, f32[4,12,268]{2,1,0:T(8,128)S(1)} %copy-done.26, pred[268,268]{0,1:T(8,128)(4,1)S(1)} %copy-done.19), kind=kLoop, calls=%fused_computation.4 | loop fusion | flops 20685312 | bytes 34650256 | tf_op jit(solution)/shard_map/convert_element_type | solution.py:185
  753.7 4.8 reshape.311
  758.6 8.3 fusion.29
  782.1 6.9 fusion.59
  789.0 8.7 pad_maximum_fusion
  797.7 9.6 copy.153
  808.4 6.6 reshape.317
  815.0 5.7 convert_bitcast_fusion
  820.7 8.4 reshape.321
  834.2 8.6 reduce-scatter.7.cloned.1.call-done
  842.8 13.8 %scatter_custom_fusion = bf16[2168,768]{1,0:T(8,128)(2,1)} fusion(bf16[2168,768]{1,0:T(8,128)(2,1)} %reshape.317, s32[1072]{0:T(1024)S(1)} %reshape.336, f32[1072,768]{1,0:T(8,128)S(1)} %copy-done.2, bf16[1072,768]{1,0:T(8,128)(2,1)} %reduce-scatter.7.cloned.1.call-done, f32[768]{0:T(1024)S(1)} %copy-done.58), kind=kCustom, calls=%fused_computation.87 | custom fusion | flops 3293184 | bytes 8273920
  856.5 7.0 reshape.318
  863.5 8.0 convert_element_type.119
  873.7 10.7 %multiply_reduce_fusion.3 = (f32[768]{0:T(1024)S(1)}, f32[1072]{0:T(1024)S(1)}, f32[1072]{0:T(1024)S(1)}, f32[768]{0:T(1024)S(1)}, f32[1072,768]{1,0:T(8,128)}) fusion(f32[1072]{0:T(1024)S(1)} %copy-done.41, f32[1072]{0:T(1024)S(1)} %copy-done.39, f32[1072,768]{1,0:T(8,128)S(1)} %copy-done.4, pred[1072]{0:T(1024)(128)(4,1)S(1)} %copy-done.48, ...), kind=kOutput, calls=%fused_computation.56 | convolution fusion | flops 3803623936 | bytes 15468528 | tf_op jit(solution)/shard_map/dot_general | solution.py:54
  884.4 17.0 %scatter_custom_fusion.1 = f32[2168,768]{1,0:T(8,128)} fusion(f32[2168,768]{1,0:T(8,128)} %reshape.321, s32[1072]{0:T(1024)S(1)} %reshape.336, f32[1072,768]{1,0:T(8,128)} %get-tuple-element.127, f32[1072,768]{1,0:T(8,128)} %get-tuple-element.148, f32[1072]{0:T(1024)S(1)} %broadcast_multiply_fusion, f32[1072]{0:T(1024)S(1)} %broadcast_multiply_fusion.1, ...), kind=kCustom, calls=%fused_computation.57 | custom fusion | flops 7409664 | bytes 16578560
  901.5 8.3 reshape.322
  914.4 41.3 %psum.7 = f32[13,768]{1,0:T(8,128)S(1)} all-reduce(f32[13,768]{1,0:T(8,128)S(1)} %concatenate.21), channel_id=1, replica_groups=mesh['dp'=8,'mp'=4] {'dp','mp'}, use_global_device_ids=true, to_apply=%region_27.28 | all-reduce | flops 9984 | bytes 79872 | tf_op jit(solution)/shard_map/psum | solution.py:244
  957.1 30.1 %reduce-scatter.13.cloned.1.call-done = f32[96,768]{1,0:T(8,128)} async-done(((f32[3072,768]{1,0:T(8,128)}), f32[96,768]{1,0:T(8,128)}) %reduce-scatter.13.cloned.1.call-update) | async-done | bytes 294928
  (229 shorter events, 98.6 us)
Async XLA Ops:
  7.2 70.5 %all-gather.5.cloned.1.call-start = ((), (), s32[]{:S(2)}) async-start(), calls=%async_computation.4 | async-start | bytes 4866048 | tf_op jit(solution)/shard_map/all_gather | solution.py:97
  8.9 174.9 %all-gather.9.cloned.1.call-start = ((), (), s32[]{:S(2)}) async-start(), calls=%async_computation.6 | async-start | bytes 2654208 | tf_op jit(solution)/shard_map/all_gather | solution.py:100
  10.8 292.9 %all-gather.7.cloned.1.call-start = ((), (), s32[]{:S(2)}) async-start(), calls=%async_computation.5 | async-start | bytes 8232960 | tf_op jit(solution)/shard_map/all_gather | solution.py:138
  12.3 61.2 %copy-start.46 = (pred[1072]{0:T(1024)(128)(4,1)}, pred[1072]{0:T(1024)(128)(4,1)S(1)}, u32[]{:S(2)}) copy-start(pred[1072]{0:T(1024)(128)(4,1)S(1)} %broadcast_in_dim.74) | copy-start | bytes 3220
  14.1 59.4 %copy-start.51 = (f32[768]{0:T(1024)}, f32[768]{0:T(1024)S(1)}, u32[]{:S(2)}) copy-start(f32[768]{0:T(1024)S(1)} %get-tuple-element.117) | copy-start | bytes 9220
  55.9 116.8 %copy-start.3 = (f32[1072,768]{1,0:T(8,128)}, f32[1072,768]{1,0:T(8,128)S(1)}, u32[]{:S(2)}) copy-start(f32[1072,768]{1,0:T(8,128)S(1)} %gather_fusion) | copy-start | bytes 9879556
  61.0 12.5 %copy-start.38 = (f32[1072]{0:T(1024)}, f32[1072]{0:T(1024)S(1)}, u32[]{:S(2)}) copy-start(f32[1072]{0:T(1024)S(1)} %div.41) | copy-start | bytes 12868
  64.8 8.7 copy-start.40
  64.8 5.8 copy-start.31
  73.4 10.8 %copy-start.42 = (f32[1072]{0:T(1024)}, f32[1072]{0:T(1024)S(1)}, u32[]{:S(2)}) copy-start(f32[1072]{0:T(1024)S(1)} %convolution_reduce_fusion) | copy-start | bytes 12868
  73.4 99.3 %copy-start.44 = (f32[1072]{0:T(1024)}, f32[1072]{0:T(1024)S(1)}, u32[]{:S(2)}) copy-start(f32[1072]{0:T(1024)S(1)} %add_divide_fusion) | copy-start | bytes 12868
  105.7 7.1 copy-start.18
  152.3 12.5 %copy-start.25 = (f32[4,12,268]{2,1,0:T(8,128)}, f32[4,12,268]{2,1,0:T(8,128)S(1)}, u32[]{:S(2)}) copy-start(f32[4,12,268]{2,1,0:T(8,128)S(1)} %log_add_fusion) | copy-start | bytes 154372
  164.8 8.0 copy-start.47
  164.8 8.0 copy-start.57
  182.1 241.4 %all-gather.11.cloned.1.call-start = ((), (), s32[]{:S(2)}) async-start(), calls=%async_computation.8 | async-start | bytes 8232960 | tf_op jit(solution)/shard_map/all_gather | solution.py:157
  183.6 482.4 %reduce-scatter.9.cloned.1.call-start = ((), (), s32[]{:S(2)}) async-start(), calls=%async_computation.9 | async-start | bytes 16465920 | tf_op jit(solution)/shard_map/reduce_scatter | solution.py:164
  183.8 239.8 %copy-start.64 = (bf16[2,768,768]{2,1,0:T(8,128)(2,1)S(1)}, bf16[2,768,768]{2,1,0:T(8,128)(2,1)}, u32[]{:S(2)}) copy-start(bf16[2,768,768]{2,1,0:T(8,128)(2,1)} %all-gather.9.cloned.1.call-done) | copy-start | bytes 7077892
  446.2 383.2 %reduce-scatter.11.cloned.1.call-start = ((), (), s32[]{:S(2)}) async-start(), calls=%async_computation.10 | async-start | bytes 5308416 | tf_op jit(solution)/shard_map/reduce_scatter | solution.py:224
  467.9 374.9 %reduce-scatter.7.cloned.1.call-start = ((), (), s32[]{:S(2)}) async-start(), calls=%async_computation.7 | async-start | bytes 8232960 | tf_op jit(solution)/shard_map/reduce_scatter | solution.py:142
  478.1 187.9 %copy-start.2 = (f32[1072,768]{1,0:T(8,128)S(1)}, f32[1072,768]{1,0:T(8,128)}, u32[]{:S(2)}) copy-start(f32[1072,768]{1,0:T(8,128)} %copy-done.1) | copy-start | bytes 9879556
  478.1 187.9 %copy-start.35 = (f32[1072]{0:T(1024)S(1)}, f32[1072]{0:T(1024)}, u32[]{:S(2)}) copy-start(f32[1072]{0:T(1024)} %copy-done.34) | copy-start | bytes 12868
  478.1 187.9 %copy-start.37 = (f32[1072]{0:T(1024)S(1)}, f32[1072]{0:T(1024)}, u32[]{:S(2)}) copy-start(f32[1072]{0:T(1024)} %copy-done.36) | copy-start | bytes 12868
  478.1 187.9 %copy-start.50 = (f32[768]{0:T(1024)S(1)}, f32[768]{0:T(1024)}, u32[]{:S(2)}) copy-start(f32[768]{0:T(1024)} %get-tuple-element.112) | copy-start | bytes 9220
  478.1 191.3 %copy-start.45 = (f32[1072]{0:T(1024)S(1)}, f32[1072]{0:T(1024)}, u32[]{:S(2)}) copy-start(f32[1072]{0:T(1024)} %copy-done.44) | copy-start | bytes 12868
  478.1 191.3 %copy-start.48 = (pred[1072]{0:T(1024)(128)(4,1)S(1)}, pred[1072]{0:T(1024)(128)(4,1)}, u32[]{:S(2)}) copy-start(pred[1072]{0:T(1024)(128)(4,1)} %copy-done.46) | copy-start | bytes 3220
  478.2 509.0 %reduce-scatter.13.cloned.1.call-start = ((), (), s32[]{:S(2)}) async-start(), calls=%async_computation.11 | async-start | bytes 9732096
  666.0 3.5 copy-start.8
  666.0 3.5 copy-start.11
  684.2 6.9 copy-start.19
  684.2 6.9 copy-start.26
  730.9 15.8 %copy-start.9 = (bf16[4,268,12,64]{1,3,2,0:T(8,128)(2,1)S(1)}, bf16[4,268,12,64]{1,3,2,0:T(8,128)(2,1)}, u32[]{:S(2)}) copy-start(bf16[4,268,12,64]{1,3,2,0:T(8,128)(2,1)} %copy.128) | copy-start | bytes 4939780
  746.7 3.8 copy-start
  808.3 6.7 copy-start.60
  829.1 13.6 %copy-start.58 = (f32[768]{0:T(1024)S(1)}, f32[768]{0:T(1024)}, u32[]{:S(2)}) copy-start(f32[768]{0:T(1024)} %get-tuple-element.118) | copy-start | bytes 9220
  829.4 3.9 copy-start.27
  863.5 8.1 copy-start.5
  863.5 8.1 copy-start.10
  909.8 3.7 copy-start.17
  909.8 46.6 %copy-start.32 = (f32[13,768]{1,0:T(8,128)S(1)}, f32[13,768]{1,0:T(8,128)}, u32[]{:S(2)}) copy-start(f32[13,768]{1,0:T(8,128)} %param.27) | copy-start | bytes 119812
  909.8 46.6 %copy-start.54 = (f32[13,768]{1,0:T(8,128)S(1)}, f32[13,768]{1,0:T(8,128)}, u32[]{:S(2)}) copy-start(f32[13,768]{1,0:T(8,128)} %param.30) | copy-start | bytes 119812
  909.8 46.6 %copy-start.55 = (f32[13,768]{1,0:T(8,128)S(1)}, f32[13,768]{1,0:T(8,128)}, u32[]{:S(2)}) copy-start(f32[13,768]{1,0:T(8,128)} %param.29) | copy-start | bytes 119812
  909.8 46.5 %copy-start.56 = (f32[13,768]{1,0:T(8,128)S(1)}, f32[13,768]{1,0:T(8,128)}, u32[]{:S(2)}) copy-start(f32[13,768]{1,0:T(8,128)} %param.28) | copy-start | bytes 119812
  909.8 77.3 %copy-start.24 = (f32[768,96]{0,1:T(8,128)S(1)}, f32[768,96]{0,1:T(8,128)}, u32[]{:S(2)}) copy-start(f32[768,96]{0,1:T(8,128)} %param.19) | copy-start | bytes 884740
  909.9 77.3 %copy-start.28 = (f32[768,96]{0,1:T(8,128)S(1)}, f32[768,96]{0,1:T(8,128)}, u32[]{:S(2)}) copy-start(f32[768,96]{0,1:T(8,128)} %param.21) | copy-start | bytes 884740
  909.9 77.3 %copy-start.29 = (f32[768,96]{0,1:T(8,128)S(1)}, f32[768,96]{0,1:T(8,128)}, u32[]{:S(2)}) copy-start(f32[768,96]{0,1:T(8,128)} %param.20) | copy-start | bytes 884740
  913.5 75.6 %copy-start.30 = (f32[768,96]{0,1:T(8,128)S(1)}, f32[768,96]{0,1:T(8,128)}, u32[]{:S(2)}) copy-start(f32[768,96]{0,1:T(8,128)} %param.22) | copy-start | bytes 884740
  955.7 34.2 %copy-start.33 = (f32[13,768]{1,0:T(8,128)}, f32[13,768]{1,0:T(8,128)S(1)}, u32[]{:S(2)}) copy-start(f32[13,768]{1,0:T(8,128)S(1)} %psum.7) | copy-start | bytes 119812
  (26 other events, 46.2 us)
Sparse Core Ops, SparseCore 0:
  11.4 66.2 all-gather.4
  80.2 27.8 all-gather.8
  182.2 121.4 all-gather.6
  305.1 118.3 all-gather.10
  446.3 219.5 reduce-scatter.8
  669.9 54.9 reduce-scatter.10
  727.2 115.4 reduce-scatter.6
  850.3 136.8 reduce-scatter.12
where the time goes:
time: 1010 us; the launch traced here: 997 us
  waiting for transfers between devices  430 us (43%)
  matrix products  194 us (19%)
  local copies, waits for them, and re-layouts  186 us (18%)
  other arithmetic  130 us (13%)
  blocking collectives  41.3 us (4%)
  between operations  15.4 us (2%)
    reduce_scatter x1, waiting for transfers between devices, per_device(): lax.psum_scatter(product_transposed(piece, feed_rows[0]), 'mp', scatter_d...  188 us
    all_gather x1, waiting for transfers between devices, per_device(): rows_all = lax.all_gather(normed_two, 'mp', axis=0, tiled=True)  120 us
    all_gather x1, waiting for transfers between devices, per_device(): cot_all = lax.all_gather(cot_kept, 'mp', axis=0, tiled=True)  81.6 us
    unnamed x140, local copies, waits for them, and re-layouts  53.8 us
    psum x1, blocking collectives, per_device(): vector_gradient = lax.psum(vector_local, ('dp', 'mp'))  41.3 us
    dot_general x1, matrix products, per_device(): jnp.dot(rows_all, feed_rows[0], preferred_element_type=f32) + bias_used  38.2 us
    unnamed x6, other arithmetic  36.7 us
    dot_general x4, matrix products, product_transposed(): lax.dot_general(left, right, (((1,), (1,)), ((), ())), preferred_element_...  33.3 us
  transfers between devices with their start and end apart: 8, of which 6 were waited for; matrix products, arithmetic and copies ran while one was open for 48% of the time, Pallas kernels for 0%

commit v1 on v0

v1 whole, which is shorter than its diff:
```python
import functools

import jax
import jax.numpy as jnp
import numpy as np
from jax import lax
from jax.experimental import pallas as pl
from jax.experimental.pallas import tpu as pltpu
from jax.sharding import PartitionSpec as P

H = 12
HD = 64
LG = 197
LL = 37
KG = LG // 2
KL = LL // 2
LOC = 4 * KL
GP = -(-KG // 16) * 16
LP = -(-LOC // 16) * 16
RI = 2 * GP + LP
UNITS = ((0, GP), (GP, GP), (2 * GP, LP))
PAIRS = H // 2
W2L = 2 * HD

bf16 = jnp.bfloat16
f32 = jnp.float32


def params(limit=56, **kw):
    return pltpu.CompilerParams(vmem_limit_bytes=limit << 20, **kw)


def full(shape):
    return pl.BlockSpec(shape, lambda *_: (0,) * len(shape))


def per_image(*shape):
    return pl.BlockSpec((1,) + shape, lambda i, *_: (i,) + (0,) * len(shape))


def nn(a, b):
    return lax.dot_general(a, b, (((1,), (0,)), ((), ())), preferred_element_type=f32)


def nt(a, b):
    return lax.dot_general(a, b, (((1,), (1,)), ((), ())), preferred_element_type=f32)


def tn(a, b):
    return lax.dot_general(a, b, (((0,), (0,)), ((), ())), preferred_element_type=f32)


def normalize(rows):
    center = rows - jnp.mean(rows, axis=-1, keepdims=True)
    spread = jnp.mean(center * center, axis=-1, keepdims=True)
    inverse = lax.rsqrt(spread + 1e-06)
    return center * inverse, inverse


def norm_backward(upstream, standard, inverse, gain):
    scaled = upstream * gain
    return inverse * (
        scaled
        - jnp.mean(scaled, axis=-1, keepdims=True)
        - standard * jnp.mean(scaled * standard, axis=-1, keepdims=True)
    )


def colsum(v):
    return jnp.sum(v, axis=0, keepdims=True)


def masks():
    key = np.arange(GP)[:, None]
    query = np.zeros((1, GP), np.int64)
    mg = np.where((key < KG) & (query == 0), 0.0, -1e9)
    key = np.arange(LP)[:, None]
    query = np.arange(LP)[None, :]
    ml = np.where((key < LOC) & (key // KL == query // KL), 0.0, -1e9)
    two = lambda m: jnp.asarray(np.concatenate([m, m], 1), f32)
    return two(mg), two(ml)


def lane_half(shape):
    return lax.broadcasted_iota(jnp.int32, shape, len(shape) - 1) < HD


def split_heads(v, scale):
    first = lane_half(v.shape)
    zero = jnp.zeros_like(v)
    if scale != 1.0:
        v = v * jnp.asarray(scale, v.dtype)
    return jnp.concatenate([jnp.where(first, v, zero), jnp.where(first, zero, v)], axis=0)


def join_heads(v):
    n = v.shape[0] // 2
    return jnp.where(lane_half((n, v.shape[1])), v[:n], v[n:])


def softmax_keys(st):
    p = jnp.exp(st - jnp.max(st, axis=0, keepdims=True))
    return p * (1.0 / jnp.sum(p, axis=0, keepdims=True))


def gather_kernel(tok_ref, cot_ref, idx_ref, vec_ref, kept_ref, normed_ref, cotk_ref):
    hot = (
        lax.broadcasted_iota(jnp.int32, (RI, tok_ref.shape[1]), 1) == idx_ref[0]
    ).astype(f32).astype(bf16)
    kept = nn(hot, tok_ref[0])
    kept_ref[0] = kept.astype(bf16)
    cotk_ref[0] = nn(hot, cot_ref[0]).astype(bf16)
    standard, _ = normalize(kept)
    normed_ref[0] = (standard * vec_ref[0:1] + vec_ref[1:2]).astype(bf16)


def router_score(normed, vec_ref):
    logit = jnp.sum(normed.astype(f32) * vec_ref[2:3], axis=-1, keepdims=True)
    return jax.nn.sigmoid(logit)


def forward_kernel(
    normed_ref, kept_ref, watt_ref, vec_ref, mg_ref, ml_ref,
    proj_ref, mixed_ref, branch_ref, n2_ref,
):
    d = normed_ref.shape[2]
    normed = normed_ref[0]
    for j, row in ((0, 3), (1, None), (2, 4)):
        part = nt(normed, watt_ref[j * d : (j + 1) * d, :])
        if row is not None:
            part = part + vec_ref[row : row + 1]
        proj_ref[0, :, j * d : (j + 1) * d] = part.astype(bf16)
    for start, n in UNITS:
        mask_ref = mg_ref if n == GP else ml_ref
        for pair in range(PAIRS):
            cols = lambda j: slice(j * d + pair * W2L, j * d + (pair + 1) * W2L)
            rows = slice(start, start + n)
            qs = split_heads(proj_ref[0, rows, cols(0)], HD ** -0.5)
            st = nt(proj_ref[0, rows, cols(1)], qs) + mask_ref[...]
            pt = softmax_keys(st).astype(bf16)
            out = tn(pt, proj_ref[0, rows, cols(2)])
            mixed_ref[0, rows, pair * W2L : (pair + 1) * W2L] = join_heads(out).astype(bf16)
    branch = nt(mixed_ref[0], watt_ref[3 * d :, :]) + vec_ref[5:6]
    branch_ref[0] = branch
    residual = kept_ref[0].astype(f32) + router_score(normed, vec_ref) * branch
    standard, _ = normalize(residual)
    n2_ref[0] = (standard * vec_ref[6:7] + vec_ref[7:8]).astype(bf16)


def feed_kernel(
    n2_ref, cot_ref, w_ref, bias_ref, out_ref, n2g_ref, gff_ref, bg_ref, act_s, ig_s,
):
    step = pl.program_id(0)
    images = n2_ref.shape[0]
    d, hb = w_ref.shape[2], w_ref.shape[3]
    bg_ref[0] = jnp.zeros((1, hb), f32)

    @pl.when(step == 0)
    def _():
        out_ref[...] = jnp.zeros_like(out_ref)
        n2g_ref[...] = jnp.zeros_like(n2g_ref)

    @pl.loop(0, images)
    def _(i):
        inner = nn(n2_ref[i], w_ref[0, 0]) + bias_ref[0]
        ag = nn(cot_ref[i], w_ref[0, 1])
        phi = 0.5 * (1.0 + lax.erf(inner * 0.7071067811865476))
        act = (inner * phi).astype(bf16)
        slope = phi + inner * jnp.exp(-0.5 * inner * inner) * 0.3989422804014327
        ig = (ag * slope).astype(bf16)
        rows = pl.ds(pl.multiple_of(i * RI, 16), RI)
        act_s[rows, :] = act
        ig_s[rows, :] = ig
        bg_ref[0] += colsum(ig.astype(f32))
        out_ref[i] += nt(act, w_ref[0, 1])
        n2g_ref[i] += nt(ig, w_ref[0, 0])

    n2 = n2_ref[...].reshape(images * RI, d)
    cot = cot_ref[...].reshape(images * RI, d)
    gff_ref[0, 0] = tn(n2, ig_s[...]).astype(bf16)
    gff_ref[0, 1] = tn(cot, act_s[...]).astype(bf16)


def backward_kernel(
    n2g_ref, cotk_ref, branch_ref, kept_ref, normed_ref, proj_ref, mixed_ref, watt_ref,
    vec_ref, mg_ref, ml_ref, dp_ref, resg_ref, rg_ref, vecg_ref, dproj_s, mg_s,
):
    d = normed_ref.shape[2]
    normed = normed_ref[0]
    score = router_score(normed, vec_ref)
    branch = branch_ref[0]
    residual = kept_ref[0].astype(f32) + score * branch
    standard, inverse = normalize(residual)
    n2g = n2g_ref[0]
    cot = cotk_ref[0].astype(f32)
    resg = cot + norm_backward(n2g, standard, inverse, vec_ref[6:7])
    resg_ref[0] = resg
    bg = (score * resg).astype(bf16)
    rg = jnp.sum(resg * branch, axis=-1, keepdims=True) * score * (1.0 - score)
    rg_ref[0] = rg
    dp_ref[0, :, 3 * d :] = bg
    mg_s[...] = nn(bg, watt_ref[3 * d :, :]).astype(bf16)
    for start, n in UNITS:
        mask_ref = mg_ref if n == GP else ml_ref
        rows = slice(start, start + n)
        for pair in range(PAIRS):
            cols = lambda j: slice(j * d + pair * W2L, j * d + (pair + 1) * W2L)
            qs = split_heads(proj_ref[0, rows, cols(0)], HD ** -0.5)
            kk = proj_ref[0, rows, cols(1)]
            pt = softmax_keys(nt(kk, qs) + mask_ref[...])
            ds = split_heads(mg_s[rows, cols(0)], 1.0)
            gpt = nt(proj_ref[0, rows, cols(2)], ds)
            sg = (pt * (gpt - jnp.sum(pt * gpt, axis=0, keepdims=True))).astype(bf16)
            qg = join_heads(tn(sg, kk)) * HD ** -0.5
            dp_ref[0, rows, cols(0)] = qg.astype(bf16)
            dp_ref[0, rows, cols(1)] = nn(sg, qs).astype(bf16)
            dp_ref[0, rows, cols(2)] = nn(pt.astype(bf16), ds).astype(bf16)
    zero = jnp.zeros((1, d), f32)
    sums = jnp.concatenate(
        [
            colsum(rg * normed.astype(f32)),
            colsum(dp_ref[0, :, :d].astype(f32)),
            colsum(dp_ref[0, :, 2 * d : 3 * d].astype(f32)),
            colsum(bg.astype(f32)),
            colsum(n2g * standard),
            colsum(n2g),
            colsum(cot),
            zero,
        ],
        axis=0,
    )

    @pl.when(pl.program_id(0) == 0)
    def _():
        vecg_ref[...] = jnp.zeros_like(vecg_ref)

    vecg_ref[...] += sums


def grad_kernel(dp_ref, normed_ref, mixed_ref, g_ref):
    rows = dp_ref.shape[0] * dp_ref.shape[1]
    left = dp_ref[...].reshape(rows, dp_ref.shape[2])
    d = normed_ref.shape[2]

    @pl.when(pl.program_id(0) < 3)
    def _():
        g_ref[...] = tn(left, normed_ref[...].reshape(rows, d)).astype(bf16)

    @pl.when(pl.program_id(0) == 3)
    def _():
        g_ref[...] = tn(left, mixed_ref[...].reshape(rows, d)).astype(bf16)


def input_kernel(
    dp_ref, rg_ref, resg_ref, kept_ref, cot_ref, idx_ref, watt_ref, vec_ref, ing_ref, vecg_ref,
):
    d = kept_ref.shape[2]
    standard, inverse = normalize(kept_ref[0].astype(f32))
    ng = rg_ref[0] * vec_ref[2:3] + nn(dp_ref[0, :, : 3 * d], watt_ref[: 3 * d, :])
    grad = resg_ref[0] + norm_backward(ng, standard, inverse, vec_ref[0:1])
    hot, taken = scatter_matrix(idx_ref, cot_ref.shape[1])
    high = grad.astype(bf16)
    low = (grad - high.astype(f32)).astype(bf16)
    spread = nn(hot, high) + nn(hot, low)
    ing_ref[0] = jnp.where(taken, spread, cot_ref[0].astype(f32))
    sums = jnp.concatenate(
        [colsum(ng * standard), colsum(ng), jnp.zeros((6, d), f32)], axis=0
    )

    @pl.when(pl.program_id(0) == 0)
    def _():
        vecg_ref[...] = jnp.zeros_like(vecg_ref)

    vecg_ref[...] += sums


def scatter_matrix(idx_ref, length):
    hot = (lax.broadcasted_iota(jnp.int32, (length, RI), 0) == idx_ref[0]).astype(f32)
    taken = jnp.sum(hot, axis=-1, keepdims=True) > 0.5
    return hot.astype(bf16), taken


def output_kernel(out_ref, branch_ref, kept_ref, normed_ref, tok_ref, idx_ref, vec_ref, o_ref):
    score = router_score(normed_ref[0], vec_ref)
    residual = kept_ref[0].astype(f32) + score * branch_ref[0]
    result = (residual + out_ref[0] + vec_ref[8:9]).astype(bf16)
    hot, taken = scatter_matrix(idx_ref, tok_ref.shape[1])
    o_ref[0] = jnp.where(taken, nn(hot, result), tok_ref[0].astype(f32)).astype(bf16)


def adamw(grad, first, second, master, average, rate, decay):
    first_new = 0.5 * first + 0.5 * grad
    second_new = 0.5 * second + 0.5 * grad * grad
    update = first_new / (jnp.sqrt(second_new) + 1e-08)
    master_new = master - rate * (update + decay * master)
    average_new = 0.9 * average + 0.1 * master_new
    return (first_new, second_new, master_new, average_new)


def sds(*shape_dtype):
    return jax.ShapeDtypeStruct(shape_dtype[:-1], shape_dtype[-1])


def gather_weights(att_t, ff):
    watt = lax.all_gather(att_t, ("dp", "mp"), axis=0, tiled=True)
    wff = lax.all_gather(ff, "dp", axis=1, tiled=True)
    wff = lax.all_gather(wff, "mp", axis=0, tiled=False)
    return watt, wff


def reduce_grads(gatt, gff):
    gatt = lax.psum_scatter(gatt, ("dp", "mp"), scatter_dimension=0, tiled=True)
    gff = lax.psum_scatter(gff, "mp", scatter_dimension=0, tiled=False)
    gff = lax.psum_scatter(gff, "dp", scatter_dimension=1, tiled=True)
    return gatt.astype(f32), gff.astype(f32)


def per_device(
    tokens, cotangent, kept_index,
    attention_weights, attention_first, attention_second, attention_average,
    feedforward_weights, feedforward_first, feedforward_second, feedforward_average,
    vector_weights, vector_first, vector_second, vector_average,
):
    images, length, d = tokens.shape
    vec = vector_weights
    nmp = lax.axis_size("mp")
    hb = feedforward_weights.shape[2]
    ff = nmp * hb
    fill = lambda n: jnp.full((images, n), -1, jnp.int32)
    idx = jnp.concatenate(
        [
            kept_index[:, :KG], fill(GP - KG),
            kept_index[:, KG : 2 * KG], fill(GP - KG),
            kept_index[:, 2 * KG :], fill(LP - LOC),
        ],
        axis=1,
    )
    idx_col, idx_row = idx[:, :, None], idx[:, None, :]
    mg, ml = masks()

    watt, wff = gather_weights(
        attention_weights.T.astype(bf16), feedforward_weights.astype(bf16)
    )

    kept, normed, cotk = pl.pallas_call(
        gather_kernel,
        grid=(images,),
        in_specs=[per_image(length, d), per_image(length, d), per_image(RI, 1), full(vec.shape)],
        out_specs=[per_image(RI, d)] * 3,
        out_shape=[sds(images, RI, d, bf16)] * 3,
        compiler_params=params(),
        name="gather_norm",
    )(tokens, cotangent, idx_col, vec)

    proj, mixed, branch, n2 = pl.pallas_call(
        forward_kernel,
        grid=(images,),
        in_specs=[
            per_image(RI, d), per_image(RI, d), full(watt.shape), full(vec.shape),
            full(mg.shape), full(ml.shape),
        ],
        out_specs=[per_image(RI, 3 * d), per_image(RI, d), per_image(RI, d), per_image(RI, d)],
        out_shape=[
            sds(images, RI, 3 * d, bf16), sds(images, RI, d, bf16),
            sds(images, RI, d, f32), sds(images, RI, d, bf16),
        ],
        compiler_params=params(),
        name="attention_forward",
    )(normed, kept, watt, vec, mg, ml)

    bias = vec[9:].reshape(nmp, 1, hb)
    whole = lambda *s: pl.BlockSpec(s, lambda j: (0,) * len(s), pipeline_mode=pl.Buffered(1))
    out_acc, n2g, gff, bg = pl.pallas_call(
        feed_kernel,
        grid=(nmp,),
        in_specs=[
            whole(images, RI, d), whole(images, RI, d),
            pl.BlockSpec((1, 2, d, hb), lambda j: (j, 0, 0, 0)),
            pl.BlockSpec((1, 1, hb), lambda j: (j, 0, 0)),
        ],
        out_specs=[
            full((images, RI, d)), full((images, RI, d)),
            pl.BlockSpec((1, 2, d, hb), lambda j: (j, 0, 0, 0)),
            pl.BlockSpec((1, 1, hb), lambda j: (j, 0, 0)),
        ],
        out_shape=[
            sds(images, RI, d, f32), sds(images, RI, d, f32),
            sds(nmp, 2, d, hb, bf16), sds(nmp, 1, hb, f32),
        ],
        scratch_shapes=[pltpu.VMEM((images * RI, hb), bf16), pltpu.VMEM((images * RI, hb), bf16)],
        compiler_params=params(),
        name="feedforward",
    )(n2, cotk, wff, bias)

    dp, resg, rg, vecg = pl.pallas_call(
        backward_kernel,
        grid=(images,),
        in_specs=[
            per_image(RI, d), per_image(RI, d), per_image(RI, d), per_image(RI, d),
            per_image(RI, d), per_image(RI, 3 * d), per_image(RI, d),
            full(watt.shape), full(vec.shape), full(mg.shape), full(ml.shape),
        ],
        out_specs=[per_image(RI, 4 * d), per_image(RI, d), per_image(RI, 1), full((8, d))],
        out_shape=[
            sds(images, RI, 4 * d, bf16), sds(images, RI, d, f32), sds(images, RI, 1, f32),
            sds(8, d, f32),
        ],
        scratch_shapes=[pltpu.VMEM((16, 128), f32), pltpu.VMEM((RI, d), bf16)],
        compiler_params=params(),
        name="attention_backward",
    )(n2g, cotk, branch, kept, normed, proj, mixed, watt, vec, mg, ml)

    gatt = pl.pallas_call(
        grad_kernel,
        grid=(4,),
        in_specs=[
            pl.BlockSpec((images, RI, d), lambda j: (0, 0, j)),
            whole(images, RI, d), whole(images, RI, d),
        ],
        out_specs=pl.BlockSpec((d, d), lambda j: (j, 0)),
        out_shape=sds(4 * d, d, bf16),
        compiler_params=params(),
        name="attention_grads",
    )(dp, normed, mixed)

    input_gradient, vecg_in = pl.pallas_call(
        input_kernel,
        grid=(images,),
        in_specs=[
            per_image(RI, 4 * d), per_image(RI, 1), per_image(RI, d), per_image(RI, d),
            per_image(length, d), per_image(1, RI), full(watt.shape), full(vec.shape),
        ],
        out_specs=[per_image(length, d), full((8, d))],
        out_shape=[sds(images, length, d, f32), sds(8, d, f32)],
        compiler_params=params(),
        name="input_grad",
    )(dp, rg, resg, kept, cotangent, idx_row, watt, vec)

    block_output = pl.pallas_call(
        output_kernel,
        grid=(images,),
        in_specs=[
            per_image(RI, d), per_image(RI, d), per_image(RI, d), per_image(RI, d),
            per_image(length, d), per_image(1, RI), full(vec.shape),
        ],
        out_specs=per_image(length, d),
        out_shape=sds(images, length, d, bf16),
        compiler_params=params(),
        name="block_output",
    )(out_acc, branch, kept, normed, tokens, idx_row, vec)

    gatt, feedforward_gradient = reduce_grads(gatt, gff)
    attention_gradient = gatt.T
    vector_local = jnp.concatenate([vecg_in[:2], vecg[:7], bg.reshape(ff // d, d)], axis=0)
    vector_gradient = lax.psum(vector_local, ("dp", "mp"))
    attention_new = adamw(
        attention_gradient, attention_first, attention_second,
        attention_weights, attention_average, 0.02, 0.05,
    )
    feedforward_new = adamw(
        feedforward_gradient, feedforward_first, feedforward_second,
        feedforward_weights, feedforward_average, 0.02, 0.05,
    )
    vector_new = adamw(
        vector_gradient, vector_first, vector_second, vector_weights, vector_average, 0.2, 0.0
    )
    return (
        block_output, input_gradient,
        attention_gradient, *attention_new, attention_new[2].astype(bf16),
        feedforward_gradient, *feedforward_new, feedforward_new[2].astype(bf16),
        vector_gradient, *vector_new, vector_gradient[3],
    )


def solution(mesh):
    rows = P(("dp", "mp"), None, None)
    att = P(None, ("dp", "mp"))
    feed = P(None, "dp", "mp")
    in_specs = (rows, rows, P(("dp", "mp"), None)) + (att,) * 4 + (feed,) * 4 + (P(),) * 4
    out_specs = (rows, rows) + (att,) * 6 + (feed,) * 6 + (P(),) * 6
    return jax.shard_map(
        per_device, mesh=mesh, in_specs=in_specs, out_specs=out_specs, check_vma=False
    )
```

time: 1010 us -> 653 us (0.65); the launches traced: 997 us -> 652 us
  matrix products: 194 us -> 0 us
  Pallas kernels: 0 us -> 161 us
  local copies, waits for them, and re-layouts: 186 us -> 26.6 us
  other arithmetic: 130 us -> 10.4 us
  waiting for transfers between devices: 430 us -> 397 us
    dot_general x20 -> x0, matrix products: 194 us -> none  [the longest x1 38.2 us: per_device(): jnp.dot(rows_all, feed_rows[0], preferred_element_type=f32) + bias_used]
    pallas_call x0 -> x7, Pallas kernels: none -> 161 us  [the longest x1 46.4 us: per_device(): pl.pallas_call(feed_kernel, grid=(nmp,), in_specs=[whole(images, RI, d),...]
    reshape x13 -> x1, local copies, waits for them, and re-layouts: 66.8 us -> 0.61 us  [per_device(): bias = vec[9:].reshape(nmp, 1, hb)]
    gather x4 -> x0, local copies, waits for them, and re-layouts: 38.1 us -> none  [the longest x2 19.7 us: per_device(): jnp.take_along_axis(cotangent, kept_index[:, :, None], axis=1)]
    convert_element_type x7 -> x1, other arithmetic: 38.5 us -> 1.64 us  [per_device(): attention_weights.T.astype(bf16)]
    unnamed x6 -> x0, other arithmetic: 36.7 us -> none
    unnamed x140 -> x45, local copies, waits for them, and re-layouts: 53.8 us -> 21.9 us
    unnamed x9 -> x6, waiting for transfers between devices: 30.2 us -> 0.1 us
  transfers between devices with their start and end apart: 8 -> 6, of which waited for: 6 -> 6; matrix products, arithmetic and copies ran while one was open for 48% -> 5% of each run, Pallas kernels for 0% -> 18%
where the time goes in v1:
time: 653 us; the launch traced here: 652 us
  waiting for transfers between devices  397 us (61%)
  Pallas kernels  161 us (25%)
  blocking collectives  42.5 us (7%)
  local copies, waits for them, and re-layouts  26.6 us (4%)
  between operations  14.3 us (2%)
  other arithmetic  10.4 us (2%)
    all_gather x1, waiting for transfers between devices, gather_weights(): wff = lax.all_gather(wff, 'mp', axis=0, tiled=False)  136 us
    reduce_scatter x1, waiting for transfers between devices, reduce_grads(): gff = lax.psum_scatter(gff, 'mp', scatter_dimension=0, tiled=False)  113 us
    all_gather x1, waiting for transfers between devices, gather_weights(): watt = lax.all_gather(att_t, ('dp', 'mp'), axis=0, tiled=True)  51 us
    pallas_call x1, Pallas kernels, per_device(): pl.pallas_call(feed_kernel, grid=(nmp,), in_specs=[whole(images, RI, d),...  46.4 us
    reduce_scatter x1, waiting for transfers between devices, reduce_grads(): gff = lax.psum_scatter(gff, 'dp', scatter_dimension=1, tiled=True)  42.5 us
    psum x1, blocking collectives, per_device(): vector_gradient = lax.psum(vector_local, ('dp', 'mp'))  42.5 us
    pallas_call x1, Pallas kernels, per_device(): pl.pallas_call(backward_kernel, grid=(images,), in_specs=[per_image(RI, d...  34.9 us
    all_gather x1, waiting for transfers between devices, gather_weights(): wff = lax.all_gather(ff, 'dp', axis=1, tiled=True)  31.3 us
  transfers between devices with their start and end apart: 6, of which 6 were waited for; matrix products, arithmetic and copies ran while one was open for 5% of the time, Pallas kernels for 18%

profile of v1, /device:TPU:0, one launch (start us, length us, event | category | flops | bytes accessed | tf_op | source)
XLA Modules:
  0.0 652.2 jit_solution(12073057631112950425)
XLA Ops:
  7.2 0.0 all-gather.7.cloned.1.call-start
  7.3 2.0 convert_element_type.21
  9.2 0.0 all-gather.7.cloned.1.call-update
  9.2 0.0 all-gather.5.cloned.1.call-start
  9.3 1.6 convert_bitcast_fusion.1
  10.9 0.0 all-gather.5.cloned.1.call-update
  11.0 0.0 all-gather.9.cloned.1.call-start
  11.0 31.3 %all-gather.7.cloned.1.call-done = bf16[2,768,768]{2,1,0:T(8,128)(2,1)} async-done(((bf16[2,96,768]{2,1,0:T(8,128)(2,1)}), bf16[2,768,768]{2,1,0:T(8,128)(2,1)}) %all-gather.7.cloned.1.call-update) | async-done | bytes 2359312 | tf_op jit(solution)/shard_map/all_gather | solution.py:306
  42.3 0.0 all-gather.9.cloned.1.call-update
  42.3 0.0 reduce-scatter.6.cloned.1.call-start
  42.3 0.1 slice.23
  42.4 0.7 slice.24
  43.2 0.6 reshape.46.bias_ref
  43.8 0.1 fusion.8
  43.8 0.1 concatenate.6
  43.9 1.1 copy.46.idx_ref
  45.0 2.1 copy.44.tok_ref
  47.2 1.0 copy-done.1
  48.2 2.1 copy.45.cot_ref
  50.3 7.9 %gather_norm.1 = (bf16[4,304,768]{2,1,0:T(8,128)(2,1)}, bf16[4,304,768]{2,1,0:T(8,128)(2,1)}, bf16[4,304,768]{2,1,0:T(8,128)(2,1)}) custom-call(bf16[4,542,768]{2,1,0:T(8,128)(2,1)} %copy.44.tok_ref, bf16[4,542,768]{2,1,0:T(8,128)(2,1)} %copy.45.cot_ref, s32[4,304,1]{2,1,0:T(8,128)} %copy.46.idx_ref, f32[13,768]{1,0:T(8,128)} %vec_ref.9), custom_call_target="tpu_custom_call" | custom-call | tf_op jit(solution)/shard_map/gather_norm/pallas_call | solution.py:345
  58.2 51.0 %all-gather.5.cloned.1.call-done.watt_ref = bf16[3072,768]{1,0:T(8,128)(2,1)} async-done(((bf16[96,768]{1,0:T(8,128)(2,1)}), bf16[3072,768]{1,0:T(8,128)(2,1)}) %all-gather.5.cloned.1.call-update) | async-done | bytes 4718608 | tf_op jit(solution)/shard_map/all_gather | solution.py:305
  109.2 31.0 %attention_forward.1 = (bf16[4,304,2304]{2,1,0:T(8,128)(2,1)}, bf16[4,304,768]{2,1,0:T(8,128)(2,1)}, f32[4,304,768]{2,1,0:T(8,128)}, bf16[4,304,768]{2,1,0:T(8,128)(2,1)}) custom-call(bf16[4,304,768]{2,1,0:T(8,128)(2,1)} %get-tuple-element.37.normed_ref, bf16[4,304,768]{2,1,0:T(8,128)(2,1)} %get-tuple-element.38.kept_ref, ...), custom_call_target="tpu_custom_call" | custom-call | tf_op jit(solution)/shard_map/attention_forward/pallas_call | solution.py:355
  140.2 136.3 %all-gather.9.cloned.1.call-done = bf16[8,768,768]{2,1,0:T(8,128)(2,1)} async-done(((bf16[2,768,768]{2,1,0:T(8,128)(2,1)}), bf16[8,768,768]{2,1,0:T(8,128)(2,1)}) %all-gather.9.cloned.1.call-update) | async-done | bytes 9437200 | tf_op jit(solution)/shard_map/all_gather | solution.py:307
  276.5 46.4 %feedforward.1 = (f32[4,304,768]{2,1,0:T(8,128)}, f32[4,304,768]{2,1,0:T(8,128)}, bf16[4,2,768,768]{3,2,1,0:T(8,128)(2,1)}, f32[4,1,768]{2,1,0:T(1,128)}) custom-call(bf16[4,304,768]{2,1,0:T(8,128)(2,1)} %get-tuple-element.39.n2_ref, bf16[4,304,768]{2,1,0:T(8,128)(2,1)} %get-tuple-element.40.cot_ref.cotk_ref, bf16[4,2,768,768]{3,2,1,0:T(8,128)(2,1)} %bitcast.12, ...), custom_call_target="tpu_custom_call" | custom-call | tf_op jit(solution)/shard_map/feedforward/pallas_call | solution.py:373
  322.9 0.0 reduce-scatter.6.cloned.1.call-update
  322.9 0.2 reduce-scatter.4.cloned.1.call-start
  323.1 34.9 %attention_backward.1 = (bf16[4,304,3072]{2,1,0:T(8,128)(2,1)}, f32[4,304,768]{2,1,0:T(8,128)}, f32[4,304,1]{2,1,0:T(8,128)}, f32[8,768]{1,0:T(8,128)}) custom-call(f32[4,304,768]{2,1,0:T(8,128)} %get-tuple-element.43.n2g_ref, bf16[4,304,768]{2,1,0:T(8,128)(2,1)} %get-tuple-element.40.cot_ref.cotk_ref, f32[4,304,768]{2,1,0:T(8,128)} %get-tuple-element.42.branch_ref, ...), custom_call_target="tpu_custom_call" | custom-call | tf_op jit(solution)/shard_map/attention_backward/pallas_call | solution.py:395
  358.0 11.4 %attention_grads.1 = bf16[3072,768]{1,0:T(8,128)(2,1)} custom-call(bf16[4,304,3072]{2,1,0:T(8,128)(2,1)} %get-tuple-element.46.dp_ref, bf16[4,304,768]{2,1,0:T(8,128)(2,1)} %get-tuple-element.37.normed_ref, bf16[4,304,768]{2,1,0:T(8,128)(2,1)} %get-tuple-element.45.mixed_ref), custom_call_target="tpu_custom_call" | custom-call | tf_op jit(solution)/shard_map/attention_grads/pallas_call | solution.py:413
  369.4 0.0 reduce-scatter.4.cloned.1.call-update
  369.4 0.3 reduce-scatter.8.cloned.1.call-start
  369.7 112.8 %reduce-scatter.6.cloned.1.call-done = bf16[1,2,768,768]{3,2,1,0:T(8,128)(2,1)} async-done(((bf16[4,2,768,768]{3,2,1,0:T(8,128)(2,1)}), bf16[1,2,768,768]{3,2,1,0:T(8,128)(2,1)}) %reduce-scatter.6.cloned.1.call-update) | async-done | bytes 2359312 | tf_op jit(solution)/shard_map/reduce_scatter | solution.py:313
  482.5 0.0 reduce-scatter.8.cloned.1.call-update
  482.5 0.6 broadcast_in_dim.11.idx_ref
  483.1 8.9 %block_output.1 = bf16[4,542,768]{2,1,0:T(8,128)(2,1)} custom-call(f32[4,304,768]{2,1,0:T(8,128)} %get-tuple-element.41.out_ref, f32[4,304,768]{2,1,0:T(8,128)} %get-tuple-element.42.branch_ref, bf16[4,304,768]{2,1,0:T(8,128)(2,1)} %get-tuple-element.38.kept_ref, bf16[4,304,768]{2,1,0:T(8,128)(2,1)} %get-tuple-element.37.normed_ref, ...), custom_call_target="tpu_custom_call" | custom-call | tf_op jit(solution)/shard_map/block_output/pallas_call | solution.py:439
  492.0 6.2 copy.49
  498.2 20.2 %input_grad.1 = (f32[4,542,768]{2,1,0:T(8,128)}, f32[8,768]{1,0:T(8,128)}) custom-call(bf16[4,304,3072]{2,1,0:T(8,128)(2,1)} %get-tuple-element.46.dp_ref, f32[4,304,1]{2,1,0:T(8,128)} %get-tuple-element.47.rg_ref, f32[4,304,768]{2,1,0:T(8,128)} %get-tuple-element.48.resg_ref, bf16[4,304,768]{2,1,0:T(8,128)(2,1)} %get-tuple-element.38.kept_ref, ...), custom_call_target="tpu_custom_call" | custom-call | tf_op jit(solution)/shard_map/input_grad/pallas_call | solution.py:426
  518.6 10.3 %copy.50 = f32[4,542,768]{2,0,1:T(4,128)} copy(f32[4,542,768]{2,1,0:T(8,128)} %get-tuple-element.75) | data formatting | bytes 13320192
  528.8 0.9 slice.25
  529.7 42.5 %psum.7 = f32[13,768]{1,0:T(8,128)S(1)} all-reduce(f32[13,768]{1,0:T(8,128)S(1)} %pad_maximum_fusion), channel_id=1, replica_groups=mesh['dp'=8,'mp'=4] {'dp','mp'}, use_global_device_ids=true, to_apply=%region_3.0 | all-reduce | flops 9984 | bytes 79872 | tf_op jit(solution)/shard_map/psum | solution.py:455
  572.2 0.0 copy-start.13
  572.2 0.6 slice_reduce_fusion
  572.8 0.7 multiply_add_fusion.5
  573.5 23.2 %reduce-scatter.4.cloned.1.call-done = bf16[96,768]{1,0:T(8,128)(2,1)} async-done(((bf16[3072,768]{1,0:T(8,128)(2,1)}), bf16[96,768]{1,0:T(8,128)(2,1)}) %reduce-scatter.4.cloned.1.call-update) | async-done | bytes 147472 | tf_op jit(solution)/shard_map/reduce_scatter | solution.py:312
  596.7 1.9 fusion.6
  598.7 0.8 multiply_add_fusion.3
  599.4 42.5 %reduce-scatter.8.cloned.1.call-done = bf16[2,96,768]{2,1,0:T(8,128)(2,1)} async-done(((bf16[2,768,768]{2,1,0:T(8,128)(2,1)}), bf16[2,96,768]{2,1,0:T(8,128)(2,1)}) %reduce-scatter.8.cloned.1.call-update) | async-done | bytes 294928 | tf_op jit(solution)/shard_map/reduce_scatter | solution.py:314
  641.9 2.4 fusion.4
  644.3 1.0 multiply_add_fusion.1
  (42 shorter events, 0.1 us)
Async XLA Ops:
  7.2 35.1 %copy-start.19 = (s32[4,268]{1,0:T(4,128)S(1)}, s32[4,268]{1,0:T(4,128)}, u32[]{:S(2)}) copy-start(s32[4,268]{1,0:T(4,128)} %param.19) | copy-start | bytes 12868
  7.2 37.8 %copy-start = (bf16[4,542,768]{2,0,1:T(4,128)(2,1)S(1)}, bf16[4,542,768]{2,0,1:T(4,128)(2,1)}, u32[]{:S(2)}) copy-start(bf16[4,542,768]{2,0,1:T(4,128)(2,1)} %param.17) | copy-start | bytes 9990148
  7.2 35.1 %all-gather.7.cloned.1.call-start = ((), (), s32[]{:S(2)}) async-start(), calls=%async_computation.4 | async-start | bytes 2654208 | tf_op jit(solution)/shard_map/all_gather | solution.py:306
  9.2 100.0 %all-gather.5.cloned.1.call-start = ((), (), s32[]{:S(2)}) async-start(), calls=%async_computation.3 | async-start | bytes 4866048 | tf_op jit(solution)/shard_map/all_gather | solution.py:305
  11.0 265.5 %all-gather.9.cloned.1.call-start = ((), (), s32[]{:S(2)}) async-start(), calls=%async_computation.8 | async-start | bytes 11796480 | tf_op jit(solution)/shard_map/all_gather | solution.py:307
  42.3 440.2 %reduce-scatter.6.cloned.1.call-start = ((), (), s32[]{:S(2)}) async-start(), calls=%async_computation.6 | async-start | bytes 11796480 | tf_op jit(solution)/shard_map/reduce_scatter | solution.py:313
  45.0 3.1 copy-start.1
  322.9 273.8 %reduce-scatter.4.cloned.1.call-start = ((), (), s32[]{:S(2)}) async-start(), calls=%async_computation.5 | async-start | bytes 4866048 | tf_op jit(solution)/shard_map/reduce_scatter | solution.py:312
  369.4 272.5 %reduce-scatter.8.cloned.1.call-start = ((), (), s32[]{:S(2)}) async-start(), calls=%async_computation.7 | async-start | bytes 2654208 | tf_op jit(solution)/shard_map/reduce_scatter | solution.py:314
  518.4 11.3 %copy-start.18 = (f32[4,1,768]{2,1,0:T(1,128)S(1)}, f32[4,1,768]{2,1,0:T(1,128)}, u32[]{:S(2)}) copy-start(f32[4,1,768]{2,1,0:T(1,128)} %get-tuple-element.53) | copy-start | bytes 36868
  518.4 11.3 %copy-start.17 = (f32[8,768]{1,0:T(8,128)S(1)}, f32[8,768]{1,0:T(8,128)}, u32[]{:S(2)}) copy-start(f32[8,768]{1,0:T(8,128)} %get-tuple-element.52) | copy-start | bytes 73732
  518.5 54.4 %copy-start.4 = (f32[13,768]{1,0:T(8,128)S(1)}, f32[13,768]{1,0:T(8,128)}, u32[]{:S(2)}) copy-start(f32[13,768]{1,0:T(8,128)} %vec_ref.9) | copy-start | bytes 119812
  518.5 54.4 %copy-start.14 = (f32[13,768]{1,0:T(8,128)S(1)}, f32[13,768]{1,0:T(8,128)}, u32[]{:S(2)}) copy-start(f32[13,768]{1,0:T(8,128)} %param.31) | copy-start | bytes 119812
  518.5 54.4 %copy-start.15 = (f32[13,768]{1,0:T(8,128)S(1)}, f32[13,768]{1,0:T(8,128)}, u32[]{:S(2)}) copy-start(f32[13,768]{1,0:T(8,128)} %param.30) | copy-start | bytes 119812
  518.5 54.3 %copy-start.16 = (f32[13,768]{1,0:T(8,128)S(1)}, f32[13,768]{1,0:T(8,128)}, u32[]{:S(2)}) copy-start(f32[13,768]{1,0:T(8,128)} %param.29) | copy-start | bytes 119812
  518.5 78.2 %copy-start.6 = (f32[768,96]{0,1:T(8,128)S(1)}, f32[768,96]{0,1:T(8,128)}, u32[]{:S(2)}) copy-start(f32[768,96]{0,1:T(8,128)} %param.20) | copy-start | bytes 884740
  518.5 78.2 %copy-start.10 = (f32[768,96]{0,1:T(8,128)S(1)}, f32[768,96]{0,1:T(8,128)}, u32[]{:S(2)}) copy-start(f32[768,96]{0,1:T(8,128)} %param.22) | copy-start | bytes 884740
  518.5 78.2 %copy-start.11 = (f32[768,96]{0,1:T(8,128)S(1)}, f32[768,96]{0,1:T(8,128)}, u32[]{:S(2)}) copy-start(f32[768,96]{0,1:T(8,128)} %param.21) | copy-start | bytes 884740
  518.5 80.1 %copy-start.12 = (f32[768,96]{0,1:T(8,128)S(1)}, f32[768,96]{0,1:T(8,128)}, u32[]{:S(2)}) copy-start(f32[768,96]{0,1:T(8,128)} %param.23) | copy-start | bytes 884740
  528.8 113.1 %copy-start.3 = (f32[2,96,768]{2,1,0:T(8,128)S(1)}, f32[2,96,768]{2,1,0:T(8,128)}, u32[]{:S(2)}) copy-start(f32[2,96,768]{2,1,0:T(8,128)} %param.24) | copy-start | bytes 1769476
  528.8 113.1 %copy-start.7 = (f32[2,96,768]{2,1,0:T(8,128)S(1)}, f32[2,96,768]{2,1,0:T(8,128)}, u32[]{:S(2)}) copy-start(f32[2,96,768]{2,1,0:T(8,128)} %param.26) | copy-start | bytes 1769476
  528.8 113.1 %copy-start.8 = (f32[2,96,768]{2,1,0:T(8,128)S(1)}, f32[2,96,768]{2,1,0:T(8,128)}, u32[]{:S(2)}) copy-start(f32[2,96,768]{2,1,0:T(8,128)} %param.25) | copy-start | bytes 1769476
  572.2 72.1 %copy-start.13 = (f32[13,768]{1,0:T(8,128)}, f32[13,768]{1,0:T(8,128)S(1)}, u32[]{:S(2)}) copy-start(f32[13,768]{1,0:T(8,128)S(1)} %psum.7) | copy-start | bytes 119812
  598.6 46.7 %copy-start.5 = (f32[768,96]{0,1:T(8,128)}, f32[768,96]{0,1:T(8,128)S(1)}, u32[]{:S(2)}) copy-start(f32[768,96]{0,1:T(8,128)S(1)} %get-tuple-element.104) | copy-start | bytes 884740
  598.7 45.7 %copy-start.9 = (f32[2,96,768]{2,1,0:T(8,128)S(1)}, f32[2,96,768]{2,1,0:T(8,128)}, u32[]{:S(2)}) copy-start(f32[2,96,768]{2,1,0:T(8,128)} %param.27) | copy-start | bytes 1769476
  644.3 1.0 copy-start.2
Sparse Core Ops, SparseCore 0:
  10.5 31.7 all-gather.6
  45.6 63.5 all-gather.4
  110.8 165.6 all-gather.8
  323.0 159.4 reduce-scatter.5
  487.8 108.8 reduce-scatter.3
  600.3 41.5 reduce-scatter.7

commit v2 on v1

--- a/solution.py
+++ b/solution.py
@@ -15,10 +15,10 @@
 KG = LG // 2
 KL = LL // 2
 LOC = 4 * KL
-GP = -(-KG // 16) * 16
-LP = -(-LOC // 16) * 16
-RI = 2 * GP + LP
-UNITS = ((0, GP), (GP, GP), (2 * GP, LP))
+KEPT = 2 * KG + LOC
+RI = -(-KEPT // 16) * 16
+SPANS = ((0, KG), (KG, 2 * KG), (2 * KG, KEPT))
+UNITS = tuple((a // 16 * 16, -(-b // 16) * 16) for a, b in SPANS)
 PAIRS = H // 2
 W2L = 2 * HD
 
@@ -71,14 +71,18 @@
 
 
 def masks():
-    key = np.arange(GP)[:, None]
-    query = np.zeros((1, GP), np.int64)
-    mg = np.where((key < KG) & (query == 0), 0.0, -1e9)
-    key = np.arange(LP)[:, None]
-    query = np.arange(LP)[None, :]
-    ml = np.where((key < LOC) & (key // KL == query // KL), 0.0, -1e9)
-    two = lambda m: jnp.asarray(np.concatenate([m, m], 1), f32)
-    return two(mg), two(ml)
+    crop = np.full(RI, -1)
+    crop[:KG], crop[KG : 2 * KG] = 0, 1
+    for c in range(4):
+        crop[2 * KG + c * KL : 2 * KG + (c + 1) * KL] = 2 + c
+    adds, valids = [], []
+    for (a, b), (lo, hi) in zip(SPANS, UNITS):
+        rows = np.arange(lo, hi)
+        inside = (rows >= a) & (rows < b)
+        same = (crop[lo:hi, None] == crop[None, lo:hi]) & inside[:, None] & inside[None, :]
+        adds.append(np.tile(np.where(same, 0.0, -1e9), (1, 2)).astype(np.float32))
+        valids.append(np.tile(inside[None, :].astype(np.float32), (8, 2)))
+    return [jnp.asarray(m) for m in adds + valids]
 
 
 def lane_half(shape):
@@ -98,9 +102,18 @@
     return jnp.where(lane_half((n, v.shape[1])), v[:n], v[n:])
 
 
-def softmax_keys(st):
+def softmax_keys(st, valid):
     p = jnp.exp(st - jnp.max(st, axis=0, keepdims=True))
-    return p * (1.0 / jnp.sum(p, axis=0, keepdims=True))
+    return p * (valid / jnp.sum(p, axis=0, keepdims=True))
+
+
+def store_window(ref, lo, hi, last, cols, value, tail):
+    value = value.astype(bf16)
+    if tail is not None:
+        value = jnp.concatenate([value[:16] + tail, value[16:]], axis=0)
+    end = hi if last else hi - 16
+    ref[0, lo:end, cols] = value[: end - lo]
+    return None if last else value[end - lo :]
 
 
 def gather_kernel(tok_ref, cot_ref, idx_ref, vec_ref, kept_ref, normed_ref, cotk_ref):
@@ -120,7 +133,7 @@
 
 
 def forward_kernel(
-    normed_ref, kept_ref, watt_ref, vec_ref, mg_ref, ml_ref,
+    normed_ref, kept_ref, watt_ref, vec_ref, m0_ref, m1_ref, m2_ref, v0_ref, v1_ref, v2_ref,
     proj_ref, mixed_ref, branch_ref, n2_ref,
 ):
     d = normed_ref.shape[2]
@@ -130,16 +143,16 @@
         if row is not None:
             part = part + vec_ref[row : row + 1]
         proj_ref[0, :, j * d : (j + 1) * d] = part.astype(bf16)
-    for start, n in UNITS:
-        mask_ref = mg_ref if n == GP else ml_ref
-        for pair in range(PAIRS):
-            cols = lambda j: slice(j * d + pair * W2L, j * d + (pair + 1) * W2L)
-            rows = slice(start, start + n)
-            qs = split_heads(proj_ref[0, rows, cols(0)], HD ** -0.5)
-            st = nt(proj_ref[0, rows, cols(1)], qs) + mask_ref[...]
-            pt = softmax_keys(st).astype(bf16)
-            out = tn(pt, proj_ref[0, rows, cols(2)])
-            mixed_ref[0, rows, pair * W2L : (pair + 1) * W2L] = join_heads(out).astype(bf16)
+    mrefs, vrefs = (m0_ref, m1_ref, m2_ref), (v0_ref, v1_ref, v2_ref)
+    for pair in range(PAIRS):
+        cols = lambda j: slice(j * d + pair * W2L, j * d + (pair + 1) * W2L)
+        tail = None
+        for unit, (lo, hi) in enumerate(UNITS):
+            qs = split_heads(proj_ref[0, lo:hi, cols(0)], HD ** -0.5)
+            st = nt(proj_ref[0, lo:hi, cols(1)], qs) + mrefs[unit][...]
+            pt = softmax_keys(st, vrefs[unit][0:1]).astype(bf16)
+            out = join_heads(tn(pt, proj_ref[0, lo:hi, cols(2)]))
+            tail = store_window(mixed_ref, lo, hi, unit == 2, cols(0), out, tail)
     branch = nt(mixed_ref[0], watt_ref[3 * d :, :]) + vec_ref[5:6]
     branch_ref[0] = branch
     residual = kept_ref[0].astype(f32) + router_score(normed, vec_ref) * branch
@@ -183,7 +196,8 @@
 
 def backward_kernel(
     n2g_ref, cotk_ref, branch_ref, kept_ref, normed_ref, proj_ref, mixed_ref, watt_ref,
-    vec_ref, mg_ref, ml_ref, dp_ref, resg_ref, rg_ref, vecg_ref, dproj_s, mg_s,
+    vec_ref, m0_ref, m1_ref, m2_ref, v0_ref, v1_ref, v2_ref, dp_ref, resg_ref, rg_ref, vecg_ref,
+    mg_s,
 ):
     d = normed_ref.shape[2]
     normed = normed_ref[0]
@@ -200,21 +214,22 @@
     rg_ref[0] = rg
     dp_ref[0, :, 3 * d :] = bg
     mg_s[...] = nn(bg, watt_ref[3 * d :, :]).astype(bf16)
-    for start, n in UNITS:
-        mask_ref = mg_ref if n == GP else ml_ref
-        rows = slice(start, start + n)
-        for pair in range(PAIRS):
-            cols = lambda j: slice(j * d + pair * W2L, j * d + (pair + 1) * W2L)
-            qs = split_heads(proj_ref[0, rows, cols(0)], HD ** -0.5)
-            kk = proj_ref[0, rows, cols(1)]
-            pt = softmax_keys(nt(kk, qs) + mask_ref[...])
-            ds = split_heads(mg_s[rows, cols(0)], 1.0)
-            gpt = nt(proj_ref[0, rows, cols(2)], ds)
+    mrefs, vrefs = (m0_ref, m1_ref, m2_ref), (v0_ref, v1_ref, v2_ref)
+    for pair in range(PAIRS):
+        cols = lambda j: slice(j * d + pair * W2L, j * d + (pair + 1) * W2L)
+        tails = [None] * 3
+        for unit, (lo, hi) in enumerate(UNITS):
+            qs = split_heads(proj_ref[0, lo:hi, cols(0)], HD ** -0.5)
+            kk = proj_ref[0, lo:hi, cols(1)]
+            pt = softmax_keys(nt(kk, qs) + mrefs[unit][...], vrefs[unit][0:1])
+            ds = split_heads(mg_s[lo:hi, cols(0)], 1.0)
+            gpt = nt(proj_ref[0, lo:hi, cols(2)], ds)
             sg = (pt * (gpt - jnp.sum(pt * gpt, axis=0, keepdims=True))).astype(bf16)
-            qg = join_heads(tn(sg, kk)) * HD ** -0.5
-            dp_ref[0, rows, cols(0)] = qg.astype(bf16)
-            dp_ref[0, rows, cols(1)] = nn(sg, qs).astype(bf16)
-            dp_ref[0, rows, cols(2)] = nn(pt.astype(bf16), ds).astype(bf16)
+            grads = (
+                join_heads(tn(sg, kk)) * HD ** -0.5, nn(sg, qs), nn(pt.astype(bf16), ds)
+            )
+            for j in range(3):
+                tails[j] = store_window(dp_ref, lo, hi, unit == 2, cols(j), grads[j], tails[j])
     zero = jnp.zeros((1, d), f32)
     sums = jnp.concatenate(
         [
@@ -301,18 +316,339 @@
     return jax.ShapeDtypeStruct(shape_dtype[:-1], shape_dtype[-1])
 
 
+MESH = pl.DeviceIdType.MESH
+ANY = pl.BlockSpec(memory_space=pl.ANY)
+MP = 4
+
+def flip(index, bit):
+    return index + bit * (1 - 2 * lax.rem(lax.div(index, bit), 2))
+
+
+class Place:
+    def __init__(self):
+        self.dp = lax.axis_index("dp")
+        self.z = lax.axis_index("mp")
+        core, x, y = flip(self.dp, 1), flip(self.dp, 2), flip(self.dp, 4)
+        self.core, self.x, self.y = (core, self.z), (x, self.z), (y, self.z)
+        self.chips = (self.dp, x, y, flip(x, 4))
+        self.mates = tuple(flip(c, 1) for c in self.chips)
+
+    def up(self, k):
+        return lax.rem(self.z + k, MP)
+
+    def down(self, k):
+        return lax.rem(self.z + MP - k, MP)
+
+    def line(self, k):
+        return (self.dp, self.up(k))
+
+    def barrier(self):
+        sem = pltpu.get_barrier_semaphore()
+        others = [self.core, self.x, self.y] + [self.line(k) for k in range(1, MP)]
+        for other in others:
+            pl.semaphore_signal(sem, inc=1, device_id=other, device_id_type=MESH)
+        pl.semaphore_wait(sem, len(others))
+
+
+def att_block(ref, dp, z, rows):
+    return ref.at[pl.ds(pl.multiple_of((dp * MP + z) * rows, 32), rows), :]
+
+
+def ff_block(ref, dp, z, rows):
+    return ref.at[z, :, pl.ds(pl.multiple_of(dp * rows, 32), rows), :]
+
+
+Z0, X0, Y0, D0, C0 = 0, 3, 7, 11, 15
+SLOTS = 31
+
+
+def gather_links_kernel(att_ref, ff_ref, watt_ref, wff_ref, send, recv, local):
+    at = Place()
+    at.barrier()
+    rows = att_ref.shape[0]
+    tensors = ((att_ref, watt_ref, att_block), (ff_ref, wff_ref, ff_block))
+    started = []
+
+    def copy(t, slot, r, k, to):
+        mine, out, block = tensors[t]
+        dst = block(out, at.chips[r], at.down(k), rows)
+        src = mine if (r, k) == (0, 0) else dst
+        c = pltpu.make_async_remote_copy(
+            src_ref=src, dst_ref=dst, send_sem=send.at[t, slot], recv_sem=recv.at[t, slot],
+            device_id=to, device_id_type=MESH,
+        )
+        c.start()
+        started.append(c)
+
+    def arrived(t, slot, dp, k):
+        mine, out, block = tensors[t]
+        dst = block(out, dp, at.down(k), rows)
+        pltpu.make_async_remote_copy(
+            src_ref=dst, dst_ref=dst, send_sem=send.at[t, slot], recv_sem=recv.at[t, slot],
+            device_id=at.core, device_id_type=MESH,
+        ).wait_recv()
+
+    def spread(t, k):
+        copy(t, X0 + k, 0, k, at.x)
+        copy(t, Y0 + k, 0, k, at.y)
+        copy(t, C0 + k, 0, k, at.core)
+
+    def begin(t):
+        for k in range(1, MP):
+            copy(t, Z0 + k - 1, 0, 0, at.line(k))
+        spread(t, 0)
+
+    locals_ = []
+    for t, (mine, out, block) in enumerate(tensors):
+        c = pltpu.make_async_copy(mine, block(out, at.dp, at.z, rows), local.at[t])
+        c.start()
+        locals_.append(c)
+    begin(0)
+    begin(1)
+    for t in range(2):
+        for k in range(1, MP):
+            arrived(t, Z0 + k - 1, at.dp, k)
+            spread(t, k)
+        for k in range(MP):
+            arrived(t, X0 + k, at.chips[1], k)
+            copy(t, C0 + 4 + k, 1, k, at.core)
+            if k < 2:
+                copy(t, D0 + k, 1, k, at.y)
+            arrived(t, Y0 + k, at.chips[2], k)
+            copy(t, C0 + 8 + k, 2, k, at.core)
+            if k >= 2:
+                copy(t, D0 + k, 2, k, at.x)
+        for k in range(MP):
+            arrived(t, D0 + k, at.chips[3], k)
+            copy(t, C0 + 12 + k, 3, k, at.core)
+    for t in range(2):
+        for r in range(4):
+            for k in range(MP):
+                arrived(t, C0 + 4 * r + k, at.mates[r], k)
+    for c in started:
+        c.wait_send()
+    for c in locals_:
+        c.wait()
+
+
+def gather_weights_links(att, ff):
+    rows, d = att.shape
+    hb = ff.shape[2]
+    n = rows * 32
+    return pl.pallas_call(
+        gather_links_kernel,
+        in_specs=[ANY, ANY],
+        out_specs=[ANY, ANY],
+        out_shape=[
+            jax.ShapeDtypeStruct((n, d), bf16), jax.ShapeDtypeStruct((MP, 2, 8 * rows, hb), bf16)
+        ],
+        scratch_shapes=[
+            pltpu.SemaphoreType.DMA((2, SLOTS)), pltpu.SemaphoreType.DMA((2, SLOTS)),
+            pltpu.SemaphoreType.DMA((2,)),
+        ],
+        compiler_params=pltpu.CompilerParams(collective_id=0, has_side_effects=True),
+        name="gather_weights",
+    )(att, ff)
+
+
+def add_into(dst, *srcs, out=None):
+    step = 32
+    rows = dst.shape[0]
+    target = dst if out is None else out
+
+    def body(i, _):
+        s = pl.ds(pl.multiple_of(i * step, step), step)
+        total = dst[s, :].astype(f32)
+        for r in srcs:
+            total = total + r[s, :].astype(f32)
+        target[s, :] = total.astype(target.dtype)
+        return 0
+
+    lax.fori_loop(0, rows // step, body, 0)
+
+
+def scatter_links_kernel(
+    gatt_ref, gff_ref, vec_ref, oatt_ref, off_ref, ovec_ref,
+    a0, a1, c0, c1, d0, d1, x0, x1, y0, y1, z0, z1, vbuf, send, recv, local, vsend, vrecv,
+):
+    at = Place()
+    at.barrier()
+    rows = oatt_ref.shape[0]
+    tensors = (
+        (gatt_ref, att_block, a0, c0, d0, x0, y0, z0, oatt_ref),
+        (gff_ref, ff_block, a1, c1, d1, x1, y1, z1, off_ref),
+    )
+    started = []
+
+    def remote(t, slot, src, dst, to):
+        c = pltpu.make_async_remote_copy(
+            src_ref=src, dst_ref=dst, send_sem=send.at[t, slot], recv_sem=recv.at[t, slot],
+            device_id=to, device_id_type=MESH,
+        )
+        c.start()
+        started.append(c)
+
+    def arrived(t, slot, dst):
+        pltpu.make_async_remote_copy(
+            src_ref=dst, dst_ref=dst, send_sem=send.at[t, slot], recv_sem=recv.at[t, slot],
+            device_id=at.core, device_id_type=MESH,
+        ).wait_recv()
+
+    loads = {}
+    for t in range(2):
+        g, block, a, c = tensors[t][:4]
+        for r in (3, 1, 2, 0):
+            for k in range(MP):
+                i = 4 * r + k
+                src = block(g, at.mates[r], at.down(k), rows)
+                remote(t, C0 + i, src, c.at[i], at.core)
+                own = pltpu.make_async_copy(
+                    block(g, at.chips[r], at.down(k), rows), a.at[i], local.at[t, i]
+                )
+                own.start()
+                loads[t, i] = own
+
+    vbuf[0] = vec_ref[...]
+    for step, to in enumerate((at.core, at.x, at.y)):
+        c = pltpu.make_async_remote_copy(
+            src_ref=vbuf.at[step], dst_ref=vbuf.at[8 + step], send_sem=vsend.at[step],
+            recv_sem=vrecv.at[step], device_id=to, device_id_type=MESH,
+        )
+        c.start()
+        c.wait()
+        vbuf[step + 1] = vbuf[step] + vbuf[8 + step]
+    zc = []
+    for k in range(1, MP):
+        c = pltpu.make_async_remote_copy(
+            src_ref=vbuf.at[3], dst_ref=vbuf.at[10 + k], send_sem=vsend.at[2 + k],
+            recv_sem=vrecv.at[2 + k], device_id=at.line(k), device_id_type=MESH,
+        )
+        c.start()
+        zc.append(c)
+
+    def ref2(buf, i):
+        return buf.at[i]
+
+    for t in range(2):
+        g, block, a, c, d, x, y, z, o = tensors[t]
+
+        def gather_in(i):
+            loads[t, i].wait()
+            arrived(t, C0 + i, c.at[i])
+
+        segs = range(1) if t == 0 else range(2)
+        view = (lambda b, i: [b.at[i]]) if t == 0 else (lambda b, i: [b.at[i, 0], b.at[i, 1]])
+
+        def accumulate(i, *bufs):
+            for s, dst in enumerate(view(a, i)):
+                add_into(dst, *[view(b, j)[s] for b, j in bufs])
+
+        for k in range(MP):
+            i = 12 + k
+            gather_in(i)
+            accumulate(i, (c, i))
+            remote(t, D0 + k, a.at[i], d.at[k], at.x if k < 2 else at.y)
+        for k in (0, 1):
+            i = 4 + k
+            gather_in(i)
+            accumulate(i, (c, i))
+            remote(t, X0 + k, a.at[i], x.at[k], at.x)
+        for k in (2, 3):
+            i = 8 + k
+            gather_in(i)
+            accumulate(i, (c, i))
+            remote(t, Y0 + k, a.at[i], y.at[k], at.y)
+        for k in (2, 3):
+            i = 4 + k
+            gather_in(i)
+            arrived(t, D0 + k, d.at[k])
+            accumulate(i, (c, i), (d, k))
+            remote(t, X0 + k, a.at[i], x.at[k], at.x)
+        for k in (0, 1):
+            i = 8 + k
+            gather_in(i)
+            arrived(t, D0 + k, d.at[k])
+            accumulate(i, (c, i), (d, k))
+            remote(t, Y0 + k, a.at[i], y.at[k], at.y)
+        for k in (1, 2, 3, 0):
+            gather_in(k)
+            arrived(t, X0 + k, x.at[k])
+            arrived(t, Y0 + k, y.at[k])
+            if k:
+                accumulate(k, (c, k), (x, k), (y, k))
+                remote(t, Z0 + k - 1, a.at[k], z.at[k - 1], (at.dp, at.down(k)))
+        for k in range(1, MP):
+            arrived(t, Z0 + k - 1, z.at[k - 1])
+        for s in segs:
+            out = o if t == 0 else o.at[s]
+            add_into(
+                view(a, 0)[s], view(c, 0)[s], view(x, 0)[s], view(y, 0)[s],
+                *[view(z, k)[s] for k in range(3)], out=out,
+            )
+    for c in zc:
+        c.wait()
+    total = None
+    own = at.z
+    parts = [vbuf[3], vbuf[11], vbuf[12], vbuf[13]]
+    for zz in range(MP):
+        k = lax.rem(own + MP - zz, MP)
+        term = jnp.where(k == 0, parts[0], jnp.where(k == 1, parts[1], jnp.where(k == 2, parts[2], parts[3])))
+        total = term if total is None else total + term
+    ovec_ref[...] = total
+    for c in started:
+        c.wait_send()
+
+
+def reduce_grads_links(gatt, gff, vec):
+    d = gatt.shape[1]
+    rows = gatt.shape[0] // 32
+    hb = gff.shape[3]
+    V = pltpu.VMEM
+    shapes = []
+    for n in (16, 16, 4, 4, 4, 3):
+        shapes += [V((n, rows, d), bf16), V((n, 2, rows, hb), bf16)]
+    vm = pl.BlockSpec(memory_space=pltpu.VMEM)
+    return pl.pallas_call(
+        scatter_links_kernel,
+        in_specs=[ANY, ANY, vm],
+        out_specs=[vm, vm, vm],
+        out_shape=[
+            jax.ShapeDtypeStruct((rows, d), f32), jax.ShapeDtypeStruct((2, rows, hb), f32),
+            jax.ShapeDtypeStruct(vec.shape, f32),
+        ],
+        scratch_shapes=shapes + [
+            V((14,) + vec.shape, f32),
+            pltpu.SemaphoreType.DMA((2, SLOTS)), pltpu.SemaphoreType.DMA((2, SLOTS)),
+            pltpu.SemaphoreType.DMA((2, 16)),
+            pltpu.SemaphoreType.DMA((6,)), pltpu.SemaphoreType.DMA((6,)),
+        ],
+        compiler_params=pltpu.CompilerParams(
+            collective_id=1, has_side_effects=True, vmem_limit_bytes=56 << 20
+        ),
+        name="reduce_grads",
+    )(gatt, gff, vec)
+
+
+def on_links():
+    return (lax.axis_size("dp"), lax.axis_size("mp")) == (8, 4)
+
+
 def gather_weights(att_t, ff):
+    if on_links():
+        return gather_weights_links(att_t, ff)
     watt = lax.all_gather(att_t, ("dp", "mp"), axis=0, tiled=True)
     wff = lax.all_gather(ff, "dp", axis=1, tiled=True)
     wff = lax.all_gather(wff, "mp", axis=0, tiled=False)
     return watt, wff
 
 
-def reduce_grads(gatt, gff):
+def reduce_grads(gatt, gff, vec):
+    if on_links():
+        return reduce_grads_links(gatt, gff, vec)
     gatt = lax.psum_scatter(gatt, ("dp", "mp"), scatter_dimension=0, tiled=True)
     gff = lax.psum_scatter(gff, "mp", scatter_dimension=0, tiled=False)
     gff = lax.psum_scatter(gff, "dp", scatter_dimension=1, tiled=True)
-    return gatt.astype(f32), gff.astype(f32)
+    return gatt.astype(f32), gff.astype(f32), lax.psum(vec, ("dp", "mp"))
 
 
 def per_device(
@@ -326,17 +662,12 @@
     nmp = lax.axis_size("mp")
     hb = feedforward_weights.shape[2]
     ff = nmp * hb
-    fill = lambda n: jnp.full((images, n), -1, jnp.int32)
     idx = jnp.concatenate(
-        [
-            kept_index[:, :KG], fill(GP - KG),
-            kept_index[:, KG : 2 * KG], fill(GP - KG),
-            kept_index[:, 2 * KG :], fill(LP - LOC),
-        ],
-        axis=1,
+        [kept_index, jnp.full((images, RI - KEPT), -1, jnp.int32)], axis=1
     )
     idx_col, idx_row = idx[:, :, None], idx[:, None, :]
-    mg, ml = masks()
+    mask = masks()
+    mask_specs = [full(m.shape) for m in mask]
 
     watt, wff = gather_weights(
         attention_weights.T.astype(bf16), feedforward_weights.astype(bf16)
@@ -357,7 +688,7 @@
         grid=(images,),
         in_specs=[
             per_image(RI, d), per_image(RI, d), full(watt.shape), full(vec.shape),
-            full(mg.shape), full(ml.shape),
+            *mask_specs,
         ],
         out_specs=[per_image(RI, 3 * d), per_image(RI, d), per_image(RI, d), per_image(RI, d)],
         out_shape=[
@@ -366,7 +697,7 @@
         ],
         compiler_params=params(),
         name="attention_forward",
-    )(normed, kept, watt, vec, mg, ml)
+    )(normed, kept, watt, vec, *mask)
 
     bias = vec[9:].reshape(nmp, 1, hb)
     whole = lambda *s: pl.BlockSpec(s, lambda j: (0,) * len(s), pipeline_mode=pl.Buffered(1))
@@ -398,17 +729,17 @@
         in_specs=[
             per_image(RI, d), per_image(RI, d), per_image(RI, d), per_image(RI, d),
             per_image(RI, d), per_image(RI, 3 * d), per_image(RI, d),
-            full(watt.shape), full(vec.shape), full(mg.shape), full(ml.shape),
+            full(watt.shape), full(vec.shape), *mask_specs,
         ],
         out_specs=[per_image(RI, 4 * d), per_image(RI, d), per_image(RI, 1), full((8, d))],
         out_shape=[
             sds(images, RI, 4 * d, bf16), sds(images, RI, d, f32), sds(images, RI, 1, f32),
             sds(8, d, f32),
         ],
-        scratch_shapes=[pltpu.VMEM((16, 128), f32), pltpu.VMEM((RI, d), bf16)],
+        scratch_shapes=[pltpu.VMEM((RI, d), bf16)],
         compiler_params=params(),
         name="attention_backward",
-    )(n2g, cotk, branch, kept, normed, proj, mixed, watt, vec, mg, ml)
+    )(n2g, cotk, branch, kept, normed, proj, mixed, watt, vec, *mask)
 
     gatt = pl.pallas_call(
         grad_kernel,
@@ -449,10 +780,9 @@
         name="block_output",
     )(out_acc, branch, kept, normed, tokens, idx_row, vec)
 
-    gatt, feedforward_gradient = reduce_grads(gatt, gff)
+    vector_local = jnp.concatenate([vecg_in[:2], vecg[:7], bg.reshape(ff // d, d)], axis=0)
+    gatt, feedforward_gradient, vector_gradient = reduce_grads(gatt, gff, vector_local)
     attention_gradient = gatt.T
-    vector_local = jnp.concatenate([vecg_in[:2], vecg[:7], bg.reshape(ff // d, d)], axis=0)
-    vector_gradient = lax.psum(vector_local, ("dp", "mp"))
     attention_new = adamw(
         attention_gradient, attention_first, attention_second,
         attention_weights, attention_average, 0.02, 0.05,

time: 653 us -> 379 us (0.58)
  waiting for transfers between devices: 397 us -> 0 us
  Pallas kernels: 161 us -> 340 us
  blocking collectives: 42.5 us -> 0 us
  between operations: 14.3 us -> 0.82 us
    all_gather x3 -> x0, waiting for transfers between devices: 219 us -> none  [the longest x1 136 us: gather_weights(): wff = lax.all_gather(wff, 'mp', axis=0, tiled=False)]
    pallas_call x0 -> x2, Pallas kernels: none -> 189 us  [the longest x1 117 us: reduce_grads_links(): pl.pallas_call(scatter_links_kernel, in_specs=[ANY, ANY, vm], out_specs=[...]
    reduce_scatter x3 -> x0, waiting for transfers between devices: 178 us -> none  [the longest x1 113 us: reduce_grads(): gff = lax.psum_scatter(gff, 'mp', scatter_dimension=0, tiled=False)]
    psum x1 -> x0, blocking collectives: 42.5 us -> none  [per_device(): vector_gradient = lax.psum(vector_local, ('dp', 'mp'))]
    unnamed x45 -> x52, local copies, waits for them, and re-layouts: 21.9 us -> 20.2 us
  transfers between devices with their start and end apart: 6 -> 0, of which waited for: 6 -> 0; matrix products, arithmetic and copies ran while one was open for 5% -> 0% of each run, Pallas kernels for 18% -> 0%
where the time goes in v2:
time: 379 us; the launch traced here: 378 us
  Pallas kernels  340 us (90%)
  local copies, waits for them, and re-layouts  26.1 us (7%)
  other arithmetic  10.7 us (3%)
    pallas_call x1, Pallas kernels, reduce_grads_links(): pl.pallas_call(scatter_links_kernel, in_specs=[ANY, ANY, vm], out_specs=[...  117 us
    pallas_call x1, Pallas kernels, gather_weights_links(): pl.pallas_call(gather_links_kernel, in_specs=[ANY, ANY], out_specs=[ANY,...  72.6 us
    pallas_call x1, Pallas kernels, per_device(): pl.pallas_call(feed_kernel, grid=(nmp,), in_specs=[whole(images, RI, d),...  43.2 us
    pallas_call x1, Pallas kernels, per_device(): pl.pallas_call(backward_kernel, grid=(images,), in_specs=[per_image(RI, d...  33.9 us
    pallas_call x1, Pallas kernels, per_device(): pl.pallas_call(forward_kernel, grid=(images,), in_specs=[per_image(RI, d)...  28.7 us
    unnamed x52, local copies, waits for them, and re-layouts  20.2 us
    pallas_call x1, Pallas kernels, per_device(): pl.pallas_call(input_kernel, grid=(images,), in_specs=[per_image(RI, 4 *...  17.6 us
    pallas_call x1, Pallas kernels, per_device(): pl.pallas_call(grad_kernel, grid=(4,), in_specs=[pl.BlockSpec((images, RI...  11.4 us

profile of v2, /device:TPU:0, one launch (start us, length us, event | category | flops | bytes accessed | tf_op | source)
XLA Modules:
  0.0 378.0 jit_solution(10382698056211112975)
XLA Ops:
  0.7 0.7 slice.12
  1.4 0.6 reshape.46.bias_ref
  2.0 0.7 fusion.8
  2.7 0.6 broadcast_in_dim.7.idx_ref
  3.3 1.6 convert_bitcast_fusion.att_ref
  4.9 1.8 convert_element_type.16.ff_ref
  6.8 1.1 copy.43.idx_ref
  7.8 4.3 %copy.41.tok_ref = bf16[4,542,768]{2,1,0:T(8,128)(2,1)} copy(bf16[4,542,768]{2,0,1:T(4,128)(2,1)} %param.21) | data formatting | bytes 6660096 | tf_op args[0]
  12.1 0.0 copy-done.2
  12.1 2.2 copy.42.cot_ref
  14.3 7.5 %gather_norm.1 = (bf16[4,272,768]{2,1,0:T(8,128)(2,1)}, bf16[4,272,768]{2,1,0:T(8,128)(2,1)}, bf16[4,272,768]{2,1,0:T(8,128)(2,1)}) custom-call(bf16[4,542,768]{2,1,0:T(8,128)(2,1)} %copy.41.tok_ref, bf16[4,542,768]{2,1,0:T(8,128)(2,1)} %copy.42.cot_ref, s32[4,272,1]{2,1,0:T(8,128)} %copy.43.idx_ref, f32[13,768]{1,0:T(8,128)} %vec_ref.9), custom_call_target="tpu_custom_call" | custom-call | tf_op jit(solution)/shard_map/gather_norm/pallas_call | solution.py:676
  21.8 72.6 %gather_weights.1 = (bf16[3072,768]{1,0:T(8,128)(2,1)}, bf16[4,2,768,768]{3,2,1,0:T(8,128)(2,1)}) custom-call(bf16[96,768]{1,0:T(8,128)(2,1)} %convert_bitcast_fusion.att_ref, bf16[2,96,768]{2,1,0:T(8,128)(2,1)} %convert_element_type.16.ff_ref), custom_call_target="tpu_custom_call" | custom-call | tf_op jit(solution)/shard_map/gather_weights/pallas_call | solution.py:438
  94.5 28.7 %attention_forward.1 = (bf16[4,272,2304]{2,1,0:T(8,128)(2,1)}, bf16[4,272,768]{2,1,0:T(8,128)(2,1)}, f32[4,272,768]{2,1,0:T(8,128)}, bf16[4,272,768]{2,1,0:T(8,128)(2,1)}) custom-call(bf16[4,272,768]{2,1,0:T(8,128)(2,1)} %get-tuple-element.42.normed_ref, bf16[4,272,768]{2,1,0:T(8,128)(2,1)} %get-tuple-element.43.kept_ref, ...), custom_call_target="tpu_custom_call" | custom-call | tf_op jit(solution)/shard_map/attention_forward/pallas_call | solution.py:686
  123.1 43.2 %feedforward.1 = (f32[4,272,768]{2,1,0:T(8,128)}, f32[4,272,768]{2,1,0:T(8,128)}, bf16[4,2,768,768]{3,2,1,0:T(8,128)(2,1)}, f32[4,1,768]{2,1,0:T(1,128)}) custom-call(bf16[4,272,768]{2,1,0:T(8,128)(2,1)} %get-tuple-element.45.n2_ref, bf16[4,272,768]{2,1,0:T(8,128)(2,1)} %get-tuple-element.46.cot_ref.cotk_ref, ...), custom_call_target="tpu_custom_call" | custom-call | tf_op jit(solution)/shard_map/feedforward/pallas_call | solution.py:704
  166.3 8.8 %block_output.1 = bf16[4,542,768]{2,1,0:T(8,128)(2,1)} custom-call(f32[4,272,768]{2,1,0:T(8,128)} %get-tuple-element.48.out_ref, f32[4,272,768]{2,1,0:T(8,128)} %get-tuple-element.49.branch_ref, bf16[4,272,768]{2,1,0:T(8,128)(2,1)} %get-tuple-element.43.kept_ref, bf16[4,272,768]{2,1,0:T(8,128)(2,1)} %get-tuple-element.42.normed_ref, ...), custom_call_target="tpu_custom_call" | custom-call | tf_op jit(solution)/shard_map/block_output/pallas_call | solution.py:770
  175.1 33.9 %attention_backward.1 = (bf16[4,272,3072]{2,1,0:T(8,128)(2,1)}, f32[4,272,768]{2,1,0:T(8,128)}, f32[4,272,1]{2,1,0:T(8,128)}, f32[8,768]{1,0:T(8,128)}) custom-call(f32[4,272,768]{2,1,0:T(8,128)} %get-tuple-element.50.n2g_ref, bf16[4,272,768]{2,1,0:T(8,128)(2,1)} %get-tuple-element.46.cot_ref.cotk_ref, f32[4,272,768]{2,1,0:T(8,128)} %get-tuple-element.49.branch_ref, ...), custom_call_target="tpu_custom_call" | custom-call | tf_op jit(solution)/shard_map/attention_backward/pallas_call | solution.py:726
  208.9 0.0 copy-done
  208.9 4.3 %copy.46 = bf16[4,542,768]{2,0,1:T(4,128)(2,1)} copy(bf16[4,542,768]{2,1,0:T(8,128)(2,1)S(1)} %copy-done) | data formatting | bytes 6660096
  213.2 17.6 %input_grad.1 = (f32[4,542,768]{2,1,0:T(8,128)}, f32[8,768]{1,0:T(8,128)}) custom-call(bf16[4,272,3072]{2,1,0:T(8,128)(2,1)} %get-tuple-element.53.dp_ref, f32[4,272,1]{2,1,0:T(8,128)} %get-tuple-element.54.rg_ref, f32[4,272,768]{2,1,0:T(8,128)} %get-tuple-element.55.resg_ref, bf16[4,272,768]{2,1,0:T(8,128)(2,1)} %get-tuple-element.43.kept_ref, ...), custom_call_target="tpu_custom_call" | custom-call | tf_op jit(solution)/shard_map/input_grad/pallas_call | solution.py:757
  230.9 11.4 %attention_grads.1.gatt_ref = bf16[3072,768]{1,0:T(8,128)(2,1)} custom-call(bf16[4,272,3072]{2,1,0:T(8,128)(2,1)} %get-tuple-element.53.dp_ref, bf16[4,272,768]{2,1,0:T(8,128)(2,1)} %get-tuple-element.42.normed_ref, bf16[4,272,768]{2,1,0:T(8,128)(2,1)} %get-tuple-element.52.mixed_ref), custom_call_target="tpu_custom_call" | custom-call | tf_op jit(solution)/shard_map/attention_grads/pallas_call | solution.py:744
  242.3 0.0 copy-done.1
  242.3 7.1 %copy.47 = f32[4,542,768]{2,0,1:T(4,128)} copy(f32[4,542,768]{2,1,0:T(8,128)S(1)} %copy-done.1) | data formatting | bytes 13320192
  249.4 0.7 slice.13
  250.1 0.6 pad_maximum_fusion.vec_ref
  250.8 0.0 copy-start.8
  250.8 0.0 copy-start.13
  250.8 0.0 copy-start.14
  250.8 0.0 copy-start.15
  250.8 116.8 %reduce_grads.1 = (f32[96,768]{1,0:T(8,128)}, f32[2,96,768]{2,1,0:T(8,128)}, f32[13,768]{1,0:T(8,128)}) custom-call(bf16[3072,768]{1,0:T(8,128)(2,1)} %attention_grads.1.gatt_ref, bf16[4,2,768,768]{3,2,1,0:T(8,128)(2,1)} %get-tuple-element.57.gff_ref, f32[13,768]{1,0:T(8,128)} %pad_maximum_fusion.vec_ref), custom_call_target="tpu_custom_call" | custom-call | tf_op jit(solution)/shard_map/reduce_grads/pallas_call | solution.py:611
  367.6 0.0 copy-start.4
  367.6 0.0 copy-start.10
  367.6 0.0 copy-start.11
  367.7 1.5 slice_reduce_fusion
  369.2 0.0 copy-done.17
  369.2 1.5 multiply_add_fusion.5
  370.7 0.0 copy-done.14
  370.7 0.0 copy-start.12
  370.7 2.0 fusion.6
  372.7 0.8 multiply_add_fusion.3
  373.4 0.0 copy-done.4
  373.5 0.0 copy-done.10
  373.5 1.4 fusion.4
  374.9 1.0 multiply_add_fusion.1
  375.9 0.0 copy-done.9
  375.9 0.7 copy.54
  376.6 0.8 copy.55
  377.4 0.6 copy.56
  378.0 0.0 copy-done.3
  (28 shorter events, 0.1 us)
Async XLA Ops:
  7.8 4.3 %copy-start.2 = (bf16[4,542,768]{2,0,1:T(4,128)(2,1)S(1)}, bf16[4,542,768]{2,0,1:T(4,128)(2,1)}, u32[]{:S(2)}) copy-start(bf16[4,542,768]{2,0,1:T(4,128)(2,1)} %param.22) | copy-start | bytes 9990148
  175.1 33.9 %copy-start = (bf16[4,542,768]{2,1,0:T(8,128)(2,1)S(1)}, bf16[4,542,768]{2,1,0:T(8,128)(2,1)}, u32[]{:S(2)}) copy-start(bf16[4,542,768]{2,1,0:T(8,128)(2,1)} %block_output.1) | copy-start | bytes 9990148
  230.9 11.4 %copy-start.1 = (f32[4,542,768]{2,1,0:T(8,128)S(1)}, f32[4,542,768]{2,1,0:T(8,128)}, u32[]{:S(2)}) copy-start(f32[4,542,768]{2,1,0:T(8,128)} %get-tuple-element.65) | copy-start | bytes 19980292
  242.3 7.9 %copy-start.21 = (f32[4,1,768]{2,1,0:T(1,128)S(1)}, f32[4,1,768]{2,1,0:T(1,128)}, u32[]{:S(2)}) copy-start(f32[4,1,768]{2,1,0:T(1,128)} %get-tuple-element.60) | copy-start | bytes 36868
  242.3 7.9 %copy-start.20 = (f32[8,768]{1,0:T(8,128)S(1)}, f32[8,768]{1,0:T(8,128)}, u32[]{:S(2)}) copy-start(f32[8,768]{1,0:T(8,128)} %get-tuple-element.59) | copy-start | bytes 73732
  250.8 118.4 %copy-start.6 = (f32[13,768]{1,0:T(8,128)S(1)}, f32[13,768]{1,0:T(8,128)}, u32[]{:S(2)}) copy-start(f32[13,768]{1,0:T(8,128)} %vec_ref.9) | copy-start | bytes 119812
  250.8 118.4 %copy-start.17 = (f32[13,768]{1,0:T(8,128)S(1)}, f32[13,768]{1,0:T(8,128)}, u32[]{:S(2)}) copy-start(f32[13,768]{1,0:T(8,128)} %param.35) | copy-start | bytes 119812
  250.8 118.4 %copy-start.18 = (f32[13,768]{1,0:T(8,128)S(1)}, f32[13,768]{1,0:T(8,128)}, u32[]{:S(2)}) copy-start(f32[13,768]{1,0:T(8,128)} %param.34) | copy-start | bytes 119812
  250.8 118.4 %copy-start.19 = (f32[13,768]{1,0:T(8,128)S(1)}, f32[13,768]{1,0:T(8,128)}, u32[]{:S(2)}) copy-start(f32[13,768]{1,0:T(8,128)} %param.33) | copy-start | bytes 119812
  250.8 119.9 %copy-start.8 = (f32[768,96]{0,1:T(8,128)S(1)}, f32[768,96]{0,1:T(8,128)}, u32[]{:S(2)}) copy-start(f32[768,96]{0,1:T(8,128)} %param.24) | copy-start | bytes 884740
  250.8 119.8 %copy-start.13 = (f32[768,96]{0,1:T(8,128)S(1)}, f32[768,96]{0,1:T(8,128)}, u32[]{:S(2)}) copy-start(f32[768,96]{0,1:T(8,128)} %param.26) | copy-start | bytes 884740
  250.8 119.8 %copy-start.14 = (f32[768,96]{0,1:T(8,128)S(1)}, f32[768,96]{0,1:T(8,128)}, u32[]{:S(2)}) copy-start(f32[768,96]{0,1:T(8,128)} %param.25) | copy-start | bytes 884740
  250.8 121.8 %copy-start.15 = (f32[768,96]{0,1:T(8,128)S(1)}, f32[768,96]{0,1:T(8,128)}, u32[]{:S(2)}) copy-start(f32[768,96]{0,1:T(8,128)} %param.27) | copy-start | bytes 884740
  367.6 5.8 %copy-start.4 = (f32[2,96,768]{2,1,0:T(8,128)S(1)}, f32[2,96,768]{2,1,0:T(8,128)}, u32[]{:S(2)}) copy-start(f32[2,96,768]{2,1,0:T(8,128)} %param.28) | copy-start | bytes 1769476
  367.6 5.8 %copy-start.5 = (f32[2,96,768]{2,1,0:T(8,128)S(1)}, f32[2,96,768]{2,1,0:T(8,128)}, u32[]{:S(2)}) copy-start(f32[2,96,768]{2,1,0:T(8,128)} %get-tuple-element.126) | copy-start | bytes 1769476
  367.6 5.8 %copy-start.10 = (f32[2,96,768]{2,1,0:T(8,128)S(1)}, f32[2,96,768]{2,1,0:T(8,128)}, u32[]{:S(2)}) copy-start(f32[2,96,768]{2,1,0:T(8,128)} %param.30) | copy-start | bytes 1769476
  367.6 5.8 %copy-start.11 = (f32[2,96,768]{2,1,0:T(8,128)S(1)}, f32[2,96,768]{2,1,0:T(8,128)}, u32[]{:S(2)}) copy-start(f32[2,96,768]{2,1,0:T(8,128)} %param.29) | copy-start | bytes 1769476
  370.7 4.2 %copy-start.12 = (f32[2,96,768]{2,1,0:T(8,128)S(1)}, f32[2,96,768]{2,1,0:T(8,128)}, u32[]{:S(2)}) copy-start(f32[2,96,768]{2,1,0:T(8,128)} %param.31) | copy-start | bytes 1769476
  372.7 3.2 copy-start.7
  372.7 3.2 copy-start.9
  373.5 3.9 %copy-start.16 = (f32[13,768]{1,0:T(8,128)S(1)}, f32[13,768]{1,0:T(8,128)}, u32[]{:S(2)}) copy-start(f32[13,768]{1,0:T(8,128)} %get-tuple-element.132) | copy-start | bytes 119812
  374.9 3.2 copy-start.3

commit v3 on v1

v3 whole, which is shorter than its diff:
```python
import functools

import jax
import jax.numpy as jnp
import numpy as np
from jax import lax
from jax.experimental import pallas as pl
from jax.experimental.pallas import tpu as pltpu
from jax.sharding import PartitionSpec as P

H = 12
HD = 64
LG = 197
LL = 37
KG = LG // 2
KL = LL // 2
LOC = 4 * KL
KEPT = 2 * KG + LOC
RI = -(-KEPT // 16) * 16
SPANS = ((0, KG), (KG, 2 * KG), (2 * KG, KEPT))
UNITS = tuple((a // 16 * 16, -(-b // 16) * 16) for a, b in SPANS)
PAIRS = H // 2
W2L = 2 * HD

bf16 = jnp.bfloat16
f32 = jnp.float32


def params(limit=56, **kw):
    return pltpu.CompilerParams(vmem_limit_bytes=limit << 20, **kw)


def full(shape):
    return pl.BlockSpec(shape, lambda *_: (0,) * len(shape))


def per_image(*shape):
    return pl.BlockSpec((1,) + shape, lambda i, *_: (i,) + (0,) * len(shape))


def nn(a, b):
    return lax.dot_general(a, b, (((1,), (0,)), ((), ())), preferred_element_type=f32)


def nt(a, b):
    return lax.dot_general(a, b, (((1,), (1,)), ((), ())), preferred_element_type=f32)


def tn(a, b):
    return lax.dot_general(a, b, (((0,), (0,)), ((), ())), preferred_element_type=f32)


def normalize(rows):
    center = rows - jnp.mean(rows, axis=-1, keepdims=True)
    spread = jnp.mean(center * center, axis=-1, keepdims=True)
    inverse = lax.rsqrt(spread + 1e-06)
    return center * inverse, inverse


def norm_backward(upstream, standard, inverse, gain):
    scaled = upstream * gain
    return inverse * (
        scaled
        - jnp.mean(scaled, axis=-1, keepdims=True)
        - standard * jnp.mean(scaled * standard, axis=-1, keepdims=True)
    )


def colsum(v):
    return jnp.sum(v, axis=0, keepdims=True)


def masks():
    crop = np.full(RI, -1)
    crop[:KG], crop[KG : 2 * KG] = 0, 1
    for c in range(4):
        crop[2 * KG + c * KL : 2 * KG + (c + 1) * KL] = 2 + c
    adds, valids = [], []
    for (a, b), (lo, hi) in zip(SPANS, UNITS):
        rows = np.arange(lo, hi)
        inside = (rows >= a) & (rows < b)
        same = (crop[lo:hi, None] == crop[None, lo:hi]) & inside[:, None] & inside[None, :]
        adds.append(np.tile(np.where(same, 0.0, -1e9), (1, 2)).astype(np.float32))
        valids.append(np.tile(inside[None, :].astype(np.float32), (8, 2)))
    return [jnp.asarray(m) for m in adds + valids]


def lane_half(shape):
    return lax.broadcasted_iota(jnp.int32, shape, len(shape) - 1) < HD


def split_heads(v, scale):
    first = lane_half(v.shape)
    zero = jnp.zeros_like(v)
    if scale != 1.0:
        v = v * jnp.asarray(scale, v.dtype)
    return jnp.concatenate([jnp.where(first, v, zero), jnp.where(first, zero, v)], axis=0)


def join_heads(v):
    n = v.shape[0] // 2
    return jnp.where(lane_half((n, v.shape[1])), v[:n], v[n:])


def softmax_keys(st, valid):
    p = jnp.exp(st - jnp.max(st, axis=0, keepdims=True))
    return p * (valid / jnp.sum(p, axis=0, keepdims=True))


def store_window(ref, image, lo, hi, last, cols, value, tail):
    value = value.astype(bf16)
    if tail is not None:
        value = jnp.concatenate([value[:16] + tail, value[16:]], axis=0)
    end = hi if last else hi - 16
    ref[image, lo:end, cols] = value[: end - lo]
    return None if last else value[end - lo :]


MESH = pl.DeviceIdType.MESH
ANY = pl.BlockSpec(memory_space=pl.ANY)
MP = 4
CROPS = ((0, LG), (LG, 2 * LG), (2 * LG, 2 * LG + 4 * LL))
ORDER = ((0, 1, 2, 3), (1, 0, 1, 2), (2, 2, 3, 1), (3, 3, 0, 0))


def flip(index, bit):
    return index + bit * (1 - 2 * lax.rem(lax.div(index, bit), 2))


def remote(src, dst, send, recv, to):
    return pltpu.make_async_remote_copy(
        src_ref=src, dst_ref=dst, send_sem=send, recv_sem=recv, device_id=to, device_id_type=MESH
    )


class Sends:
    def __init__(self):
        self.made = []

    def start(self, make, when=None):
        def go():
            make().start()

        go() if when is None else pl.when(when)(go)
        self.made.append((make, when))

    def finish(self):
        for make, when in self.made:
            def wait(make=make):
                make().wait_send()

            wait() if when is None else pl.when(when)(wait)


class Place:
    def __init__(self):
        self.dp = lax.axis_index("dp")
        self.z = lax.axis_index("mp")
        x, y = flip(self.dp, 2), flip(self.dp, 4)
        self.core = (flip(self.dp, 1), self.z)
        self.x, self.y = (x, self.z), (y, self.z)
        self.chips = (self.dp, x, y, flip(x, 4))
        self.mates = tuple(flip(c, 1) for c in self.chips)
        power = (1 + 3 * lax.rem(self.z, 2)) * (1 + 15 * lax.div(self.z, 2))
        self.event = []
        for row in ORDER:
            code = sum(v << (2 * i) for i, v in enumerate(row))
            self.event.append(lax.rem(lax.div(0 * power + code, power), 4))
        self.low, self.high = self.z > 0, self.z < MP - 1
        self.middle = self.low & self.high
        self.line = [lax.rem(self.z + k, MP) for k in range(MP)]
        self.up, self.down = (self.dp, self.z + 1), (self.dp, self.z - 1)
        self.onward = (self.up, self.down, (self.dp, 3 * (self.z - 1)))

    def barrier(self):
        sem = pltpu.get_barrier_semaphore()
        others = [self.core, self.x, self.y]
        others += [(self.dp, k) for k in self.line[1:]]
        for other in others:
            pl.semaphore_signal(sem, inc=1, device_id=other, device_id_type=MESH)
        pl.semaphore_wait(sem, len(others))


def att_block(ref, dp, z, rows):
    return ref.at[pl.ds(pl.multiple_of((dp * MP + z) * rows, 32), rows), :]


def ff_block(ref, dp, z, rows):
    return ref.at[z, :, pl.ds(pl.multiple_of(dp * rows, 32), rows), :]


class Gather:
    ALONG, X, Y, D, C, SLOTS = 0, 4, 8, 12, 16, 32

    def __init__(self, at, tensors, send, recv, local, rows):
        self.at, self.tensors, self.rows = at, tensors, rows
        self.send, self.recv, self.local = send, recv, local
        self.sends = Sends()

    def copy(self, t, base, e, dp, to, own=False):
        mine, out, block = self.tensors[t]
        zb = self.at.event[e]
        dst = block(out, dp, zb, self.rows)
        sems = self.send.at[t, base + zb], self.recv.at[t, base + zb]
        return remote(mine if own else dst, dst, *sems, to)

    def put(self, t, base, e, r, to, own=False, when=None):
        self.sends.start(lambda: self.copy(t, base, e, self.at.chips[r], to, own), when)

    def got(self, t, base, e, dp):
        self.copy(t, base, e, dp, self.at.core).wait_recv()

    def keep(self, t):
        mine, out, block = self.tensors[t]
        return pltpu.make_async_copy(
            mine, block(out, self.at.dp, self.at.z, self.rows), self.local.at[t]
        )

    def spread(self, t, e):
        own = e == 0
        self.put(t, self.X, e, 0, self.at.x, own)
        self.put(t, self.Y, e, 0, self.at.y, own)
        self.put(t, self.C, e, 0, self.at.core, own)

    def begin(self, t):
        at = self.at
        self.keep(t).start()
        self.put(t, self.ALONG, 0, 0, at.up, True, at.high)
        self.put(t, self.ALONG, 0, 0, at.down, True, at.low)
        self.spread(t, 0)

    def along(self, t, e):
        at = self.at
        self.got(t, self.ALONG, e, at.dp)
        self.put(t, self.ALONG, e, 0, at.onward[e - 1], False, at.middle)
        self.spread(t, e)

    def plane(self, t, e):
        at = self.at
        self.got(t, self.X, e, at.chips[1])
        if e % 2 == 0:
            self.put(t, self.D, e, 1, at.y)
        self.put(t, self.C + 4, e, 1, at.core)
        self.got(t, self.Y, e, at.chips[2])
        if e % 2 == 1:
            self.put(t, self.D, e, 2, at.x)
        self.put(t, self.C + 8, e, 2, at.core)

    def corner(self, t, e):
        self.got(t, self.D, e, self.at.chips[3])
        self.put(t, self.C + 12, e, 3, self.at.core)

    def actions(self, t):
        do = lambda f, e: lambda: f(t, e)
        order = [
            (self.along, 1), (self.plane, 0), (self.along, 2), (self.plane, 1), (self.along, 3),
            (self.plane, 2), (self.plane, 3),
        ]
        return [do(f, e) for f, e in order] + [do(self.corner, e) for e in range(4)]

    def finish(self, t):
        for r in range(4):
            for e in range(4):
                self.got(t, self.C + 4 * r, e, self.at.mates[r])
        self.keep(t).wait()


def add_into(target, first, *others):
    step = 32

    @pl.loop(0, first.shape[0] // step)
    def _(i):
        s = pl.ds(pl.multiple_of(i * step, step), step)
        total = first[s, :].astype(f32)
        for ref in others:
            total = total + ref[s, :].astype(f32)
        target[s, :] = total.astype(target.dtype)


class Reduce:
    C, D, X, Y, ALONG, SLOTS = 0, 16, 20, 24, 28, 32

    def __init__(self, at, source, own, parts, bufs, send, recv, load=None):
        self.at, self.source, self.own, self.parts = at, source, own, parts
        self.c, self.d, self.x, self.y, self.line = bufs
        self.send, self.recv, self.load = send, recv, load
        self.sends = Sends()

    def put(self, slot, src, dst, to):
        self.sends.start(
            lambda: remote(src(), dst(), self.send.at[slot], self.recv.at[slot], to)
        )

    def got(self, slot, dst):
        remote(dst, dst, self.send.at[slot], self.recv.at[slot], self.at.core).wait_recv()

    def cross(self, e, r):
        i = 4 * e + r
        self.put(self.C + i, lambda: self.source(e, self.at.mates[r]), lambda: self.c.at[i], self.at.core)
        if self.load is not None:
            self.load(e, r).start()

    def add(self, e, r, *others, target=None):
        i = 4 * e + r
        self.got(self.C + i, self.c.at[i])
        if self.load is not None:
            self.load(e, r).wait()
        refs = [self.own(e, r), self.c.at[i]] + list(others)
        target = refs[0] if target is None else target
        for t, *rest in zip(self.parts(target), *[self.parts(ref) for ref in refs]):
            add_into(t, *rest)

    def corner(self, e):
        at = self.at
        self.add(e, 3)
        to = at.y if e % 2 else at.x
        self.put(self.D + e, lambda: self.own(e, 3), lambda: self.d.at[e], to)
        r, base, buf, to = (2, self.Y, self.y, at.y) if e % 2 else (1, self.X, self.x, at.x)
        self.add(e, r)
        self.put(base + e, lambda: self.own(e, r), lambda: buf.at[e], to)

    def plane(self, e):
        at = self.at
        r, base, buf, to = (1, self.X, self.x, at.x) if e % 2 else (2, self.Y, self.y, at.y)
        self.got(self.D + e, self.d.at[e])
        self.add(e, r, self.d.at[e])
        self.put(base + e, lambda: self.own(e, r), lambda: buf.at[e], to)

    def along(self, e, out=None):
        at = self.at
        self.got(self.X + e, self.x.at[e])
        self.got(self.Y + e, self.y.at[e])
        if e:
            self.add(e, 0, self.x.at[e], self.y.at[e])
            zb = at.event[e]
            self.sends.start(
                lambda: remote(
                    self.own(e, 0), self.line.at[at.z], self.send.at[self.ALONG + zb],
                    self.recv.at[self.ALONG + at.z], (at.dp, zb),
                )
            )
        else:
            lines = []
            for k in range(1, MP):
                zb = at.line[k]
                dst = self.line.at[zb]
                self.got(self.ALONG + zb, dst)
                lines.append(dst)
            self.add(0, 0, self.x.at[0], self.y.at[0], *lines, target=out)


def pump(schedule, step, point):
    for (s, p), action in schedule:
        if p == point:
            pl.when(step == s)(action)


def forward_kernel(
    links, tok_ref, cot_ref, idx_ref, vec_ref, m0_ref, m1_ref, m2_ref, v0_ref, v1_ref, v2_ref,
    att_ref, ff_ref,
    kept_ref, normed_ref, cotk_ref, proj_ref, mixed_ref, branch_ref, resid_ref, n2_ref,
    watt_out, *rest,
):
    if links:
        wff_ref, watt_ref, tok_s, cot_s, load, send, recv, local = rest
    else:
        watt_ref, tok_s, cot_s, load = rest
    step = pl.program_id(0)
    images, _, d = kept_ref.shape
    loads = [
        pltpu.make_async_copy(tok_ref, tok_s, load.at[0]),
        pltpu.make_async_copy(cot_ref, cot_s, load.at[1]),
    ]
    if links:
        at = Place()
        rows = att_ref.shape[0]
        tensors = ((att_ref, watt_ref, att_block), (ff_ref, wff_ref, ff_block))
        gather = Gather(at, tensors, send, recv, local, rows)
        store = pltpu.make_async_copy(watt_ref, watt_out, load.at[2])
        att, feed = gather.actions(0), gather.actions(1)
        spots = [(1, 1), (1, 1), (1, 4), (2, 2), (2, 3), (3, 1), (4, 2), (4, 4), (4, 4), (4, 4), (4, 4)]
        schedule = list(zip(spots, feed))
    else:
        att, schedule = [lambda: None] * 11, []
        fetch = pltpu.make_async_copy(att_ref, watt_ref, load.at[2])

    @pl.when(step == 0)
    def _():
        if links:
            at.barrier()
            gather.begin(0)
        else:
            fetch.start()
        for c in loads:
            c.start()
        offset = 0
        loads[0].wait()
        loads[1].wait()
        for crop, ((a, b), (lo, hi)) in enumerate(zip(CROPS, UNITS)):
            n, k = hi - lo, images * (b - a)
            index = idx_ref[offset : offset + images * n, :]
            offset += images * n
            hot = (lax.broadcasted_iota(jnp.int32, (images * n, k), 1) == index)
            hot = hot.astype(f32).astype(bf16)
            for src, dst in ((tok_s, kept_ref), (cot_s, cotk_ref)):
                got = nn(hot, src[a:b].reshape(k, d)).astype(bf16)
                for i in range(images):
                    part = got[i * n : (i + 1) * n]
                    if crop:
                        dst[i, lo : lo + 16] = dst[i, lo : lo + 16] + part[:16]
                        dst[i, lo + 16 : hi] = part[16:]
                    else:
                        dst[i, lo:hi] = part
            att[crop]()
        for i in range(images):
            standard, _ = normalize(kept_ref[i].astype(f32))
            normed_ref[i] = (standard * vec_ref[0:1] + vec_ref[1:2]).astype(bf16)
            if i == 1:
                att[3]()
        for action in att[4:6]:
            action()
        if links:
            gather.begin(1)
        for action in att[6:]:
            action()
        if links:
            gather.finish(0)
            store.start()
        else:
            fetch.wait()
            done = pltpu.make_async_copy(watt_ref, watt_out, load.at[2])
            done.start()
            done.wait()

    @pl.when(step > 0)
    def _():
        image = step - 1
        normed = normed_ref[image]
        for j, row in ((0, 3), (1, None), (2, 4)):
            part = nt(normed, watt_ref[j * d : (j + 1) * d, :])
            if row is not None:
                part = part + vec_ref[row : row + 1]
            proj_ref[0, :, j * d : (j + 1) * d] = part.astype(bf16)
        pump(schedule, step, 1)
        mrefs, vrefs = (m0_ref, m1_ref, m2_ref), (v0_ref, v1_ref, v2_ref)
        for pair in range(PAIRS):
            cols = lambda j: slice(j * d + pair * W2L, j * d + (pair + 1) * W2L)
            tail = None
            for unit, (lo, hi) in enumerate(UNITS):
                qs = split_heads(proj_ref[0, lo:hi, cols(0)], HD ** -0.5)
                st = nt(proj_ref[0, lo:hi, cols(1)], qs) + mrefs[unit][...]
                pt = softmax_keys(st, vrefs[unit][0:1]).astype(bf16)
                out = join_heads(tn(pt, proj_ref[0, lo:hi, cols(2)]))
                tail = store_window(mixed_ref, 0, lo, hi, unit == 2, cols(0), out, tail)
            if pair == 1:
                pump(schedule, step, 2)
            if pair == 3:
                pump(schedule, step, 3)
        branch = nt(mixed_ref[0], watt_ref[3 * d :, :]) + vec_ref[5:6]
        branch_ref[0] = branch
        residual = kept_ref[image].astype(f32) + router_score(normed, vec_ref) * branch
        resid_ref[0] = residual
        standard, _ = normalize(residual)
        n2_ref[0] = (standard * vec_ref[6:7] + vec_ref[7:8]).astype(bf16)
        pump(schedule, step, 4)

    if links:
        @pl.when(step == images)
        def _():
            gather.finish(1)
            gather.sends.finish()
            store.wait()


def router_score(normed, vec_ref):
    logit = jnp.sum(normed.astype(f32) * vec_ref[2:3], axis=-1, keepdims=True)
    return jax.nn.sigmoid(logit)


def feed_kernel(
    n2_ref, cot_ref, resid_ref, w_ref, bias_ref, vec_ref,
    result_ref, n2g_ref, gff_ref, bg_ref, out_s, act_s, ig_s,
):
    step = pl.program_id(0)
    images = n2_ref.shape[0]
    d, hb = w_ref.shape[2], w_ref.shape[3]
    bg_ref[0] = jnp.zeros((1, hb), f32)

    @pl.when(step == 0)
    def _():
        out_s[...] = resid_ref[...] + vec_ref[8:9]
        n2g_ref[...] = jnp.zeros_like(n2g_ref)

    @pl.loop(0, images)
    def _(i):
        inner = nn(n2_ref[i], w_ref[0, 0]) + bias_ref[0]
        ag = nn(cot_ref[i], w_ref[0, 1])
        phi = 0.5 * (1.0 + lax.erf(inner * 0.7071067811865476))
        act = (inner * phi).astype(bf16)
        slope = phi + inner * jnp.exp(-0.5 * inner * inner) * 0.3989422804014327
        ig = (ag * slope).astype(bf16)
        rows = pl.ds(pl.multiple_of(i * RI, 16), RI)
        act_s[rows, :] = act
        ig_s[rows, :] = ig
        bg_ref[0] += colsum(ig.astype(f32))
        out_s[i] += nt(act, w_ref[0, 1])
        n2g_ref[i] += nt(ig, w_ref[0, 0])

    n2 = n2_ref[...].reshape(images * RI, d)
    cot = cot_ref[...].reshape(images * RI, d)
    gff_ref[0, 0] = tn(n2, ig_s[...]).astype(bf16)
    gff_ref[0, 1] = tn(cot, act_s[...]).astype(bf16)

    @pl.when(step == pl.num_programs(0) - 1)
    def _():
        result_ref[...] = out_s[...].astype(bf16)


def backward_kernel(
    links, n2g_ref, cotk_ref, branch_ref, resid_ref, normed_ref, proj_ref, watt_ref,
    vec_ref, m0_ref, m1_ref, m2_ref, v0_ref, v1_ref, v2_ref, *rest,
):
    if links:
        gff_ref, dp_ref, resg_ref, rg_ref, vecg_ref, gout_ref = rest[:6]
        mg_s, a, c, dd, x, y, line, send, recv, local = rest[6:]
    else:
        dp_ref, resg_ref, rg_ref, vecg_ref, mg_s = rest
    step = pl.program_id(0)
    schedule = []
    if links:
        at = Place()
        rows = gout_ref.shape[1]
        load = lambda e, r: pltpu.make_async_copy(
            ff_block(gff_ref, at.chips[r], at.event[e], rows), a.at[4 * e + r], local.at[4 * e + r]
        )
        reduce = Reduce(
            at, lambda e, dp: ff_block(gff_ref, dp, at.event[e], rows), lambda e, r: a.at[4 * e + r],
            lambda ref: (ref.at[0], ref.at[1]), (c, dd, x, y, line), send, recv, load,
        )

        def cross(e):
            for r in (3, 1, 2, 0):
                reduce.cross(e, r)

        def start():
            at.barrier()
            for e in (3, 2, 1, 0):
                cross(e)

        do = lambda f, e: lambda: f(e)
        schedule = [
            ((0, 0), start),
            ((0, 1), do(reduce.corner, 3)),
            ((0, 3), do(reduce.corner, 2)),
            ((1, 1), do(reduce.plane, 3)),
            ((1, 2), do(reduce.corner, 1)),
            ((2, 0), do(reduce.plane, 2)),
            ((2, 1), do(reduce.along, 3)),
            ((2, 2), do(reduce.corner, 0)),
            ((3, 0), do(reduce.plane, 1)),
            ((3, 2), do(reduce.along, 2)),
        ]

    pump(schedule, step, 0)
    d = normed_ref.shape[2]
    normed = normed_ref[0]
    score = router_score(normed, vec_ref)
    branch = branch_ref[0]
    standard, inverse = normalize(resid_ref[0])
    n2g = n2g_ref[0]
    cot = cotk_ref[0].astype(f32)
    resg = cot + norm_backward(n2g, standard, inverse, vec_ref[6:7])
    resg_ref[0] = resg
    bg = (score * resg).astype(bf16)
    rg = jnp.sum(resg * branch, axis=-1, keepdims=True) * score * (1.0 - score)
    rg_ref[0] = rg
    dp_ref[0, :, 3 * d :] = bg
    mg_s[...] = nn(bg, watt_ref[3 * d :, :]).astype(bf16)
    pump(schedule, step, 1)
    mrefs, vrefs = (m0_ref, m1_ref, m2_ref), (v0_ref, v1_ref, v2_ref)
    for pair in range(PAIRS):
        cols = lambda j: slice(j * d + pair * W2L, j * d + (pair + 1) * W2L)
        tails = [None] * 3
        for unit, (lo, hi) in enumerate(UNITS):
            qs = split_heads(proj_ref[0, lo:hi, cols(0)], HD ** -0.5)
            kk = proj_ref[0, lo:hi, cols(1)]
            pt = softmax_keys(nt(kk, qs) + mrefs[unit][...], vrefs[unit][0:1])
            ds = split_heads(mg_s[lo:hi, cols(0)], 1.0)
            gpt = nt(proj_ref[0, lo:hi, cols(2)], ds)
            sg = (pt * (gpt - jnp.sum(pt * gpt, axis=0, keepdims=True))).astype(bf16)
            grads = (
                join_heads(tn(sg, kk)) * HD ** -0.5, nn(sg, qs), nn(pt.astype(bf16), ds)
            )
            for j in range(3):
                tails[j] = store_window(dp_ref, 0, lo, hi, unit == 2, cols(j), grads[j], tails[j])
        if pair == 1:
            pump(schedule, step, 2)
        if pair == 3:
            pump(schedule, step, 3)
    sums = jnp.concatenate(
        [
            colsum(rg * normed.astype(f32)),
            colsum(dp_ref[0, :, :d].astype(f32)),
            colsum(dp_ref[0, :, 2 * d : 3 * d].astype(f32)),
            colsum(bg.astype(f32)),
            colsum(n2g * standard),
            colsum(n2g),
            colsum(cot),
            jnp.zeros((1, d), f32),
        ],
        axis=0,
    )

    @pl.when(step == 0)
    def _():
        vecg_ref[...] = jnp.zeros_like(vecg_ref)

    vecg_ref[...] += sums
    if links:
        @pl.when(step == pl.num_programs(0) - 1)
        def _():
            reduce.plane(0)
            reduce.along(1)
            reduce.along(0, gout_ref)
            reduce.sends.finish()


def grads_kernel(
    links, dp_ref, normed_ref, mixed_ref, rg_ref, resg_ref, kept_ref, vec_ref, watt_ref, *rest,
):
    if links:
        vecb_ref, bias_ref, high_ref, low_ref, gout_ref, vecout_ref = rest[:6]
        watt_s, gatt_s, vecg_s, load, c, dd, x, y, line, send, recv, vbuf, vsend, vrecv = rest[6:]
    else:
        high_ref, low_ref, gatt_s, vecg_s, watt_s, load = rest
    step = pl.program_id(0)
    images, _, d = normed_ref.shape
    fetch = pltpu.make_async_copy(watt_ref.at[: 3 * d], watt_s, load.at[0])
    schedule = []
    turn = step
    if links:
        at = Place()
        rows = gout_ref.shape[0]
        block = lambda e, dp: att_block(gatt_s, dp, at.event[e], rows)
        reduce = Reduce(
            at, block, lambda e, r: block(e, at.chips[r]), lambda ref: (ref,),
            (c, dd, x, y, line), send, recv,
        )

        def cross(r):
            for e in (3, 2, 1, 0):
                reduce.cross(e, r)

        chip = lax.div(at.dp, 2)
        turn = jnp.where(step == 0, 3 - chip, jnp.where(step == 1, flip(chip, 1), jnp.where(step == 2, flip(chip, 2), chip)))
        do = lambda f, e: lambda: f(e)
        schedule = [
            ((0, 1), do(cross, 3)),
            ((1, 1), do(cross, 1)),
            ((2, 1), do(cross, 2)),
            ((3, 1), do(cross, 0)),
            ((3, 1), do(reduce.corner, 3)),
            ((4, 1), do(reduce.corner, 2)),
            ((4, 1), do(reduce.plane, 3)),
            ((5, 1), do(reduce.corner, 1)),
            ((5, 1), do(reduce.plane, 2)),
            ((6, 1), do(reduce.along, 3)),
            ((6, 1), do(reduce.corner, 0)),
            ((7, 1), do(reduce.plane, 1)),
        ]

    @pl.when(step == 0)
    def _():
        if links:
            at.barrier()
        fetch.start()
        vecg_s[...] = jnp.zeros_like(vecg_s)

    @pl.when(step < 4)
    def _():
        total = images * RI
        left = dp_ref[:, :, pl.ds(pl.multiple_of(turn * d, 128), d)].reshape(total, d)
        where = pl.ds(pl.multiple_of(turn * d, 128), d)

        @pl.when(turn < 3)
        def _():
            gatt_s[where, :] = tn(left, normed_ref[...].reshape(total, d)).astype(bf16)

        @pl.when(turn == 3)
        def _():
            gatt_s[where, :] = tn(left, mixed_ref[...].reshape(total, d)).astype(bf16)

    @pl.when(step == 3)
    def _():
        fetch.wait()

    @pl.when(step > 3)
    def _():
        image = step - 4
        standard, inverse = normalize(kept_ref[image].astype(f32))
        ng = rg_ref[image] * vec_ref[2:3] + nn(dp_ref[image, :, : 3 * d], watt_s[...])
        grad = resg_ref[image] + norm_backward(ng, standard, inverse, vec_ref[0:1])
        high = grad.astype(bf16)
        high_ref[image] = high
        low_ref[image] = (grad - high.astype(f32)).astype(bf16)
        vecg_s[...] += jnp.concatenate([colsum(ng * standard), colsum(ng), jnp.zeros((6, d), f32)], axis=0)

    pump(schedule, step, 1)
    if links:
        @pl.when(step == 3 + images)
        def _():
            vbuf[0, 0:2] = vecg_s[0:2]
            vbuf[0, 2:9] = vecb_ref[0:7]
            vbuf[0, 9:13] = bias_ref[...]
            vbuf[0, 13:16] = jnp.zeros((3, d), f32)
            exchange = lambda k, to: remote(
                vbuf.at[k], vbuf.at[8 + k], vsend.at[k], vrecv.at[k], to
            )
            exchange(0, at.core).start()
            reduce.plane(0)
            exchange(0, at.core).wait()
            vbuf[1] = vbuf[0] + vbuf[8]
            exchange(1, at.x).start()
            reduce.along(2)
            exchange(1, at.x).wait()
            vbuf[2] = vbuf[1] + vbuf[9]
            exchange(2, at.y).start()
            reduce.along(1)
            exchange(2, at.y).wait()
            vbuf[3] = vbuf[2] + vbuf[10]
            lines = [
                lambda k=k: remote(
                    vbuf.at[3], vbuf.at[4 + at.z], vsend.at[2 + k], vrecv.at[3 + at.z],
                    (at.dp, at.line[k]),
                )
                for k in range(1, MP)
            ]
            for make in lines:
                make().start()
            vbuf[4 + at.z] = vbuf[3]
            reduce.along(0, gout_ref)
            for k in range(1, MP):
                zb = at.line[k]
                remote(
                    vbuf.at[3], vbuf.at[4 + zb], vsend.at[2 + k], vrecv.at[3 + zb], at.core
                ).wait_recv()
            total = vbuf[4] + vbuf[5] + vbuf[6] + vbuf[7]
            vecout_ref[...] = total[: vecout_ref.shape[0]]
            for make in lines:
                make().wait_send()
            reduce.sends.finish()
    else:
        @pl.when(step == 3 + images)
        def _():
            pass


def scatter_kernel(
    high_ref, low_ref, result_ref, idx_ref, tok_ref, cot_ref, ing_ref, out_ref,
    tok_s, cot_s, ing_s, out_s, load, store,
):
    images, _, d = high_ref.shape
    loads = []
    for k, (a, b) in enumerate(CROPS):
        for j, (src, dst) in enumerate(((cot_ref, cot_s), (tok_ref, tok_s))):
            c = pltpu.make_async_copy(src.at[a:b], dst.at[a:b], load.at[j, k])
            c.start()
            loads.append(c)
    stores = []
    offset = 0
    for k, ((a, b), (lo, hi)) in enumerate(zip(CROPS, UNITS)):
        n, rows = hi - lo, images * (b - a)
        index = idx_ref[0:1, offset : offset + images * n]
        offset += images * n
        hot = (lax.broadcasted_iota(jnp.int32, (rows, images * n), 0) == index).astype(f32)
        taken = jnp.sum(hot, axis=-1, keepdims=True) > 0.5
        hot = hot.astype(bf16)
        window = lambda ref: jnp.concatenate([ref[i, lo:hi] for i in range(images)], axis=0)
        spread = nn(hot, window(high_ref)) + nn(hot, window(low_ref))
        loads[2 * k].wait()
        old = cot_s[a:b].reshape(rows, d).astype(f32)
        ing_s[a:b] = jnp.where(taken, spread, old).reshape(b - a, images, d)
        stores.append(pltpu.make_async_copy(ing_s.at[a:b], ing_ref.at[a:b], store.at[0, k]))
        stores[-1].start()
        loads[2 * k + 1].wait()
        old = tok_s[a:b].reshape(rows, d).astype(f32)
        new = jnp.where(taken, nn(hot, window(result_ref)), old).astype(bf16)
        out_s[a:b] = new.reshape(b - a, images, d)
        stores.append(pltpu.make_async_copy(out_s.at[a:b], out_ref.at[a:b], store.at[1, k]))
        stores[-1].start()
    for c in stores:
        c.wait()


def adamw(grad, first, second, master, average, rate, decay):
    first_new = 0.5 * first + 0.5 * grad
    second_new = 0.5 * second + 0.5 * grad * grad
    update = first_new / (jnp.sqrt(second_new) + 1e-08)
    master_new = master - rate * (update + decay * master)
    average_new = 0.9 * average + 0.1 * master_new
    return (first_new, second_new, master_new, average_new)


def sds(*shape_dtype):
    return jax.ShapeDtypeStruct(shape_dtype[:-1], shape_dtype[-1])


def window_index(kept_index):
    images = kept_index.shape[0]
    padded = jnp.concatenate([kept_index, jnp.full((images, RI - KEPT), -1, jnp.int32)], axis=1)
    pieces = []
    for (a, b), (s, e), (lo, hi) in zip(CROPS, SPANS, UNITS):
        row = lax.broadcasted_iota(jnp.int32, (images, hi - lo), 1) + lo
        image = lax.broadcasted_iota(jnp.int32, (images, hi - lo), 0)
        place = (padded[:, lo:hi] - a) * images + image
        pieces.append(jnp.where((row >= s) & (row < e), place, -1).reshape(-1))
    return jnp.concatenate(pieces)


def scratch(*shape_dtype):
    return pltpu.VMEM(shape_dtype[:-1], shape_dtype[-1])


def dma(*shape):
    return pltpu.SemaphoreType.DMA(shape)


def per_device(
    tokens, cotangent, kept_index,
    attention_weights, attention_first, attention_second, attention_average,
    feedforward_weights, feedforward_first, feedforward_second, feedforward_average,
    vector_weights, vector_first, vector_second, vector_average,
):
    images, length, d = tokens.shape
    ndp, nmp = lax.axis_size("dp"), lax.axis_size("mp")
    links = (ndp, nmp) == (8, MP)
    vec = vector_weights
    rows, hb = feedforward_weights.shape[1:]
    hidden = nmp * hb
    mask = masks()
    mask_specs = [full(m.shape) for m in mask]
    places = window_index(kept_index)
    index_col, index_row = places[:, None], places[None, :]
    tok, cot = tokens.transpose(1, 0, 2), cotangent.transpose(1, 0, 2)
    comm = (lambda i: dict(collective_id=i, has_side_effects=True)) if links else (lambda i: {})

    att, ff = attention_weights.T.astype(bf16), feedforward_weights.astype(bf16)
    if not links:
        att = lax.all_gather(att, ("dp", "mp"), axis=0, tiled=True)
        wff = lax.all_gather(lax.all_gather(ff, "dp", axis=1, tiled=True), "mp", axis=0)
    now = lambda *s: pl.BlockSpec((1,) + s, lambda i: (jnp.maximum(i - 1, 0), 0, 0))
    whole = lambda *s: pl.BlockSpec(s, lambda j: (0,) * len(s), pipeline_mode=pl.Buffered(1))
    rowspec = (images, RI, d)
    outs = pl.pallas_call(
        functools.partial(forward_kernel, links),
        grid=(1 + images,),
        in_specs=[ANY, ANY, full(index_col.shape), full(vec.shape), *mask_specs, ANY, ANY],
        out_specs=[full(rowspec)] * 3 + [
            now(RI, 3 * d), now(RI, d), now(RI, d), now(RI, d), now(RI, d), ANY,
        ] + [ANY] * links,
        out_shape=[sds(*rowspec, bf16)] * 3 + [
            sds(images, RI, 3 * d, bf16), sds(*rowspec, bf16), sds(*rowspec, f32),
            sds(*rowspec, f32), sds(*rowspec, bf16), sds(4 * d, d, bf16),
        ] + [sds(nmp, 2, d, hb, bf16)] * links,
        scratch_shapes=[
            scratch(4 * d, d, bf16), scratch(length, images, d, bf16), scratch(length, images, d, bf16),
            dma(3),
        ] + ([dma(2, Gather.SLOTS), dma(2, Gather.SLOTS), dma(2)] if links else []),
        compiler_params=params(**comm(0)),
        name="forward",
    )(tok, cot, index_col, vec, *mask, att, ff)
    kept, normed, cotk, proj, mixed, branch, resid, n2, watt = outs[:9]
    if links:
        wff = outs[9]

    bias = vec[9:].reshape(nmp, 1, hb)
    result, n2g, gff, bg = pl.pallas_call(
        feed_kernel,
        grid=(nmp,),
        in_specs=[
            whole(*rowspec), whole(*rowspec), whole(*rowspec),
            pl.BlockSpec((1, 2, d, hb), lambda j: (j, 0, 0, 0)),
            pl.BlockSpec((1, 1, hb), lambda j: (j, 0, 0)),
            full(vec.shape),
        ],
        out_specs=[
            full(rowspec), full(rowspec),
            pl.BlockSpec((1, 2, d, hb), lambda j: (j, 0, 0, 0)),
            pl.BlockSpec((1, 1, hb), lambda j: (j, 0, 0)),
        ],
        out_shape=[
            sds(*rowspec, bf16), sds(*rowspec, f32),
            sds(nmp, 2, d, hb, bf16), sds(nmp, 1, hb, f32),
        ],
        scratch_shapes=[
            scratch(*rowspec, f32), scratch(images * RI, hb, bf16), scratch(images * RI, hb, bf16),
        ],
        compiler_params=params(),
        name="feedforward",
    )(n2, cotk, resid, wff, bias, vec)

    spans = (16, 16, 4, 4, 4, 4)
    outs = pl.pallas_call(
        functools.partial(backward_kernel, links),
        grid=(images,),
        in_specs=[
            per_image(RI, d), per_image(RI, d), per_image(RI, d), per_image(RI, d),
            per_image(RI, d), per_image(RI, 3 * d),
            full(watt.shape), full(vec.shape), *mask_specs,
        ] + [ANY] * links,
        out_specs=[per_image(RI, 4 * d), per_image(RI, d), per_image(RI, 1), full((8, d))]
        + [full((2, rows, hb))] * links,
        out_shape=[
            sds(images, RI, 4 * d, bf16), sds(*rowspec, f32), sds(images, RI, 1, f32), sds(8, d, f32),
        ] + [sds(2, rows, hb, f32)] * links,
        scratch_shapes=[scratch(RI, d, bf16)] + (
            [scratch(n, 2, rows, hb, bf16) for n in spans]
            + [dma(Reduce.SLOTS), dma(Reduce.SLOTS), dma(16)] if links else []
        ),
        compiler_params=params(**comm(1)),
        name="attention_backward",
    )(n2g, cotk, branch, resid, normed, proj, watt, vec, *mask, *([gff] if links else []))
    dp, resg, rg, vecg = outs[:4]
    if links:
        feedforward_gradient = outs[4]

    full_d = (4 * d, d)
    outs = pl.pallas_call(
        functools.partial(grads_kernel, links),
        grid=(4 + images,),
        in_specs=[
            whole(images, RI, 4 * d), whole(*rowspec), whole(*rowspec), whole(images, RI, 1),
            whole(*rowspec), whole(*rowspec), full(vec.shape), ANY,
        ] + [full((8, d)), full((hidden // d, d))] * links,
        out_specs=[full(rowspec), full(rowspec)]
        + ([full((rows, d)), full(vec.shape)] if links else [full(full_d), full((8, d))]),
        out_shape=[sds(*rowspec, bf16), sds(*rowspec, bf16)]
        + ([sds(rows, d, f32), sds(*vec.shape, f32)] if links else [sds(*full_d, bf16), sds(8, d, f32)]),
        scratch_shapes=[scratch(3 * d, d, bf16)] + (
            [scratch(*full_d, bf16), scratch(8, d, f32), dma(1)]
            + [scratch(n, rows, d, bf16) for n in spans[1:]]
            + [dma(Reduce.SLOTS), dma(Reduce.SLOTS), scratch(11, 16, d, f32), dma(8), dma(8)]
            if links else [dma(1)]
        ),
        compiler_params=params(**comm(2)),
        name="attention_grads",
    )(
        dp, normed, mixed, rg, resg, kept, vec, watt,
        *([vecg, bg.reshape(hidden // d, d)] if links else []),
    )
    high, low = outs[:2]
    if links:
        gatt, vector_gradient = outs[2:]
    else:
        gatt, vecg_in = outs[2:]
        local = jnp.concatenate([vecg_in[:2], vecg[:7], bg.reshape(hidden // d, d)], axis=0)
        gatt = lax.psum_scatter(gatt, ("dp", "mp"), scatter_dimension=0, tiled=True).astype(f32)
        gff = lax.psum_scatter(gff, "mp", scatter_dimension=0, tiled=False)
        gff = lax.psum_scatter(gff, "dp", scatter_dimension=1, tiled=True)
        feedforward_gradient, vector_gradient = gff.astype(f32), lax.psum(local, ("dp", "mp"))

    ing, out = pl.pallas_call(
        scatter_kernel,
        in_specs=[pl.BlockSpec(memory_space=pltpu.VMEM)] * 4 + [ANY, ANY],
        out_specs=[ANY, ANY],
        out_shape=[sds(length, images, d, f32), sds(length, images, d, bf16)],
        scratch_shapes=[
            scratch(length, images, d, bf16), scratch(length, images, d, bf16),
            scratch(length, images, d, f32), scratch(length, images, d, bf16), dma(2, 3), dma(2, 3),
        ],
        compiler_params=params(),
        name="scatter_rows",
    )(high, low, result, index_row, tok, cot)
    input_gradient, block_output = ing.transpose(1, 0, 2), out.transpose(1, 0, 2)

    attention_gradient = gatt.T
    attention_new = adamw(
        attention_gradient, attention_first, attention_second,
        attention_weights, attention_average, 0.02, 0.05,
    )
    feedforward_new = adamw(
        feedforward_gradient, feedforward_first, feedforward_second,
        feedforward_weights, feedforward_average, 0.02, 0.05,
    )
    vector_new = adamw(
        vector_gradient, vector_first, vector_second, vector_weights, vector_average, 0.2, 0.0
    )
    return (
        block_output, input_gradient,
        attention_gradient, *attention_new, attention_new[2].astype(bf16),
        feedforward_gradient, *feedforward_new, feedforward_new[2].astype(bf16),
        vector_gradient, *vector_new, vector_gradient[3],
    )


def solution(mesh):
    rows = P(("dp", "mp"), None, None)
    att = P(None, ("dp", "mp"))
    feed = P(None, "dp", "mp")
    in_specs = (rows, rows, P(("dp", "mp"), None)) + (att,) * 4 + (feed,) * 4 + (P(),) * 4
    out_specs = (rows, rows) + (att,) * 6 + (feed,) * 6 + (P(),) * 6
    return jax.shard_map(
        per_device, mesh=mesh, in_specs=in_specs, out_specs=out_specs, check_vma=False
    )
```

time: 653 us -> 284 us (0.43)
  waiting for transfers between devices: 397 us -> 0 us
  Pallas kernels: 161 us -> 264 us
  blocking collectives: 42.5 us -> 0 us
  local copies, waits for them, and re-layouts: 26.6 us -> 7.67 us
  between operations: 14.3 us -> 0.83 us
    all_gather x3 -> x0, waiting for transfers between devices: 219 us -> none  [the longest x1 136 us: gather_weights(): wff = lax.all_gather(wff, 'mp', axis=0, tiled=False)]
    reduce_scatter x3 -> x0, waiting for transfers between devices: 178 us -> none  [the longest x1 113 us: reduce_grads(): gff = lax.psum_scatter(gff, 'mp', scatter_dimension=0, tiled=False)]
    pallas_call x7 -> x5, Pallas kernels: 161 us -> 264 us  [the longest x1 87.7 us: per_device(): pl.pallas_call(functools.partial(forward_kernel, links), grid=(1 + images...]
    psum x1 -> x0, blocking collectives: 42.5 us -> none  [per_device(): vector_gradient = lax.psum(vector_local, ('dp', 'mp'))]
    unnamed x45 -> x40, local copies, waits for them, and re-layouts: 21.9 us -> 2.84 us
  transfers between devices with their start and end apart: 6 -> 0, of which waited for: 6 -> 0; matrix products, arithmetic and copies ran while one was open for 5% -> 0% of each run, Pallas kernels for 18% -> 0%
where the time goes in v3:
time: 284 us
  Pallas kernels  264 us (93%)
  other arithmetic  11.7 us (4%)
  local copies, waits for them, and re-layouts  7.67 us (3%)
    pallas_call x1, Pallas kernels, per_device(): pl.pallas_call(functools.partial(forward_kernel, links), grid=(1 + images...  87.7 us
    pallas_call x1, Pallas kernels, per_device(): pl.pallas_call(functools.partial(backward_kernel, links), grid=(images,),...  66.6 us
    pallas_call x1, Pallas kernels, per_device(): pl.pallas_call(functools.partial(grads_kernel, links), grid=(4 + images,)...  51.1 us
    pallas_call x1, Pallas kernels, per_device(): pl.pallas_call(feed_kernel, grid=(nmp,), in_specs=[whole(*rowspec), whole...  45.9 us
    pallas_call x1, Pallas kernels, per_device(): pl.pallas_call(scatter_kernel, in_specs=[pl.BlockSpec(memory_space=pltpu....  12.2 us

profile of v3, /device:TPU:0, one launch (start us, length us, event | category | flops | bytes accessed | tf_op | source)
XLA Modules:
  0.0 283.8 jit_solution(11523358618881232498)
XLA Ops:
  0.7 0.8 fusion.6
  1.4 0.1 reshape.57
  1.5 0.8 add_select_fusion
  2.4 0.1 reshape.56
  2.5 0.1 reshape.55
  2.5 0.1 concatenate.7
  2.6 0.6 broadcast_in_dim.18.idx_ref
  3.2 0.7 slice.18
  4.0 0.6 reshape.58.bias_ref
  4.6 1.6 convert_bitcast_fusion.att_ref
  6.2 1.8 convert_element_type.16.ff_ref
  8.0 1.1 broadcast_in_dim.19.idx_ref
  9.1 87.7 %forward.1 = (bf16[4,272,768]{2,1,0:T(8,128)(2,1)}, bf16[4,272,768]{2,1,0:T(8,128)(2,1)}, bf16[4,272,768]{2,1,0:T(8,128)(2,1)}, bf16[4,272,2304]{2,1,0:T(8,128)(...) custom-call(bf16[542,4,768]{2,1,0:T(4,128)(2,1)} %bitcast.11, ...), custom_call_target="tpu_custom_call" | custom-call | tf_op jit(solution)/shard_map/forward/pallas_call | solution.py:854
  96.7 45.9 %feedforward.1 = (bf16[4,272,768]{2,1,0:T(8,128)(2,1)}, f32[4,272,768]{2,1,0:T(8,128)}, bf16[4,2,768,768]{3,2,1,0:T(8,128)(2,1)}, f32[4,1,768]{2,1,0:T(1,128)}) custom-call(bf16[4,272,768]{2,1,0:T(8,128)(2,1)} %get-tuple-element.45.n2_ref, bf16[4,272,768]{2,1,0:T(8,128)(2,1)} %get-tuple-element.46.cot_ref.cotk_ref, ...), custom_call_target="tpu_custom_call" | custom-call | tf_op jit(solution)/shard_map/feedforward/pallas_call | solution.py:877
  142.6 66.6 %attention_backward.1 = (bf16[4,272,3072]{2,1,0:T(8,128)(2,1)}, f32[4,272,768]{2,1,0:T(8,128)}, f32[4,272,1]{2,1,0:T(8,128)}, f32[8,768]{1,0:T(8,128)}, f32[2,96,768]{2,1,0:T(8,128)}) custom-call(f32[4,272,768]{2,1,0:T(8,128)} %get-tuple-element.49.n2g_ref, bf16[4,272,768]{2,1,0:T(8,128)(2,1)} %get-tuple-element.46.cot_ref.cotk_ref, ...), custom_call_target="tpu_custom_call" | custom-call | tf_op jit(solution)/shard_map/attention_backward/pallas_call | solution.py:903
  209.2 0.0 copy-done.17
  209.2 0.6 copy.44
  209.9 0.0 copy-start.5
  209.9 0.0 copy-start.10
  209.9 0.0 copy-start.11
  209.9 0.0 copy-start.12
  209.9 51.1 %attention_grads.1 = (bf16[4,272,768]{2,1,0:T(8,128)(2,1)}, bf16[4,272,768]{2,1,0:T(8,128)(2,1)}, f32[96,768]{1,0:T(8,128)}, f32[13,768]{1,0:T(8,128)}) custom-call(bf16[4,272,3072]{2,1,0:T(8,128)(2,1)} %get-tuple-element.55.dp_ref, bf16[4,272,768]{2,1,0:T(8,128)(2,1)} %get-tuple-element.51.normed_ref, bf16[4,272,768]{2,1,0:T(8,128)(2,1)} %get-tuple-element.56.mixed_ref, ...), custom_call_target="tpu_custom_call" | custom-call | tf_op jit(solution)/shard_map/attention_grads/pallas_call | solution.py:928
  261.1 0.0 copy-start.1
  261.1 0.0 copy-start.2
  261.1 0.0 copy-start.7
  261.1 0.0 copy-start.8
  261.1 1.5 slice_reduce_fusion
  262.6 0.0 copy-done.3
  262.6 0.0 copy-done.14
  262.6 0.0 copy-done.15
  262.6 0.0 copy-done.16
  262.6 1.5 multiply_add_fusion.5
  264.1 0.0 copy-done.5
  264.1 0.0 copy-done.10
  264.1 0.0 copy-done.11
  264.1 0.0 copy-start.9
  264.1 2.0 fusion.10
  266.1 0.0 copy-done.12
  266.1 0.8 multiply_add_fusion.3
  266.9 0.0 copy-done.1
  266.9 0.0 copy-done.2
  266.9 0.0 copy-done.7
  266.9 1.4 fusion.8
  268.3 1.0 multiply_add_fusion.1
  269.4 12.2 %scatter_rows.1 = (f32[542,4,768]{2,1,0:T(4,128)}, bf16[542,4,768]{2,1,0:T(4,128)(2,1)}) custom-call(bf16[4,272,768]{2,1,0:T(8,128)(2,1)} %get-tuple-element.62.high_ref, bf16[4,272,768]{2,1,0:T(8,128)(2,1)} %get-tuple-element.63.low_ref, bf16[4,272,768]{2,1,0:T(8,128)(2,1)} %get-tuple-element.64.result_ref, s32[1,1216]{1,0:T(1,128)} %broadcast_in_dim.18.idx_ref, ...), custom_call_target="tpu_custom_call" | custom-call | tf_op jit(solution)/shard_map/scatter_rows/pallas_call | solution.py:962
  281.6 0.7 copy.48
  282.3 0.8 copy.49
  283.2 0.6 copy.50
  (17 shorter events, 0.0 us)
Async XLA Ops:
  142.6 66.7 %copy-start.17 = (f32[4,1,768]{2,1,0:T(1,128)S(1)}, f32[4,1,768]{2,1,0:T(1,128)}, u32[]{:S(2)}) copy-start(f32[4,1,768]{2,1,0:T(1,128)} %get-tuple-element.61) | copy-start | bytes 36868
  209.8 52.8 %copy-start.3 = (f32[13,768]{1,0:T(8,128)S(1)}, f32[13,768]{1,0:T(8,128)}, u32[]{:S(2)}) copy-start(f32[13,768]{1,0:T(8,128)} %vec_ref.7) | copy-start | bytes 119812
  209.9 52.8 %copy-start.14 = (f32[13,768]{1,0:T(8,128)S(1)}, f32[13,768]{1,0:T(8,128)}, u32[]{:S(2)}) copy-start(f32[13,768]{1,0:T(8,128)} %param.35) | copy-start | bytes 119812
  209.9 52.8 %copy-start.15 = (f32[13,768]{1,0:T(8,128)S(1)}, f32[13,768]{1,0:T(8,128)}, u32[]{:S(2)}) copy-start(f32[13,768]{1,0:T(8,128)} %param.34) | copy-start | bytes 119812
  209.9 52.8 %copy-start.16 = (f32[13,768]{1,0:T(8,128)S(1)}, f32[13,768]{1,0:T(8,128)}, u32[]{:S(2)}) copy-start(f32[13,768]{1,0:T(8,128)} %param.33) | copy-start | bytes 119812
  209.9 54.2 %copy-start.5 = (f32[768,96]{0,1:T(8,128)S(1)}, f32[768,96]{0,1:T(8,128)}, u32[]{:S(2)}) copy-start(f32[768,96]{0,1:T(8,128)} %param.24) | copy-start | bytes 884740
  209.9 54.2 %copy-start.10 = (f32[768,96]{0,1:T(8,128)S(1)}, f32[768,96]{0,1:T(8,128)}, u32[]{:S(2)}) copy-start(f32[768,96]{0,1:T(8,128)} %param.26) | copy-start | bytes 884740
  209.9 54.2 %copy-start.11 = (f32[768,96]{0,1:T(8,128)S(1)}, f32[768,96]{0,1:T(8,128)}, u32[]{:S(2)}) copy-start(f32[768,96]{0,1:T(8,128)} %param.25) | copy-start | bytes 884740
  209.9 56.2 %copy-start.12 = (f32[768,96]{0,1:T(8,128)S(1)}, f32[768,96]{0,1:T(8,128)}, u32[]{:S(2)}) copy-start(f32[768,96]{0,1:T(8,128)} %param.27) | copy-start | bytes 884740
  261.1 5.9 %copy-start.1 = (f32[2,96,768]{2,1,0:T(8,128)S(1)}, f32[2,96,768]{2,1,0:T(8,128)}, u32[]{:S(2)}) copy-start(f32[2,96,768]{2,1,0:T(8,128)} %param.28) | copy-start | bytes 1769476
  261.1 5.9 %copy-start.2 = (f32[2,96,768]{2,1,0:T(8,128)S(1)}, f32[2,96,768]{2,1,0:T(8,128)}, u32[]{:S(2)}) copy-start(f32[2,96,768]{2,1,0:T(8,128)} %get-tuple-element.114) | copy-start | bytes 1769476
  261.1 5.9 %copy-start.7 = (f32[2,96,768]{2,1,0:T(8,128)S(1)}, f32[2,96,768]{2,1,0:T(8,128)}, u32[]{:S(2)}) copy-start(f32[2,96,768]{2,1,0:T(8,128)} %param.30) | copy-start | bytes 1769476
  261.1 5.8 %copy-start.8 = (f32[2,96,768]{2,1,0:T(8,128)S(1)}, f32[2,96,768]{2,1,0:T(8,128)}, u32[]{:S(2)}) copy-start(f32[2,96,768]{2,1,0:T(8,128)} %param.29) | copy-start | bytes 1769476
  264.1 4.2 %copy-start.9 = (f32[2,96,768]{2,1,0:T(8,128)S(1)}, f32[2,96,768]{2,1,0:T(8,128)}, u32[]{:S(2)}) copy-start(f32[2,96,768]{2,1,0:T(8,128)} %param.31) | copy-start | bytes 1769476
  266.1 3.2 %copy-start.4 = (f32[768,96]{0,1:T(8,128)}, f32[768,96]{0,1:T(8,128)S(1)}, u32[]{:S(2)}) copy-start(f32[768,96]{0,1:T(8,128)S(1)} %get-tuple-element.111) | copy-start | bytes 884740
  268.3 13.3 %copy-start = (f32[2,96,768]{2,1,0:T(8,128)}, f32[2,96,768]{2,1,0:T(8,128)S(1)}, u32[]{:S(2)}) copy-start(f32[2,96,768]{2,1,0:T(8,128)S(1)} %get-tuple-element.117) | copy-start | bytes 1769476
  269.4 12.3 %copy-start.6 = (f32[96,768]{1,0:T(8,128)S(1)}, f32[96,768]{1,0:T(8,128)}, u32[]{:S(2)}) copy-start(f32[96,768]{1,0:T(8,128)} %get-tuple-element.67) | copy-start | bytes 884740
  269.4 13.8 %copy-start.13 = (f32[13,768]{1,0:T(8,128)S(1)}, f32[13,768]{1,0:T(8,128)}, u32[]{:S(2)}) copy-start(f32[13,768]{1,0:T(8,128)} %get-tuple-element.120) | copy-start | bytes 119812

commit v4 on v3

--- a/solution.py
+++ b/solution.py
@@ -192,81 +192,78 @@
 class Gather:
     ALONG, X, Y, D, C, SLOTS = 0, 4, 8, 12, 16, 32
 
-    def __init__(self, at, tensors, send, recv, local, rows):
-        self.at, self.tensors, self.rows = at, tensors, rows
+    def __init__(self, at, first, place, send, recv, local):
+        self.at, self.first, self.place = at, first, place
         self.send, self.recv, self.local = send, recv, local
         self.sends = Sends()
 
-    def copy(self, t, base, e, dp, to, own=False):
-        mine, out, block = self.tensors[t]
-        zb = self.at.event[e]
-        dst = block(out, dp, zb, self.rows)
-        sems = self.send.at[t, base + zb], self.recv.at[t, base + zb]
-        return remote(mine if own else dst, dst, *sems, to)
-
-    def put(self, t, base, e, r, to, own=False, when=None):
-        self.sends.start(lambda: self.copy(t, base, e, self.at.chips[r], to, own), when)
-
-    def got(self, t, base, e, dp):
-        self.copy(t, base, e, dp, self.at.core).wait_recv()
-
-    def keep(self, t):
-        mine, out, block = self.tensors[t]
-        return pltpu.make_async_copy(
-            mine, block(out, self.at.dp, self.at.z, self.rows), self.local.at[t]
-        )
-
-    def spread(self, t, e):
-        own = e == 0
-        self.put(t, self.X, e, 0, self.at.x, own)
-        self.put(t, self.Y, e, 0, self.at.y, own)
-        self.put(t, self.C, e, 0, self.at.core, own)
-
-    def begin(self, t):
+    def copy(self, slot, e, r, to):
+        slot = self.ALONG + self.at.event[e] if slot is None else slot
+        dst = self.place(e, self.at.chips[r])
+        src = self.first(e) if r == 0 else dst
+        return remote(src, dst, self.send.at[slot], self.recv.at[slot], to)
+
+    def put(self, slot, e, r, to, when=None):
+        self.sends.start(lambda: self.copy(slot, e, r, to), when)
+
+    def got(self, slot, e, dp):
+        dst = self.place(e, dp)
+        remote(dst, dst, self.send.at[slot], self.recv.at[slot], self.at.core).wait_recv()
+
+    def keep(self, e):
+        return pltpu.make_async_copy(self.first(e), self.place(e, self.at.dp), self.local.at[e])
+
+    def spread(self, e):
+        self.put(self.X + e, e, 0, self.at.x)
+        self.put(self.Y + e, e, 0, self.at.y)
+        self.put(self.C + 4 * e, e, 0, self.at.core)
+
+    def begin(self):
         at = self.at
-        self.keep(t).start()
-        self.put(t, self.ALONG, 0, 0, at.up, True, at.high)
-        self.put(t, self.ALONG, 0, 0, at.down, True, at.low)
-        self.spread(t, 0)
-
-    def along(self, t, e):
+        self.keep(0).start()
+        for to, when in ((at.up, at.high), (at.down, at.low)):
+            self.put(None, 0, 0, to, when)
+        self.spread(0)
+
+    def direct(self):
+        self.keep(0).start()
+        for zb in self.at.line[1:]:
+            self.put(None, 0, 0, (self.at.dp, zb))
+
+    def arrived(self, e):
+        self.got(self.ALONG + self.at.event[e], e, self.at.dp)
+
+    def along(self, e):
         at = self.at
-        self.got(t, self.ALONG, e, at.dp)
-        self.put(t, self.ALONG, e, 0, at.onward[e - 1], False, at.middle)
-        self.spread(t, e)
-
-    def plane(self, t, e):
+        self.arrived(e)
+        self.put(None, e, 0, at.onward[e - 1], at.middle)
+        self.spread(e)
+
+    def plane(self, e):
         at = self.at
-        self.got(t, self.X, e, at.chips[1])
+        self.got(self.X + e, e, at.chips[1])
         if e % 2 == 0:
-            self.put(t, self.D, e, 1, at.y)
-        self.put(t, self.C + 4, e, 1, at.core)
-        self.got(t, self.Y, e, at.chips[2])
+            self.put(self.D + e, e, 1, at.y)
+        self.put(self.C + 4 * e + 1, e, 1, at.core)
+        self.got(self.Y + e, e, at.chips[2])
         if e % 2 == 1:
-            self.put(t, self.D, e, 2, at.x)
-        self.put(t, self.C + 8, e, 2, at.core)
-
-    def corner(self, t, e):
-        self.got(t, self.D, e, self.at.chips[3])
-        self.put(t, self.C + 12, e, 3, self.at.core)
-
-    def actions(self, t):
-        do = lambda f, e: lambda: f(t, e)
-        order = [
-            (self.along, 1), (self.plane, 0), (self.along, 2), (self.plane, 1), (self.along, 3),
-            (self.plane, 2), (self.plane, 3),
-        ]
-        return [do(f, e) for f, e in order] + [do(self.corner, e) for e in range(4)]
-
-    def finish(self, t):
+            self.put(self.D + e, e, 2, at.x)
+        self.put(self.C + 4 * e + 2, e, 2, at.core)
+
+    def corner(self, e):
+        self.got(self.D + e, e, self.at.chips[3])
+        self.put(self.C + 4 * e + 3, e, 3, self.at.core)
+
+    def finish(self, e):
         for r in range(4):
-            for e in range(4):
-                self.got(t, self.C + 4 * r, e, self.at.mates[r])
-        self.keep(t).wait()
+            self.got(self.C + 4 * e + r, e, self.at.mates[r])
 
 
 def add_into(target, first, *others):
-    step = 32
+    if len(others) == 1 and target.dtype == bf16:
+        target[...] = first[...] + others[0][...]
+        return
+    step = 48
 
     @pl.loop(0, first.shape[0] // step)
     def _(i):
@@ -280,8 +277,8 @@
 class Reduce:
     C, D, X, Y, ALONG, SLOTS = 0, 16, 20, 24, 28, 32
 
-    def __init__(self, at, source, own, parts, bufs, send, recv, load=None):
-        self.at, self.source, self.own, self.parts = at, source, own, parts
+    def __init__(self, at, source, own, parts, bufs, send, recv, load=None, base=0):
+        self.at, self.source, self.own, self.parts, self.base = at, source, own, parts, base
         self.c, self.d, self.x, self.y, self.line = bufs
         self.send, self.recv, self.load = send, recv, load
         self.sends = Sends()
@@ -294,65 +291,83 @@
     def got(self, slot, dst):
         remote(dst, dst, self.send.at[slot], self.recv.at[slot], self.at.core).wait_recv()
 
+    def slot(self, e, r):
+        return 4 * (e - self.base) + r
+
     def cross(self, e, r):
-        i = 4 * e + r
+        i = self.slot(e, r)
         self.put(self.C + i, lambda: self.source(e, self.at.mates[r]), lambda: self.c.at[i], self.at.core)
         if self.load is not None:
             self.load(e, r).start()
 
     def add(self, e, r, *others, target=None):
-        i = 4 * e + r
+        i = self.slot(e, r)
         self.got(self.C + i, self.c.at[i])
         if self.load is not None:
             self.load(e, r).wait()
         refs = [self.own(e, r), self.c.at[i]] + list(others)
-        target = refs[0] if target is None else target
+        self.total(refs[0] if target is None else target, *refs)
+
+    def total(self, target, *refs):
         for t, *rest in zip(self.parts(target), *[self.parts(ref) for ref in refs]):
             add_into(t, *rest)
 
     def corner(self, e):
+        at, i = self.at, e - self.base
+        self.add(e, 3)
+        self.put(
+            self.D + i, lambda: self.own(e, 3), lambda: self.d.at[i], at.x if e % 2 else at.y
+        )
+        r, slot, buf, to = (1, self.X, self.x, at.x) if e % 2 else (2, self.Y, self.y, at.y)
+        self.add(e, r)
+        self.put(slot + i, lambda: self.own(e, r), lambda: buf.at[i], to)
+
+    def plane(self, e):
+        at, i = self.at, e - self.base
+        r, slot, buf, to = (2, self.Y, self.y, at.y) if e % 2 else (1, self.X, self.x, at.x)
+        self.got(self.D + i, self.d.at[i])
+        self.add(e, r, self.d.at[i])
+        self.put(slot + i, lambda: self.own(e, r), lambda: buf.at[i], to)
+
+    def gathered(self, e, *others, target=None):
+        i = e - self.base
+        self.got(self.X + i, self.x.at[i])
+        self.got(self.Y + i, self.y.at[i])
+        self.add(e, 0, self.x.at[i], self.y.at[i], *others, target=target)
+
+    def send_along(self, e, src):
         at = self.at
-        self.add(e, 3)
-        to = at.y if e % 2 else at.x
-        self.put(self.D + e, lambda: self.own(e, 3), lambda: self.d.at[e], to)
-        r, base, buf, to = (2, self.Y, self.y, at.y) if e % 2 else (1, self.X, self.x, at.x)
-        self.add(e, r)
-        self.put(base + e, lambda: self.own(e, r), lambda: buf.at[e], to)
-
-    def plane(self, e):
-        at = self.at
-        r, base, buf, to = (1, self.X, self.x, at.x) if e % 2 else (2, self.Y, self.y, at.y)
-        self.got(self.D + e, self.d.at[e])
-        self.add(e, r, self.d.at[e])
-        self.put(base + e, lambda: self.own(e, r), lambda: buf.at[e], to)
-
-    def along(self, e, out=None):
-        at = self.at
-        self.got(self.X + e, self.x.at[e])
-        self.got(self.Y + e, self.y.at[e])
-        if e:
-            self.add(e, 0, self.x.at[e], self.y.at[e])
-            zb = at.event[e]
-            self.sends.start(
-                lambda: remote(
-                    self.own(e, 0), self.line.at[at.z], self.send.at[self.ALONG + zb],
-                    self.recv.at[self.ALONG + at.z], (at.dp, zb),
-                )
+        zb = at.event[e]
+        self.sends.start(
+            lambda: remote(
+                src(), self.line.at[at.z], self.send.at[self.ALONG + zb],
+                self.recv.at[self.ALONG + at.z], (at.dp, zb),
             )
-        else:
-            lines = []
-            for k in range(1, MP):
-                zb = at.line[k]
-                dst = self.line.at[zb]
-                self.got(self.ALONG + zb, dst)
-                lines.append(dst)
-            self.add(0, 0, self.x.at[0], self.y.at[0], *lines, target=out)
+        )
+
+    def along(self, e):
+        self.gathered(e)
+        self.send_along(e, lambda: self.own(e, 0))
+
+    def lines(self):
+        got = []
+        for zb in self.at.line[1:]:
+            got.append(self.line.at[zb])
+            self.got(self.ALONG + zb, got[-1])
+        return got
 
 
 def pump(schedule, step, point):
     for (s, p), action in schedule:
-        if p == point:
-            pl.when(step == s)(action)
+        if isinstance(point, int):
+            if p == point:
+                pl.when(step == s)(action)
+        else:
+            pl.when((step == s) & (point == p))(action)
+
+
+def do(action, *args):
+    return lambda: action(*args)
 
 
 def forward_kernel(
@@ -362,7 +377,7 @@
     watt_out, *rest,
 ):
     if links:
-        wff_ref, watt_ref, tok_s, cot_s, load, send, recv, local = rest
+        wff_ref, watt_ref, tok_s, cot_s, load, att_s, ff_s, send, recv, local = rest
     else:
         watt_ref, tok_s, cot_s, load = rest
     step = pl.program_id(0)
@@ -371,29 +386,55 @@
         pltpu.make_async_copy(tok_ref, tok_s, load.at[0]),
         pltpu.make_async_copy(cot_ref, cot_s, load.at[1]),
     ]
+    acts, schedule = [[]] * 6, []
     if links:
         at = Place()
         rows = att_ref.shape[0]
-        tensors = ((att_ref, watt_ref, att_block), (ff_ref, wff_ref, ff_block))
-        gather = Gather(at, tensors, send, recv, local, rows)
-        store = pltpu.make_async_copy(watt_ref, watt_out, load.at[2])
-        att, feed = gather.actions(0), gather.actions(1)
-        spots = [(1, 1), (1, 1), (1, 4), (2, 2), (2, 3), (3, 1), (4, 2), (4, 4), (4, 4), (4, 4), (4, 4)]
-        schedule = list(zip(spots, feed))
+        att = Gather(
+            at, lambda e: att_block(watt_ref, at.dp, at.event[e], rows) if e else att_s,
+            lambda e, dp: att_block(watt_ref, dp, at.event[e], rows),
+            send.at[0], recv.at[0], local.at[0],
+        )
+        feed = Gather(
+            at, lambda e: ff_block(wff_ref, at.dp, at.event[e], rows) if e else ff_s,
+            lambda e, dp: ff_block(wff_ref, dp, at.event[e], rows),
+            send.at[1], recv.at[1], local.at[1],
+        )
+        acts = [
+            [do(att.along, 1), do(att.along, 2)],
+            [],
+            [do(att.along, 3), feed.direct, do(att.plane, 2)],
+            [do(att.plane, 1)],
+            [],
+            [do(att.plane, 0), do(att.plane, 3)] + [do(att.corner, e) for e in (0, 3, 2, 1)],
+        ]
+        schedule = [
+            ((2, 0), do(feed.arrived, 2)),
+            ((2, 0), do(feed.spread, 2)),
+            ((2, 1), do(feed.arrived, 3)),
+            ((2, 1), do(feed.spread, 3)),
+            ((3, 3), do(feed.plane, 2)),
+            ((4, 0), do(feed.plane, 3)),
+        ]
     else:
-        att, schedule = [lambda: None] * 11, []
         fetch = pltpu.make_async_copy(att_ref, watt_ref, load.at[2])
+    store = pltpu.make_async_copy(watt_ref, watt_out, load.at[2])
 
     @pl.when(step == 0)
     def _():
         if links:
+            att_s[...] = att_ref[...].astype(bf16)
             at.barrier()
-            gather.begin(0)
+            att.begin()
         else:
             fetch.start()
         for c in loads:
             c.start()
+        if links:
+            ff_s[...] = ff_ref[...].astype(bf16)
         offset = 0
+        run = lambda point: [action() for action in acts[point]]
+        run(0)
         loads[0].wait()
         loads[1].wait()
         for crop, ((a, b), (lo, hi)) in enumerate(zip(CROPS, UNITS)):
@@ -411,26 +452,22 @@
                         dst[i, lo + 16 : hi] = part[16:]
                     else:
                         dst[i, lo:hi] = part
-            att[crop]()
+            run(1 + crop)
         for i in range(images):
             standard, _ = normalize(kept_ref[i].astype(f32))
             normed_ref[i] = (standard * vec_ref[0:1] + vec_ref[1:2]).astype(bf16)
             if i == 1:
-                att[3]()
-        for action in att[4:6]:
-            action()
+                run(4)
+        run(5)
         if links:
-            gather.begin(1)
-        for action in att[6:]:
-            action()
-        if links:
-            gather.finish(0)
-            store.start()
+            for e in range(4):
+                att.finish(e)
+            att.keep(0).wait()
         else:
             fetch.wait()
-            done = pltpu.make_async_copy(watt_ref, watt_out, load.at[2])
-            done.start()
-            done.wait()
+        store.start()
+
+    pump(schedule, step, 0)
 
     @pl.when(step > 0)
     def _():
@@ -452,9 +489,7 @@
                 pt = softmax_keys(st, vrefs[unit][0:1]).astype(bf16)
                 out = join_heads(tn(pt, proj_ref[0, lo:hi, cols(2)]))
                 tail = store_window(mixed_ref, 0, lo, hi, unit == 2, cols(0), out, tail)
-            if pair == 1:
-                pump(schedule, step, 2)
-            if pair == 3:
+            if pair == 2:
                 pump(schedule, step, 3)
         branch = nt(mixed_ref[0], watt_ref[3 * d :, :]) + vec_ref[5:6]
         branch_ref[0] = branch
@@ -462,14 +497,19 @@
         resid_ref[0] = residual
         standard, _ = normalize(residual)
         n2_ref[0] = (standard * vec_ref[6:7] + vec_ref[7:8]).astype(bf16)
-        pump(schedule, step, 4)
-
-    if links:
-        @pl.when(step == images)
-        def _():
-            gather.finish(1)
-            gather.sends.finish()
-            store.wait()
+
+    @pl.when(step == images)
+    def _():
+        if links:
+            feed.corner(2)
+            feed.corner(3)
+            feed.finish(2)
+            feed.finish(3)
+            feed.arrived(1)
+            feed.keep(0).wait()
+            att.sends.finish()
+            feed.sends.finish()
+        store.wait()
 
 
 def router_score(normed, vec_ref):
@@ -478,42 +518,136 @@
 
 
 def feed_kernel(
-    n2_ref, cot_ref, resid_ref, w_ref, bias_ref, vec_ref,
-    result_ref, n2g_ref, gff_ref, bg_ref, out_s, act_s, ig_s,
+    links, n2_ref, cot_ref, resid_ref, w_ref, bias_ref, vec_ref,
+    result_ref, n2g_ref, gff_ref, bg_ref, *rest,
 ):
+    if links:
+        acc_ref, out_s, act_s, ig_s, w_s, g_s, load, store = rest[:8]
+        send, recv, local, a, c, dd, x, y, rsend, rrecv, rlocal = rest[8:]
+    else:
+        out_s, act_s, ig_s, w_s, g_s, load, store = rest
     step = pl.program_id(0)
-    images = n2_ref.shape[0]
-    d, hb = w_ref.shape[2], w_ref.shape[3]
-    bg_ref[0] = jnp.zeros((1, hb), f32)
+    last = pl.num_programs(0) - 1
+    images, _, d = n2_ref.shape
+    hb = w_ref.shape[3]
+    block, schedule = step, []
+    if links:
+        at = Place()
+        rows = acc_ref.shape[2]
+        block = at.event[0]
+        for e in (1, 2, 3):
+            block = jnp.where(step == 3 - e, at.event[e], block)
+        gather = Gather(
+            at, lambda e: ff_block(w_ref, at.dp, at.event[e], rows),
+            lambda e, dp: w_s.at[3 - e, :, pl.ds(pl.multiple_of(dp * rows, 32), rows), :],
+            send, recv, local,
+        )
+        reduce = Reduce(
+            at, lambda e, dp: ff_block(gff_ref, dp, at.event[e], rows),
+            lambda e, r: a.at[4 * (e - 2) + r],
+            lambda ref: (ref.at[0], ref.at[1]), (c, dd, x, y, None), rsend, rrecv,
+            lambda e, r: pltpu.make_async_copy(
+                ff_block(gff_ref, at.chips[r], at.event[e], rows), a.at[4 * (e - 2) + r],
+                rlocal.at[4 * (e - 2) + r],
+            ),
+            2,
+        )
+
+        def start():
+            at.barrier()
+            for e in (1, 0):
+                gather.spread(e)
+                gather.keep(e).start()
+
+        def ready(e):
+            gather.finish(e)
+            gather.keep(e).wait()
+
+        def cross(e):
+            for r in (3, 1, 2, 0):
+                reduce.cross(e, r)
+
+        schedule = [
+            ((1, 0), do(gather.plane, 1)),
+            ((1, 3), do(gather.plane, 0)),
+            ((1, 4), do(cross, 3)),
+            ((2, 0), do(gather.corner, 1)),
+            ((2, 0), do(reduce.corner, 3)),
+            ((2, 0), do(cross, 2)),
+            ((2, 0), do(ready, 1)),
+            ((2, 2), do(reduce.corner, 2)),
+            ((2, 2), do(gather.corner, 0)),
+            ((2, 5), do(reduce.plane, 3)),
+            ((3, 0), do(ready, 0)),
+            ((3, 0), do(reduce.plane, 2)),
+        ]
+
+    def fetch(e):
+        return pltpu.make_async_copy(
+            w_ref.at[at.event[3 - e] if links else e], w_s.at[e], load.at[e]
+        )
+
+    def save(slot, which):
+        return pltpu.make_async_copy(g_s.at[slot], gff_ref.at[which], store.at[slot])
+
+    early = (0, 1) if links else range(w_s.shape[0])
 
     @pl.when(step == 0)
     def _():
+        for e in early:
+            fetch(e).start()
+        if links:
+            start()
         out_s[...] = resid_ref[...] + vec_ref[8:9]
         n2g_ref[...] = jnp.zeros_like(n2g_ref)
+        bg_ref[...] = jnp.zeros_like(bg_ref)
+        fetch(0).wait()
+
+    for e in early[1:]:
+        @pl.when(step == e)
+        def _(e=e):
+            fetch(e).wait()
+
+    slot = lax.rem(step, 2)
+
+    @pl.when(step > 0)
+    def _():
+        save(1 - slot, 0).wait()
+
+    pump(schedule, step, 0)
 
     @pl.loop(0, images)
     def _(i):
-        inner = nn(n2_ref[i], w_ref[0, 0]) + bias_ref[0]
-        ag = nn(cot_ref[i], w_ref[0, 1])
+        pump(schedule, step, i + 1)
+        inner = nn(n2_ref[i], w_s[step, 0]) + bias_ref[block]
+        ag = nn(cot_ref[i], w_s[step, 1])
         phi = 0.5 * (1.0 + lax.erf(inner * 0.7071067811865476))
         act = (inner * phi).astype(bf16)
         slope = phi + inner * jnp.exp(-0.5 * inner * inner) * 0.3989422804014327
         ig = (ag * slope).astype(bf16)
-        rows = pl.ds(pl.multiple_of(i * RI, 16), RI)
-        act_s[rows, :] = act
-        ig_s[rows, :] = ig
-        bg_ref[0] += colsum(ig.astype(f32))
-        out_s[i] += nt(act, w_ref[0, 1])
-        n2g_ref[i] += nt(ig, w_ref[0, 0])
-
+        rows_i = pl.ds(pl.multiple_of(i * RI, 16), RI)
+        act_s[rows_i, :] = act
+        ig_s[rows_i, :] = ig
+        bg_ref[block] += colsum(ig.astype(f32))
+        out_s[i] += nt(act, w_s[step, 1])
+        n2g_ref[i] += nt(ig, w_s[step, 0])
+
+    pump(schedule, step, 5)
     n2 = n2_ref[...].reshape(images * RI, d)
     cot = cot_ref[...].reshape(images * RI, d)
-    gff_ref[0, 0] = tn(n2, ig_s[...]).astype(bf16)
-    gff_ref[0, 1] = tn(cot, act_s[...]).astype(bf16)
-
-    @pl.when(step == pl.num_programs(0) - 1)
+    g_s[slot, 0] = tn(n2, ig_s[...]).astype(bf16)
+    g_s[slot, 1] = tn(cot, act_s[...]).astype(bf16)
+    save(slot, block).start()
+
+    @pl.when(step == last)
     def _():
         result_ref[...] = out_s[...].astype(bf16)
+        if links:
+            reduce.gathered(3, target=acc_ref.at[0])
+            reduce.gathered(2, target=acc_ref.at[1])
+            gather.sends.finish()
+            reduce.sends.finish()
+        save(slot, 0).wait()
 
 
 def backward_kernel(
@@ -521,8 +655,8 @@
     vec_ref, m0_ref, m1_ref, m2_ref, v0_ref, v1_ref, v2_ref, *rest,
 ):
     if links:
-        gff_ref, dp_ref, resg_ref, rg_ref, vecg_ref, gout_ref = rest[:6]
-        mg_s, a, c, dd, x, y, line, send, recv, local = rest[6:]
+        gff_ref, acc_ref, dp_ref, resg_ref, rg_ref, vecg_ref, gout_ref = rest[:7]
+        mg_s, a, c, dd, x, y, line, send, recv, local = rest[7:]
     else:
         dp_ref, resg_ref, rg_ref, vecg_ref, mg_s = rest
     step = pl.program_id(0)
@@ -530,35 +664,31 @@
     if links:
         at = Place()
         rows = gout_ref.shape[1]
-        load = lambda e, r: pltpu.make_async_copy(
-            ff_block(gff_ref, at.chips[r], at.event[e], rows), a.at[4 * e + r], local.at[4 * e + r]
+        reduce = Reduce(
+            at, lambda e, dp: ff_block(gff_ref, dp, at.event[e], rows),
+            lambda e, r: a.at[4 * e + r],
+            lambda ref: (ref.at[0], ref.at[1]), (c, dd, x, y, line), send, recv,
+            lambda e, r: pltpu.make_async_copy(
+                ff_block(gff_ref, at.chips[r], at.event[e], rows), a.at[4 * e + r],
+                local.at[4 * e + r],
+            ),
         )
-        reduce = Reduce(
-            at, lambda e, dp: ff_block(gff_ref, dp, at.event[e], rows), lambda e, r: a.at[4 * e + r],
-            lambda ref: (ref.at[0], ref.at[1]), (c, dd, x, y, line), send, recv, load,
-        )
-
-        def cross(e):
-            for r in (3, 1, 2, 0):
-                reduce.cross(e, r)
 
         def start():
             at.barrier()
-            for e in (3, 2, 1, 0):
-                cross(e)
-
-        do = lambda f, e: lambda: f(e)
+            reduce.send_along(2, lambda: acc_ref.at[1])
+            for e in (1, 0):
+                for r in (3, 1, 2, 0):
+                    reduce.cross(e, r)
+
         schedule = [
             ((0, 0), start),
-            ((0, 1), do(reduce.corner, 3)),
-            ((0, 3), do(reduce.corner, 2)),
-            ((1, 1), do(reduce.plane, 3)),
-            ((1, 2), do(reduce.corner, 1)),
-            ((2, 0), do(reduce.plane, 2)),
-            ((2, 1), do(reduce.along, 3)),
-            ((2, 2), do(reduce.corner, 0)),
-            ((3, 0), do(reduce.plane, 1)),
-            ((3, 2), do(reduce.along, 2)),
+            ((0, 1), do(reduce.corner, 1)),
+            ((0, 3), do(reduce.send_along, 3, lambda: acc_ref.at[0])),
+            ((1, 1), do(reduce.plane, 1)),
+            ((1, 3), do(reduce.corner, 0)),
+            ((2, 1), do(reduce.along, 1)),
+            ((3, 0), do(reduce.plane, 0)),
         ]
 
     pump(schedule, step, 0)
@@ -593,9 +723,7 @@
             )
             for j in range(3):
                 tails[j] = store_window(dp_ref, 0, lo, hi, unit == 2, cols(j), grads[j], tails[j])
-        if pair == 1:
-            pump(schedule, step, 2)
-        if pair == 3:
+        if pair == 2:
             pump(schedule, step, 3)
     sums = jnp.concatenate(
         [
@@ -619,9 +747,7 @@
     if links:
         @pl.when(step == pl.num_programs(0) - 1)
         def _():
-            reduce.plane(0)
-            reduce.along(1)
-            reduce.along(0, gout_ref)
+            reduce.gathered(0, *reduce.lines(), target=gout_ref)
             reduce.sends.finish()
 
 
@@ -630,16 +756,18 @@
 ):
     if links:
         vecb_ref, bias_ref, high_ref, low_ref, gout_ref, vecout_ref = rest[:6]
-        watt_s, gatt_s, vecg_s, load, c, dd, x, y, line, send, recv, vbuf, vsend, vrecv = rest[6:]
+        gatt_s, vecg_s, watt_s, dp_s, act_s, resg_s, kept_s, load = rest[6:14]
+        c, dd, x, y, line, send, recv, vbuf, vsend, vrecv = rest[14:]
     else:
-        high_ref, low_ref, gatt_s, vecg_s, watt_s, load = rest
+        high_ref, low_ref, gatt_s, vecg_s, watt_s, dp_s, act_s, resg_s, kept_s, load = rest
     step = pl.program_id(0)
-    images, _, d = normed_ref.shape
-    fetch = pltpu.make_async_copy(watt_ref.at[: 3 * d], watt_s, load.at[0])
-    schedule = []
-    turn = step
+    images, _, d = high_ref.shape
+    last = 3 + images
+    total = images * RI
+    chip, schedule = 0, []
     if links:
         at = Place()
+        chip = lax.div(at.dp, 2)
         rows = gout_ref.shape[0]
         block = lambda e, dp: att_block(gatt_s, dp, at.event[e], rows)
         reduce = Reduce(
@@ -651,108 +779,135 @@
             for e in (3, 2, 1, 0):
                 reduce.cross(e, r)
 
-        chip = lax.div(at.dp, 2)
-        turn = jnp.where(step == 0, 3 - chip, jnp.where(step == 1, flip(chip, 1), jnp.where(step == 2, flip(chip, 2), chip)))
-        do = lambda f, e: lambda: f(e)
+        turns = (3 - chip, flip(chip, 1), flip(chip, 2), chip)
         schedule = [
-            ((0, 1), do(cross, 3)),
-            ((1, 1), do(cross, 1)),
-            ((2, 1), do(cross, 2)),
-            ((3, 1), do(cross, 0)),
-            ((3, 1), do(reduce.corner, 3)),
-            ((4, 1), do(reduce.corner, 2)),
+            ((1, 2), do(cross, 3)),
+            ((1, 2), do(cross, 1)),
+            ((2, 2), do(reduce.corner, 3)),
+            ((2, 2), do(cross, 2)),
+            ((3, 2), do(cross, 0)),
             ((4, 1), do(reduce.plane, 3)),
-            ((5, 1), do(reduce.corner, 1)),
-            ((5, 1), do(reduce.plane, 2)),
-            ((6, 1), do(reduce.along, 3)),
-            ((6, 1), do(reduce.corner, 0)),
-            ((7, 1), do(reduce.plane, 1)),
+            ((5, 0), do(reduce.corner, 2)),
+            ((6, 0), do(reduce.corner, 1)),
+            ((6, 0), do(reduce.along, 3)),
+            ((7, 0), do(reduce.plane, 2)),
         ]
+    else:
+        turns = (0, 1, 2, 3)
+    turn = turns[3]
+    for k in (2, 1, 0):
+        turn = jnp.where(step == k, turns[k], turn)
+
+    def columns(k):
+        lanes = pl.ds(pl.multiple_of(turns[k] * d, 128), d) if links else pl.ds(k * d, d)
+        return pltpu.make_async_copy(dp_ref.at[:, :, lanes], dp_s.at[turns[k]], load.at[k])
+
+    acts = [
+        pltpu.make_async_copy(normed_ref, act_s.at[0], load.at[4]),
+        pltpu.make_async_copy(mixed_ref, act_s.at[1], load.at[5]),
+    ]
+    later = [
+        pltpu.make_async_copy(watt_ref.at[: 3 * d], watt_s, load.at[6]),
+        pltpu.make_async_copy(resg_ref, resg_s, load.at[7]),
+        pltpu.make_async_copy(kept_ref, kept_s, load.at[8]),
+    ]
 
     @pl.when(step == 0)
     def _():
+        columns(0).start()
+        for copy in acts:
+            copy.start()
+        for k in (1, 2, 3):
+            columns(k).start()
+        for copy in later:
+            copy.start()
+        vecg_s[...] = jnp.zeros_like(vecg_s)
         if links:
             at.barrier()
-        fetch.start()
-        vecg_s[...] = jnp.zeros_like(vecg_s)
+        for copy in acts:
+            copy.wait()
+
+    for k in range(4):
+        @pl.when(step == k)
+        def _(k=k):
+            columns(k).wait()
 
     @pl.when(step < 4)
     def _():
-        total = images * RI
-        left = dp_ref[:, :, pl.ds(pl.multiple_of(turn * d, 128), d)].reshape(total, d)
+        which = jnp.where(turn == 3, 1, 0)
         where = pl.ds(pl.multiple_of(turn * d, 128), d)
-
-        @pl.when(turn < 3)
-        def _():
-            gatt_s[where, :] = tn(left, normed_ref[...].reshape(total, d)).astype(bf16)
-
-        @pl.when(turn == 3)
-        def _():
-            gatt_s[where, :] = tn(left, mixed_ref[...].reshape(total, d)).astype(bf16)
-
-    @pl.when(step == 3)
+        left = dp_s[turn].reshape(total, d)
+        gatt_s[where, :] = tn(left, act_s[which].reshape(total, d)).astype(bf16)
+
+    @pl.when(step == 4)
     def _():
-        fetch.wait()
+        for copy in later:
+            copy.wait()
+
+    pump(schedule, step, 0)
 
     @pl.when(step > 3)
     def _():
         image = step - 4
-        standard, inverse = normalize(kept_ref[image].astype(f32))
-        ng = rg_ref[image] * vec_ref[2:3] + nn(dp_ref[image, :, : 3 * d], watt_s[...])
-        grad = resg_ref[image] + norm_backward(ng, standard, inverse, vec_ref[0:1])
+        standard, inverse = normalize(kept_s[image].astype(f32))
+        ng = rg_ref[image] * vec_ref[2:3]
+        for j in range(3):
+            ng += nn(dp_s[j, image], watt_s[j * d : (j + 1) * d, :])
+        pump(schedule, step, 1)
+        grad = resg_s[image] + norm_backward(ng, standard, inverse, vec_ref[0:1])
         high = grad.astype(bf16)
         high_ref[image] = high
         low_ref[image] = (grad - high.astype(f32)).astype(bf16)
-        vecg_s[...] += jnp.concatenate([colsum(ng * standard), colsum(ng), jnp.zeros((6, d), f32)], axis=0)
-
-    pump(schedule, step, 1)
-    if links:
-        @pl.when(step == 3 + images)
+        vecg_s[0:1] += colsum(ng * standard)
+        vecg_s[1:2] += colsum(ng)
+
+    pump(schedule, step, 2)
+    if links:
+        exchange = lambda k, to: remote(
+            vbuf.at[k + 1], vbuf.at[8 + k], vsend.at[k], vrecv.at[k], to
+        )
+        lines = [
+            lambda k=k: remote(
+                vbuf.at[0], vbuf.at[4 + at.z], vsend.at[2 + k], vrecv.at[3 + at.z],
+                (at.dp, at.line[k]),
+            )
+            for k in range(1, MP)
+        ]
+
+        @pl.when(step == last)
         def _():
             vbuf[0, 0:2] = vecg_s[0:2]
             vbuf[0, 2:9] = vecb_ref[0:7]
             vbuf[0, 9:13] = bias_ref[...]
             vbuf[0, 13:16] = jnp.zeros((3, d), f32)
-            exchange = lambda k, to: remote(
-                vbuf.at[k], vbuf.at[8 + k], vsend.at[k], vrecv.at[k], to
-            )
-            exchange(0, at.core).start()
-            reduce.plane(0)
-            exchange(0, at.core).wait()
-            vbuf[1] = vbuf[0] + vbuf[8]
-            exchange(1, at.x).start()
-            reduce.along(2)
-            exchange(1, at.x).wait()
-            vbuf[2] = vbuf[1] + vbuf[9]
-            exchange(2, at.y).start()
-            reduce.along(1)
-            exchange(2, at.y).wait()
-            vbuf[3] = vbuf[2] + vbuf[10]
-            lines = [
-                lambda k=k: remote(
-                    vbuf.at[3], vbuf.at[4 + at.z], vsend.at[2 + k], vrecv.at[3 + at.z],
-                    (at.dp, at.line[k]),
-                )
-                for k in range(1, MP)
-            ]
             for make in lines:
                 make().start()
-            vbuf[4 + at.z] = vbuf[3]
-            reduce.along(0, gout_ref)
+            vbuf[4 + at.z] = vbuf[0]
+            reduce.plane(1)
+            reduce.corner(0)
+            reduce.along(2)
             for k in range(1, MP):
                 zb = at.line[k]
                 remote(
-                    vbuf.at[3], vbuf.at[4 + zb], vsend.at[2 + k], vrecv.at[3 + zb], at.core
+                    vbuf.at[0], vbuf.at[4 + zb], vsend.at[2 + k], vrecv.at[3 + zb], at.core
                 ).wait_recv()
-            total = vbuf[4] + vbuf[5] + vbuf[6] + vbuf[7]
-            vecout_ref[...] = total[: vecout_ref.shape[0]]
+            vbuf[1] = vbuf[4] + vbuf[5] + vbuf[6] + vbuf[7]
+            exchange(0, at.core).start()
+            reduce.along(1)
+            exchange(0, at.core).wait()
+            vbuf[2] = vbuf[1] + vbuf[8]
+            exchange(1, at.x).start()
+            reduce.plane(0)
+            exchange(1, at.x).wait()
+            vbuf[3] = vbuf[2] + vbuf[9]
+            exchange(2, at.y).start()
+            exchange(2, at.y).wait()
+            full_sum = vbuf[3] + vbuf[10]
+            vecout_ref[...] = full_sum[: vecout_ref.shape[0]]
+            reduce.gathered(0, *reduce.lines(), target=gout_ref)
             for make in lines:
                 make().wait_send()
             reduce.sends.finish()
-    else:
-        @pl.when(step == 3 + images)
-        def _():
-            pass
 
 
 def scatter_kernel(
@@ -844,8 +999,9 @@
     tok, cot = tokens.transpose(1, 0, 2), cotangent.transpose(1, 0, 2)
     comm = (lambda i: dict(collective_id=i, has_side_effects=True)) if links else (lambda i: {})
 
-    att, ff = attention_weights.T.astype(bf16), feedforward_weights.astype(bf16)
+    att, ff = attention_weights.T, feedforward_weights
     if not links:
+        att, ff = att.astype(bf16), ff.astype(bf16)
         att = lax.all_gather(att, ("dp", "mp"), axis=0, tiled=True)
         wff = lax.all_gather(lax.all_gather(ff, "dp", axis=1, tiled=True), "mp", axis=0)
     now = lambda *s: pl.BlockSpec((1,) + s, lambda i: (jnp.maximum(i - 1, 0), 0, 0))
@@ -854,7 +1010,8 @@
     outs = pl.pallas_call(
         functools.partial(forward_kernel, links),
         grid=(1 + images,),
-        in_specs=[ANY, ANY, full(index_col.shape), full(vec.shape), *mask_specs, ANY, ANY],
+        in_specs=[ANY, ANY, full(index_col.shape), full(vec.shape), *mask_specs]
+        + ([full(att.shape), full(ff.shape)] if links else [ANY, ANY]),
         out_specs=[full(rowspec)] * 3 + [
             now(RI, 3 * d), now(RI, d), now(RI, d), now(RI, d), now(RI, d), ANY,
         ] + [ANY] * links,
@@ -865,7 +1022,10 @@
         scratch_shapes=[
             scratch(4 * d, d, bf16), scratch(length, images, d, bf16), scratch(length, images, d, bf16),
             dma(3),
-        ] + ([dma(2, Gather.SLOTS), dma(2, Gather.SLOTS), dma(2)] if links else []),
+        ] + (
+            [scratch(rows, d, bf16), scratch(2, rows, hb, bf16)]
+            + [dma(2, Gather.SLOTS), dma(2, Gather.SLOTS), dma(2, 1)] if links else []
+        ),
         compiler_params=params(**comm(0)),
         name="forward",
     )(tok, cot, index_col, vec, *mask, att, ff)
@@ -874,30 +1034,30 @@
         wff = outs[9]
 
     bias = vec[9:].reshape(nmp, 1, hb)
-    result, n2g, gff, bg = pl.pallas_call(
-        feed_kernel,
+    outs = pl.pallas_call(
+        functools.partial(feed_kernel, links),
         grid=(nmp,),
         in_specs=[
-            whole(*rowspec), whole(*rowspec), whole(*rowspec),
-            pl.BlockSpec((1, 2, d, hb), lambda j: (j, 0, 0, 0)),
-            pl.BlockSpec((1, 1, hb), lambda j: (j, 0, 0)),
-            full(vec.shape),
+            whole(*rowspec), whole(*rowspec), whole(*rowspec), ANY, full((nmp, 1, hb)), full(vec.shape),
         ],
-        out_specs=[
-            full(rowspec), full(rowspec),
-            pl.BlockSpec((1, 2, d, hb), lambda j: (j, 0, 0, 0)),
-            pl.BlockSpec((1, 1, hb), lambda j: (j, 0, 0)),
-        ],
+        out_specs=[full(rowspec), full(rowspec), ANY, full((nmp, 1, hb))]
+        + [full((2, 2, rows, hb))] * links,
         out_shape=[
             sds(*rowspec, bf16), sds(*rowspec, f32),
             sds(nmp, 2, d, hb, bf16), sds(nmp, 1, hb, f32),
-        ],
+        ] + [sds(2, 2, rows, hb, bf16)] * links,
         scratch_shapes=[
             scratch(*rowspec, f32), scratch(images * RI, hb, bf16), scratch(images * RI, hb, bf16),
-        ],
-        compiler_params=params(),
+            scratch(nmp, 2, d, hb, bf16), scratch(2, 2, d, hb, bf16), dma(nmp), dma(2),
+        ] + (
+            [dma(Gather.SLOTS), dma(Gather.SLOTS), dma(4)]
+            + [scratch(n, 2, rows, hb, bf16) for n in (8, 8, 2, 2, 2)]
+            + [dma(Reduce.SLOTS), dma(Reduce.SLOTS), dma(8)] if links else []
+        ),
+        compiler_params=params(**comm(3)),
         name="feedforward",
     )(n2, cotk, resid, wff, bias, vec)
+    result, n2g, gff, bg = outs[:4]
 
     spans = (16, 16, 4, 4, 4, 4)
     outs = pl.pallas_call(
@@ -907,19 +1067,19 @@
             per_image(RI, d), per_image(RI, d), per_image(RI, d), per_image(RI, d),
             per_image(RI, d), per_image(RI, 3 * d),
             full(watt.shape), full(vec.shape), *mask_specs,
-        ] + [ANY] * links,
+        ] + [ANY, full((2, 2, rows, hb))] * links,
         out_specs=[per_image(RI, 4 * d), per_image(RI, d), per_image(RI, 1), full((8, d))]
         + [full((2, rows, hb))] * links,
         out_shape=[
             sds(images, RI, 4 * d, bf16), sds(*rowspec, f32), sds(images, RI, 1, f32), sds(8, d, f32),
         ] + [sds(2, rows, hb, f32)] * links,
         scratch_shapes=[scratch(RI, d, bf16)] + (
-            [scratch(n, 2, rows, hb, bf16) for n in spans]
-            + [dma(Reduce.SLOTS), dma(Reduce.SLOTS), dma(16)] if links else []
+            [scratch(n, 2, rows, hb, bf16) for n in (8, 8, 2, 2, 2, 4)]
+            + [dma(Reduce.SLOTS), dma(Reduce.SLOTS), dma(8)] if links else []
         ),
         compiler_params=params(**comm(1)),
         name="attention_backward",
-    )(n2g, cotk, branch, resid, normed, proj, watt, vec, *mask, *([gff] if links else []))
+    )(n2g, cotk, branch, resid, normed, proj, watt, vec, *mask, *([gff, outs[4]] if links else []))
     dp, resg, rg, vecg = outs[:4]
     if links:
         feedforward_gradient = outs[4]
@@ -928,19 +1088,19 @@
     outs = pl.pallas_call(
         functools.partial(grads_kernel, links),
         grid=(4 + images,),
-        in_specs=[
-            whole(images, RI, 4 * d), whole(*rowspec), whole(*rowspec), whole(images, RI, 1),
-            whole(*rowspec), whole(*rowspec), full(vec.shape), ANY,
-        ] + [full((8, d)), full((hidden // d, d))] * links,
+        in_specs=[ANY, ANY, ANY, full((images, RI, 1)), ANY, ANY, full(vec.shape), ANY]
+        + [full((8, d)), full((hidden // d, d))] * links,
         out_specs=[full(rowspec), full(rowspec)]
         + ([full((rows, d)), full(vec.shape)] if links else [full(full_d), full((8, d))]),
         out_shape=[sds(*rowspec, bf16), sds(*rowspec, bf16)]
         + ([sds(rows, d, f32), sds(*vec.shape, f32)] if links else [sds(*full_d, bf16), sds(8, d, f32)]),
-        scratch_shapes=[scratch(3 * d, d, bf16)] + (
-            [scratch(*full_d, bf16), scratch(8, d, f32), dma(1)]
-            + [scratch(n, rows, d, bf16) for n in spans[1:]]
+        scratch_shapes=([scratch(*full_d, bf16), scratch(8, d, f32)] if links else []) + [
+            scratch(3 * d, d, bf16), scratch(4, *rowspec, bf16), scratch(2, *rowspec, bf16),
+            scratch(*rowspec, f32), scratch(*rowspec, bf16), dma(9),
+        ] + (
+            [scratch(n, rows, d, bf16) for n in spans[1:]]
             + [dma(Reduce.SLOTS), dma(Reduce.SLOTS), scratch(11, 16, d, f32), dma(8), dma(8)]
-            if links else [dma(1)]
+            if links else []
         ),
         compiler_params=params(**comm(2)),
         name="attention_grads",

time: 284 us -> 247 us (0.87)
  Pallas kernels: 264 us -> 229 us
  other arithmetic: 11.7 us -> 8.3 us
    pallas_call x1, Pallas kernels: 66.6 us -> 43.1 us  [per_device(): pl.pallas_call(functools.partial(backward_kernel, links), grid=(images,),...]
    pallas_call x1, Pallas kernels: 87.7 us -> 74.9 us  [per_device(): pl.pallas_call(functools.partial(forward_kernel, links), grid=(1 + images...]
    pallas_call x1, Pallas kernels: 45.9 us -> 56.8 us  [per_device(): pl.pallas_call(functools.partial(feed_kernel, links), grid=(nmp,), in_spe...]
    pallas_call x1, Pallas kernels: 51.1 us -> 42.4 us  [per_device(): pl.pallas_call(functools.partial(grads_kernel, links), grid=(4 + images,)...]
    convert_element_type x2 -> x0, other arithmetic: 3.45 us -> none  [the longest x1 1.81 us: per_device(): feedforward_weights.astype(bf16)]
where the time goes in v4:
time: 247 us; the launch traced here: 246 us
  Pallas kernels  229 us (93%)
  other arithmetic  8.3 us (3%)
  local copies, waits for them, and re-layouts  7.67 us (3%)
    pallas_call x1, Pallas kernels, per_device(): pl.pallas_call(functools.partial(forward_kernel, links), grid=(1 + images...  74.9 us
    pallas_call x1, Pallas kernels, per_device(): pl.pallas_call(functools.partial(feed_kernel, links), grid=(nmp,), in_spe...  56.8 us
    pallas_call x1, Pallas kernels, per_device(): pl.pallas_call(functools.partial(backward_kernel, links), grid=(images,),...  43.1 us
    pallas_call x1, Pallas kernels, per_device(): pl.pallas_call(functools.partial(grads_kernel, links), grid=(4 + images,)...  42.4 us
    pallas_call x1, Pallas kernels, per_device(): pl.pallas_call(scatter_kernel, in_specs=[pl.BlockSpec(memory_space=pltpu....  12.2 us

profile of v4, /device:TPU:0, one launch (start us, length us, event | category | flops | bytes accessed | tf_op | source)
XLA Modules:
  0.0 246.2 jit_solution(14372192256852674915)
XLA Ops:
  0.7 0.8 fusion.6
  1.4 0.1 reshape.57
  1.5 0.8 add_select_fusion
  2.4 0.1 reshape.56
  2.5 0.1 reshape.55
  2.5 0.1 concatenate.7
  2.6 0.6 broadcast_in_dim.18.idx_ref
  3.2 0.7 slice.18
  4.0 0.6 reshape.58.bias_ref
  4.6 1.1 broadcast_in_dim.19.idx_ref
  5.6 74.9 %forward.1 = (bf16[4,272,768]{2,1,0:T(8,128)(2,1)}, bf16[4,272,768]{2,1,0:T(8,128)(2,1)}, bf16[4,272,768]{2,1,0:T(8,128)(2,1)}, bf16[4,272,2304]{2,1,0:T(8,128)(...) custom-call(bf16[542,4,768]{2,1,0:T(4,128)(2,1)} %bitcast.10, ...), custom_call_target="tpu_custom_call" | custom-call | tf_op jit(solution)/shard_map/forward/pallas_call | solution.py:1010
  80.5 56.8 %feedforward.1 = (bf16[4,272,768]{2,1,0:T(8,128)(2,1)}, f32[4,272,768]{2,1,0:T(8,128)}, bf16[4,2,768,768]{3,2,1,0:T(8,128)(2,1)}, f32[4,1,768]{2,1,0:T(1,128)}, bf16[2,2,96,768]{3,2,1,0:T(8,128)(2,1)}) custom-call(bf16[4,272,768]{2,1,0:T(8,128)(2,1)} %get-tuple-element.46.n2_ref, bf16[4,272,768]{2,1,0:T(8,128)(2,1)} %get-tuple-element.47.cot_ref.cotk_ref, ...), custom_call_target="tpu_custom_call" | custom-call | tf_op jit(solution)/shard_map/feedforward/pallas_call | solution.py:1037
  137.3 0.0 copy-start.17
  137.3 43.1 %attention_backward.1 = (bf16[4,272,3072]{2,1,0:T(8,128)(2,1)}, f32[4,272,768]{2,1,0:T(8,128)}, f32[4,272,1]{2,1,0:T(8,128)}, f32[8,768]{1,0:T(8,128)}, f32[2,96,768]{2,1,0:T(8,128)}) custom-call(f32[4,272,768]{2,1,0:T(8,128)} %get-tuple-element.50.n2g_ref, bf16[4,272,768]{2,1,0:T(8,128)(2,1)} %get-tuple-element.47.cot_ref.cotk_ref, ...), custom_call_target="tpu_custom_call" | custom-call | tf_op jit(solution)/shard_map/attention_backward/pallas_call | solution.py:1063
  180.4 0.0 copy-done.17
  180.4 0.6 copy.44
  181.1 0.0 copy-start.4
  181.1 0.0 copy-start.10
  181.1 0.0 copy-start.11
  181.1 0.0 copy-start.12
  181.1 42.4 %attention_grads.1 = (bf16[4,272,768]{2,1,0:T(8,128)(2,1)}, bf16[4,272,768]{2,1,0:T(8,128)(2,1)}, f32[96,768]{1,0:T(8,128)}, f32[13,768]{1,0:T(8,128)}) custom-call(bf16[4,272,3072]{2,1,0:T(8,128)(2,1)} %get-tuple-element.57.dp_ref, bf16[4,272,768]{2,1,0:T(8,128)(2,1)} %get-tuple-element.52.normed_ref, bf16[4,272,768]{2,1,0:T(8,128)(2,1)} %get-tuple-element.58.mixed_ref, ...), custom_call_target="tpu_custom_call" | custom-call | tf_op jit(solution)/shard_map/attention_grads/pallas_call | solution.py:1088
  223.5 0.0 copy-start
  223.6 0.0 copy-start.2
  223.6 0.0 copy-start.7
  223.6 0.0 copy-start.8
  223.6 1.5 slice_reduce_fusion
  225.1 0.0 copy-done.3
  225.1 0.0 copy-done.14
  225.1 0.0 copy-done.15
  225.1 0.0 copy-done.16
  225.1 1.5 multiply_add_fusion.5
  226.6 0.0 copy-done.4
  226.6 0.0 copy-done.10
  226.6 0.0 copy-done.11
  226.6 0.0 copy-start.9
  226.6 2.0 fusion.10
  228.6 0.0 copy-done.12
  228.6 0.8 multiply_add_fusion.3
  229.4 0.0 copy-done
  229.4 0.0 copy-done.2
  229.4 0.0 copy-done.7
  229.4 1.4 fusion.8
  230.8 0.0 copy-done.9
  230.8 1.0 multiply_add_fusion.1
  231.8 12.2 %scatter_rows.1 = (f32[542,4,768]{2,1,0:T(4,128)}, bf16[542,4,768]{2,1,0:T(4,128)(2,1)}) custom-call(bf16[4,272,768]{2,1,0:T(8,128)(2,1)} %get-tuple-element.64.high_ref, bf16[4,272,768]{2,1,0:T(8,128)(2,1)} %get-tuple-element.65.low_ref, bf16[4,272,768]{2,1,0:T(8,128)(2,1)} %get-tuple-element.66.result_ref, s32[1,1216]{1,0:T(1,128)} %broadcast_in_dim.18.idx_ref, ...), custom_call_target="tpu_custom_call" | custom-call | tf_op jit(solution)/shard_map/scatter_rows/pallas_call | solution.py:1122
  244.1 0.7 copy.48
  244.8 0.8 copy.49
  245.6 0.6 copy.50
  (15 shorter events, 0.0 us)
Async XLA Ops:
  137.3 43.2 %copy-start.17 = (f32[4,1,768]{2,1,0:T(1,128)S(1)}, f32[4,1,768]{2,1,0:T(1,128)}, u32[]{:S(2)}) copy-start(f32[4,1,768]{2,1,0:T(1,128)} %get-tuple-element.63) | copy-start | bytes 36868
  181.0 44.0 %copy-start.3 = (f32[13,768]{1,0:T(8,128)S(1)}, f32[13,768]{1,0:T(8,128)}, u32[]{:S(2)}) copy-start(f32[13,768]{1,0:T(8,128)} %vec_ref.7) | copy-start | bytes 119812
  181.0 44.0 %copy-start.14 = (f32[13,768]{1,0:T(8,128)S(1)}, f32[13,768]{1,0:T(8,128)}, u32[]{:S(2)}) copy-start(f32[13,768]{1,0:T(8,128)} %param.35) | copy-start | bytes 119812
  181.0 44.0 %copy-start.15 = (f32[13,768]{1,0:T(8,128)S(1)}, f32[13,768]{1,0:T(8,128)}, u32[]{:S(2)}) copy-start(f32[13,768]{1,0:T(8,128)} %param.34) | copy-start | bytes 119812
  181.1 44.0 %copy-start.16 = (f32[13,768]{1,0:T(8,128)S(1)}, f32[13,768]{1,0:T(8,128)}, u32[]{:S(2)}) copy-start(f32[13,768]{1,0:T(8,128)} %param.33) | copy-start | bytes 119812
  181.1 45.5 %copy-start.4 = (f32[768,96]{0,1:T(8,128)S(1)}, f32[768,96]{0,1:T(8,128)}, u32[]{:S(2)}) copy-start(f32[768,96]{0,1:T(8,128)} %param.24) | copy-start | bytes 884740
  181.1 45.5 %copy-start.10 = (f32[768,96]{0,1:T(8,128)S(1)}, f32[768,96]{0,1:T(8,128)}, u32[]{:S(2)}) copy-start(f32[768,96]{0,1:T(8,128)} %param.26) | copy-start | bytes 884740
  181.1 45.5 %copy-start.11 = (f32[768,96]{0,1:T(8,128)S(1)}, f32[768,96]{0,1:T(8,128)}, u32[]{:S(2)}) copy-start(f32[768,96]{0,1:T(8,128)} %param.25) | copy-start | bytes 884740
  181.1 47.5 %copy-start.12 = (f32[768,96]{0,1:T(8,128)S(1)}, f32[768,96]{0,1:T(8,128)}, u32[]{:S(2)}) copy-start(f32[768,96]{0,1:T(8,128)} %param.27) | copy-start | bytes 884740
  223.5 5.9 %copy-start = (f32[2,96,768]{2,1,0:T(8,128)S(1)}, f32[2,96,768]{2,1,0:T(8,128)}, u32[]{:S(2)}) copy-start(f32[2,96,768]{2,1,0:T(8,128)} %ff_ref.1) | copy-start | bytes 1769476
  223.6 5.9 %copy-start.2 = (f32[2,96,768]{2,1,0:T(8,128)S(1)}, f32[2,96,768]{2,1,0:T(8,128)}, u32[]{:S(2)}) copy-start(f32[2,96,768]{2,1,0:T(8,128)} %get-tuple-element.116) | copy-start | bytes 1769476
  223.6 5.9 %copy-start.7 = (f32[2,96,768]{2,1,0:T(8,128)S(1)}, f32[2,96,768]{2,1,0:T(8,128)}, u32[]{:S(2)}) copy-start(f32[2,96,768]{2,1,0:T(8,128)} %param.30) | copy-start | bytes 1769476
  223.6 5.8 %copy-start.8 = (f32[2,96,768]{2,1,0:T(8,128)S(1)}, f32[2,96,768]{2,1,0:T(8,128)}, u32[]{:S(2)}) copy-start(f32[2,96,768]{2,1,0:T(8,128)} %param.29) | copy-start | bytes 1769476
  226.6 4.2 %copy-start.9 = (f32[2,96,768]{2,1,0:T(8,128)S(1)}, f32[2,96,768]{2,1,0:T(8,128)}, u32[]{:S(2)}) copy-start(f32[2,96,768]{2,1,0:T(8,128)} %param.31) | copy-start | bytes 1769476
  228.6 3.2 %copy-start.5 = (f32[768,96]{0,1:T(8,128)}, f32[768,96]{0,1:T(8,128)S(1)}, u32[]{:S(2)}) copy-start(f32[768,96]{0,1:T(8,128)S(1)} %get-tuple-element.113) | copy-start | bytes 884740
  230.8 13.3 %copy-start.1 = (f32[2,96,768]{2,1,0:T(8,128)}, f32[2,96,768]{2,1,0:T(8,128)S(1)}, u32[]{:S(2)}) copy-start(f32[2,96,768]{2,1,0:T(8,128)S(1)} %get-tuple-element.119) | copy-start | bytes 1769476
  231.8 12.3 %copy-start.6 = (f32[96,768]{1,0:T(8,128)S(1)}, f32[96,768]{1,0:T(8,128)}, u32[]{:S(2)}) copy-start(f32[96,768]{1,0:T(8,128)} %get-tuple-element.69) | copy-start | bytes 884740
  231.8 13.8 %copy-start.13 = (f32[13,768]{1,0:T(8,128)S(1)}, f32[13,768]{1,0:T(8,128)}, u32[]{:S(2)}) copy-start(f32[13,768]{1,0:T(8,128)} %get-tuple-element.122) | copy-start | bytes 119812
